TPU v7x, 32 devices: a whole 2x2x4 slice. The times are simulated.
32 devices in a mesh: parts: 2 (over y), seq: 16 (over z, x, core).
Axes of the slice: x: 2, y: 2, z: 4, core: 2. Of those that a mesh axis runs over, the one named last changes fastest.
Arguments:
- queries: bfloat16 [32, 8192], P(('parts', 'seq')), parts along dimension 0, may hold values from -140 to 140
- new_keys: bfloat16 [32, 1024], P(('parts', 'seq')), parts along dimension 0, may hold values from -7 to 7
- new_values: bfloat16 [32, 1024], P(('parts', 'seq')), parts along dimension 0, may hold values from -6 to 6
- doc_keys: bfloat16 [32768, 1024], P(('parts', 'seq')), parts along dimension 0, may hold values from -6 to 6
- doc_values: bfloat16 [32768, 1024], P(('parts', 'seq')), parts along dimension 0, may hold values from -6 to 6
- suffix_keys: bfloat16 [32768, 1024], P(('parts', 'seq')), parts along dimension 0, may hold values from -6 to 6
- suffix_values: bfloat16 [32768, 1024], P(('parts', 'seq')), parts along dimension 0, may hold values from -6 to 6
- keep_lists: int32 [32, 32], P(('parts', 'seq')), parts along dimension 0, may hold values from 0 to 127, as said below
- suffix_lengths: int32 [16], P('parts'), parts along dimension 0, may hold values from 1 to 2048
Outputs:
- attended: bfloat16 [32, 8192], P(('parts', 'seq')), parts along dimension 0
There are 2 independent parts, one for each index of `parts`. A program takes and returns all parts, laid end to end along the dimension named above; each array names one. Nothing has to cross between parts.
Inputs may be any that keep to these rules, and one draw needn't show every extreme that they name: Row r's list (rows 2r and 2r+1 of keep_lists) names 64 different blocks of 0 to 127.
All inputs are finite; a program needn't handle non-finite values.
Results may differ from a plain program's by a relative error of at most 0.007.
Values may be sent and summed in bfloat16 or wider, within the bound.
No kernel may reach another device: no remote copies, remote signals or barrier semaphores. Data moves between devices by JAX's collectives and lax.ppermute only.
A program may use at most 128 MiB of HBM per device.

v0:
```python
import jax
import jax.numpy as jnp
from jax import lax
from jax.sharding import PartitionSpec as P

HEADS = 64
KVH = 8
HD = 128
BLOCK = 128


NEG_BIG = -1e30


def merge_terms(first, second):
    ceiling = jnp.maximum(first[0], second[0])
    left_scale = jnp.exp(first[0] - ceiling)
    right_scale = jnp.exp(second[0] - ceiling)
    return (
        ceiling,
        left_scale * first[1] + right_scale * second[1],
        left_scale[..., None] * first[2] + right_scale[..., None] * second[2],
    )


def block_terms(scores, live_keys, value_rows, form):
    masked = jnp.where(live_keys, scores, NEG_BIG)
    block_max = jnp.max(masked, axis=-1)
    weights = jnp.where(live_keys, jnp.exp(scores - block_max[..., None]), 0.0)
    block_sum = jnp.sum(weights, axis=-1)
    block_out = jnp.einsum(
        form, weights.astype(jnp.bfloat16), value_rows, preferred_element_type=jnp.float32
    )
    global_maximum = jnp.max(block_max, axis=-1)
    factor = jnp.exp(block_max - global_maximum[..., None])
    return (
        global_maximum,
        jnp.sum(factor * block_sum, axis=-1),
        jnp.sum(factor[..., None] * block_out, axis=-2),
    )


def per_device(
    queries,
    new_keys,
    new_values,
    doc_keys,
    doc_values,
    suffix_keys,
    suffix_values,
    keep_lists,
    suffix_lengths,
):
    groups = HEADS // KVH
    factor_scale = HD ** (-0.5)
    devices = lax.axis_size("seq")
    my_index = lax.axis_index("seq")
    row_id = my_index // 2
    parity = my_index % 2
    blocks_here = doc_keys.shape[0] // BLOCK
    gathered = lax.all_gather(queries, "seq", axis=0, tiled=True)
    every_list = lax.all_gather(keep_lists, "seq", axis=0, tiled=True)
    local_ids = every_list.reshape(devices // 2, -1) - my_index * blocks_here
    block_range = jnp.arange(blocks_here, dtype=jnp.int32)
    row_hits = jnp.any(local_ids[:, :, None] == block_range[None, None, :], axis=1)
    token_mask = jnp.repeat(row_hits, 2, axis=0)
    q_heads = gathered.reshape(devices, KVH, groups, HD).transpose(1, 0, 2, 3)
    key_heads = doc_keys.reshape(blocks_here, BLOCK, KVH, HD).transpose(2, 0, 1, 3)
    value_heads = doc_values.reshape(blocks_here, BLOCK, KVH, HD).transpose(2, 0, 1, 3)

    def doc_head(head_item):
        q_part, key_part, value_part = head_item
        scores = (
            jnp.einsum("tgd,bjd->tgbj", q_part, key_part, preferred_element_type=jnp.float32)
            * factor_scale
        )
        return block_terms(scores, token_mask[:, None, :, None], value_part, "tgbj,bjd->tgbd")

    doc_max, doc_sum, doc_out = lax.map(doc_head, (q_heads, key_heads, value_heads))
    doc_partial = (
        doc_max.transpose(1, 0, 2).reshape(devices, HEADS),
        doc_sum.transpose(1, 0, 2).reshape(devices, HEADS),
        doc_out.transpose(1, 0, 2, 3).reshape(devices, HEADS, HD),
    )
    q_rows = lax.dynamic_slice_in_dim(gathered, 2 * row_id, 2, 0).reshape(2, KVH, groups, HD)
    suffix_here = suffix_keys.shape[0]
    suffix_blocks = suffix_here // BLOCK
    keys_suf = suffix_keys.reshape(suffix_blocks, BLOCK, KVH, HD)
    values_suf = suffix_values.reshape(suffix_blocks, BLOCK, KVH, HD)
    scores = (
        jnp.einsum("tkgd,bjkd->tkgbj", q_rows, keys_suf, preferred_element_type=jnp.float32)
        * factor_scale
    )
    position = parity * suffix_here + jnp.arange(suffix_here, dtype=jnp.int32).reshape(
        suffix_blocks, BLOCK
    )
    live_keys = position < suffix_lengths[row_id]
    row_partial = block_terms(scores, live_keys, values_suf, "tkgbj,bjkd->tkgbd")
    own_scores = (
        jnp.einsum(
            "tkgd,kd->tkg", q_rows, new_keys.reshape(KVH, HD), preferred_element_type=jnp.float32
        )
        * factor_scale
    )
    visible = jnp.broadcast_to(
        (jnp.arange(2, dtype=jnp.int32) >= parity)[:, None, None], own_scores.shape
    )
    own_values = jnp.broadcast_to(
        new_values.reshape(KVH, HD).astype(jnp.float32)[None, :, None, :], (2, KVH, groups, HD)
    )
    own_partial = (
        jnp.where(visible, own_scores, NEG_BIG),
        visible.astype(jnp.float32),
        jnp.where(visible[..., None], own_values, 0.0),
    )
    row_partial = merge_terms(row_partial, own_partial)
    placed = (
        lax.dynamic_update_slice(
            jnp.full((devices, HEADS), NEG_BIG, jnp.float32),
            row_partial[0].reshape(2, HEADS),
            (2 * row_id, 0),
        ),
        lax.dynamic_update_slice(
            jnp.zeros((devices, HEADS), jnp.float32),
            row_partial[1].reshape(2, HEADS),
            (2 * row_id, 0),
        ),
        lax.dynamic_update_slice(
            jnp.zeros((devices, HEADS, HD), jnp.float32),
            row_partial[2].reshape(2, HEADS, HD),
            (2 * row_id, 0, 0),
        ),
    )
    span_max, span_sum, span_out = merge_terms(doc_partial, placed)
    units = (span_out / jnp.maximum(span_sum, 1.0)[..., None]).astype(jnp.bfloat16)
    parts_max, parts_sum = (
        lax.all_to_all(span_max[:, None, :], "seq", split_axis=0, concat_axis=1, tiled=True),
        lax.all_to_all(span_sum[:, None, :], "seq", split_axis=0, concat_axis=1, tiled=True),
    )
    parts_unit = lax.all_to_all(
        units.reshape(devices, 1, HEADS * HD), "seq", split_axis=0, concat_axis=1, tiled=True
    )
    ceiling = jnp.max(parts_max, axis=1)
    weight = jnp.exp(parts_max - ceiling[:, None, :]) * parts_sum
    total_sum = jnp.sum(weight, axis=1)
    total_out = jnp.sum(
        weight[..., None] * parts_unit.reshape(1, devices, HEADS, HD).astype(jnp.float32), axis=1
    )
    return (total_out / total_sum[..., None]).reshape(1, HEADS * HD).astype(jnp.bfloat16)


def solution(mesh):
    in_specs = (
        P(("parts", "seq"), None),
        P(("parts", "seq"), None),
        P(("parts", "seq"), None),
        P(("parts", "seq"), None),
        P(("parts", "seq"), None),
        P(("parts", "seq"), None),
        P(("parts", "seq"), None),
        P(("parts", "seq"), None),
        P("parts"),
    )
    out_specs = P(("parts", "seq"), None)
    return jax.shard_map(
        per_device, mesh=mesh, in_specs=in_specs, out_specs=out_specs, check_vma=False
    )
```

profile of v0, /device:TPU:0, one launch (start us, length us, event | category | flops | bytes accessed | tf_op | source)
XLA Modules:
  0.0 115.1 jit_solution(774386942064762164)
XLA Ops:
  0.0 24.8 %all-gather.1 = bf16[16,1,8192]{2,1,0:T(2,128)(2,1)S(1)} all-gather(bf16[1,1,8192]{2,1,0:T(2,128)(2,1)} %bitcast.210), channel_id=1, replica_groups=mesh['parts'=2,'seq'=16] {'seq'}, dimensions={0}, use_global_device_ids=true | all-gather | bytes 278528 | tf_op jit(solution)/shard_map/all_gather | solution.py:61
  24.8 2.2 %copy.160 = bf16[128,8,8,128]{3,2,1,0:T(8,128)(2,1)S(1)} copy(bf16[128,8,8,128]{3,1,2,0:T(8,128)(2,1)} %bitcast.191) | data formatting | bytes 4194304
  30.1 0.9 fusion.38
  32.1 17.4 %all-gather = s32[16,1,32]{2,1,0:T(1,128)S(1)} all-gather(s32[1,1,32]{2,1,0:T(1,128)S(1)} %bitcast.212), channel_id=1, replica_groups=mesh['parts'=2,'seq'=16] {'seq'}, dimensions={0}, use_global_device_ids=true | all-gather | bytes 2176 | tf_op jit(solution)/shard_map/all_gather | solution.py:62
  49.8 1.6 %reduce.8 = bf16[16,8192]{1,0:T(8,128)(2,1)S(1)} reduce(bf16[16,1,8192]{2,1,0:T(2,128)(2,1)S(1)} %all-gather.1, bf16[]{:T(256)} %constant.83), dimensions={1}, to_apply=%all-gather.1.reduce_sub_computation | reduce | bytes 524290 | tf_op jit(solution)/shard_map/all_gather | solution.py:61
  52.8 1.1 copy-done.2
  54.7 1.9 %copy.116 = bf16[8,8,128,128]{3,2,1,0:T(8,128)(2,1)} copy(bf16[8,8,128,128]{3,0,2,1:T(8,128)(2,1)S(1)} %bitcast_bitcast_fusion.2) | data formatting | bytes 4194304
  56.6 20.4 %while.15 = (s32[]{:T(128)}, f32[8,16,8]{1,2,0:T(8,128)S(1)}, f32[8,16,8]{1,2,0:T(8,128)S(1)}, f32[8,16,8,128]{3,2,0,1:T(8,128)S(1)}, bf16[8,16,8,128]{3,2,0,1:T...) while((s32[]{:T(128)}, f32[8,16,8]{1,2,0:T(8,128)S(1)}, ...), condition=%wide.region_7.8_spmd.clone, body=%wide.region_1.7_spmd.clone.sunk | while | flops 68535040 | bytes 2387621 | solution.py:79
  57.7 1.3 %fusion.67 = f32[16,8,128]{2,0,1:T(8,128)S(1)} fusion(bf16[16,8,8,128]{3,1,2,0:T(8,128)(2,1)S(1)} %get-tuple-element.219, bf16[8,8,128,128]{3,2,1,0:T(8,128)(2,1)} %get-tuple-element.245, s32[]{:T(128)} %get-tuple-element.230, f32[16,8,8]{0,1,2:T(8,128)S(1)} %copy.220), kind=kOutput, calls=%fused_computation.4.clone.1 | convolution fusion | flops 33800192 | bytes 594432 | tf_op jit(solution)/shard_map/while/body/eval_jaxpr/tgbj,bjd->tgbd/dot_general | solution.py:31
  60.2 1.3 %fusion.67 = f32[16,8,128]{2,0,1:T(8,128)S(1)} fusion(bf16[16,8,8,128]{3,1,2,0:T(8,128)(2,1)S(1)} %get-tuple-element.219, bf16[8,8,128,128]{3,2,1,0:T(8,128)(2,1)} %get-tuple-element.245, s32[]{:T(128)} %get-tuple-element.230, f32[16,8,8]{0,1,2:T(8,128)S(1)} %copy.220), kind=kOutput, calls=%fused_computation.4.clone.1 | convolution fusion | flops 33800192 | bytes 594432 | tf_op jit(solution)/shard_map/while/body/eval_jaxpr/tgbj,bjd->tgbd/dot_general | solution.py:31
  62.8 1.3 %fusion.67 = f32[16,8,128]{2,0,1:T(8,128)S(1)} fusion(bf16[16,8,8,128]{3,1,2,0:T(8,128)(2,1)S(1)} %get-tuple-element.219, bf16[8,8,128,128]{3,2,1,0:T(8,128)(2,1)} %get-tuple-element.245, s32[]{:T(128)} %get-tuple-element.230, f32[16,8,8]{0,1,2:T(8,128)S(1)} %copy.220), kind=kOutput, calls=%fused_computation.4.clone.1 | convolution fusion | flops 33800192 | bytes 594432 | tf_op jit(solution)/shard_map/while/body/eval_jaxpr/tgbj,bjd->tgbd/dot_general | solution.py:31
  65.3 1.3 %fusion.67 = f32[16,8,128]{2,0,1:T(8,128)S(1)} fusion(bf16[16,8,8,128]{3,1,2,0:T(8,128)(2,1)S(1)} %get-tuple-element.219, bf16[8,8,128,128]{3,2,1,0:T(8,128)(2,1)} %get-tuple-element.245, s32[]{:T(128)} %get-tuple-element.230, f32[16,8,8]{0,1,2:T(8,128)S(1)} %copy.220), kind=kOutput, calls=%fused_computation.4.clone.1 | convolution fusion | flops 33800192 | bytes 594432 | tf_op jit(solution)/shard_map/while/body/eval_jaxpr/tgbj,bjd->tgbd/dot_general | solution.py:31
  67.8 1.3 %fusion.67 = f32[16,8,128]{2,0,1:T(8,128)S(1)} fusion(bf16[16,8,8,128]{3,1,2,0:T(8,128)(2,1)S(1)} %get-tuple-element.219, bf16[8,8,128,128]{3,2,1,0:T(8,128)(2,1)} %get-tuple-element.245, s32[]{:T(128)} %get-tuple-element.230, f32[16,8,8]{0,1,2:T(8,128)S(1)} %copy.220), kind=kOutput, calls=%fused_computation.4.clone.1 | convolution fusion | flops 33800192 | bytes 594432 | tf_op jit(solution)/shard_map/while/body/eval_jaxpr/tgbj,bjd->tgbd/dot_general | solution.py:31
  70.4 1.3 %fusion.67 = f32[16,8,128]{2,0,1:T(8,128)S(1)} fusion(bf16[16,8,8,128]{3,1,2,0:T(8,128)(2,1)S(1)} %get-tuple-element.219, bf16[8,8,128,128]{3,2,1,0:T(8,128)(2,1)} %get-tuple-element.245, s32[]{:T(128)} %get-tuple-element.230, f32[16,8,8]{0,1,2:T(8,128)S(1)} %copy.220), kind=kOutput, calls=%fused_computation.4.clone.1 | convolution fusion | flops 33800192 | bytes 594432 | tf_op jit(solution)/shard_map/while/body/eval_jaxpr/tgbj,bjd->tgbd/dot_general | solution.py:31
  72.9 1.3 %fusion.67 = f32[16,8,128]{2,0,1:T(8,128)S(1)} fusion(bf16[16,8,8,128]{3,1,2,0:T(8,128)(2,1)S(1)} %get-tuple-element.219, bf16[8,8,128,128]{3,2,1,0:T(8,128)(2,1)} %get-tuple-element.245, s32[]{:T(128)} %get-tuple-element.230, f32[16,8,8]{0,1,2:T(8,128)S(1)} %copy.220), kind=kOutput, calls=%fused_computation.4.clone.1 | convolution fusion | flops 33800192 | bytes 594432 | tf_op jit(solution)/shard_map/while/body/eval_jaxpr/tgbj,bjd->tgbd/dot_general | solution.py:31
  75.5 1.3 %fusion.67 = f32[16,8,128]{2,0,1:T(8,128)S(1)} fusion(bf16[16,8,8,128]{3,1,2,0:T(8,128)(2,1)S(1)} %get-tuple-element.219, bf16[8,8,128,128]{3,2,1,0:T(8,128)(2,1)} %get-tuple-element.245, s32[]{:T(128)} %get-tuple-element.230, f32[16,8,8]{0,1,2:T(8,128)S(1)} %copy.220), kind=kOutput, calls=%fused_computation.4.clone.1 | convolution fusion | flops 33800192 | bytes 594432 | tf_op jit(solution)/shard_map/while/body/eval_jaxpr/tgbj,bjd->tgbd/dot_general | solution.py:31
  78.2 3.4 %all-to-all-start = ((f32[16,1,64]{2,1,0:T(1,128)}), f32[16,1,64]{2,1,0:T(1,128)S(1)}, u32[]{:S(2)}, u32[]{:S(2)}) async-start(f32[16,1,64]{2,1,0:T(1,128)} %copy.121), calls=%async_computation | async-start | bytes 16384 | tf_op jit(solution)/shard_map/all_to_all | solution.py:137
  81.7 2.2 %copy.161 = bf16[128,8,8,128]{3,2,1,0:T(8,128)(2,1)S(1)} copy(bf16[128,8,8,128]{3,1,2,0:T(8,128)(2,1)} %bitcast.194) | data formatting | bytes 4194304
  86.6 1.4 %all-to-all-done = f32[16,1,64]{2,1,0:T(1,128)S(1)} async-done(((f32[16,1,64]{2,1,0:T(1,128)}), f32[16,1,64]{2,1,0:T(1,128)S(1)}, u32[]{:S(2)}, u32[]{:S(2)}) %all-to-all-start) | async-done | bytes 4128 | tf_op jit(solution)/shard_map/all_to_all | solution.py:137
  88.0 4.6 %all-to-all-start.1 = ((f32[16,1,64]{2,1,0:T(1,128)}), f32[16,1,64]{2,1,0:T(1,128)S(1)}, u32[]{:S(2)}, u32[]{:S(2)}) async-start(f32[16,1,64]{2,1,0:T(1,128)} %copy.125), calls=%async_computation.1 | async-start | bytes 16384 | tf_op jit(solution)/shard_map/all_to_all | solution.py:138
  93.8 2.3 %reduce.15 = bf16[16,8192]{1,0:T(8,128)(2,1)S(1)} reduce(bf16[16,1,8192]{2,1,0:T(2,128)(2,1)S(1)} %reshape.281, bf16[]{:T(256)} %broadcast.113), dimensions={1}, to_apply=%reshape.281.reduce_sub_computation | reduce | bytes 524290 | tf_op jit(solution)/shard_map/reshape | solution.py:141
  97.0 2.0 %all-to-all-done.1 = f32[16,1,64]{2,1,0:T(1,128)S(1)} async-done(((f32[16,1,64]{2,1,0:T(1,128)}), f32[16,1,64]{2,1,0:T(1,128)S(1)}, u32[]{:S(2)}, u32[]{:S(2)}) %all-to-all-start.1) | async-done | bytes 4128 | tf_op jit(solution)/shard_map/all_to_all | solution.py:138
  99.0 4.1 %all-to-all-start.2 = ((bf16[16,2,4096]{2,1,0:T(2,128)(2,1)}), bf16[16,2,4096]{2,1,0:T(2,128)(2,1)S(1)}, u32[]{:S(2)}, u32[]{:S(2)}) async-start(bf16[16,2,4096]{2,1,0:T(2,128)(2,1)} %reshape.294), calls=%async_computation.2 | async-start | bytes 524288 | tf_op jit(solution)/shard_map/all_to_all | solution.py:140
  103.1 9.9 %all-to-all-done.2 = bf16[16,2,4096]{2,1,0:T(2,128)(2,1)S(1)} async-done(((bf16[16,2,4096]{2,1,0:T(2,128)(2,1)}), bf16[16,2,4096]{2,1,0:T(2,128)(2,1)S(1)}, u32[]{:S(2)}, u32[]{:S(2)}) %all-to-all-start.2) | async-done | bytes 262176 | tf_op jit(solution)/shard_map/all_to_all | solution.py:140
  (157 shorter events, 24.5 us)
Async XLA Ops:
  0.0 29.1 %copy-start = (bf16[1,1024]{1,0:T(2,128)(2,1)S(1)}, bf16[1,1024]{1,0:T(2,128)(2,1)}, u32[]{:S(2)}) copy-start(bf16[1,1024]{1,0:T(2,128)(2,1)} %param.12) | copy-start | bytes 6148
  24.8 6.3 %copy-start.8 = (pred[2]{0:T(512)(128)(4,1)}, pred[2]{0:T(512)(128)(4,1)S(1)}, u32[]{:S(2)}) copy-start(pred[2]{0:T(512)(128)(4,1)S(1)} %get-tuple-element.152) | copy-start | bytes 10
  27.1 0.7 copy-start.11
  29.3 2.7 %copy-start.10 = (s32[1,32]{1,0:T(1,128)S(1)}, s32[1,32]{1,0:T(1,128)}, u32[]{:S(2)}) copy-start(s32[1,32]{1,0:T(1,128)} %param.18) | copy-start | bytes 388
  30.1 21.4 %copy-start.1 = (bf16[1024,1024]{1,0:T(8,128)(2,1)S(1)}, bf16[1024,1024]{1,0:T(8,128)(2,1)}, u32[]{:S(2)}) copy-start(bf16[1024,1024]{1,0:T(8,128)(2,1)} %param.14) | copy-start | bytes 6291460
  52.3 1.6 %copy-start.2 = (bf16[1024,1024]{1,0:T(8,128)(2,1)S(1)}, bf16[1024,1024]{1,0:T(8,128)(2,1)}, u32[]{:S(2)}) copy-start(bf16[1024,1024]{1,0:T(8,128)(2,1)} %param.15) | copy-start | bytes 6291460
  54.6 1.9 %copy-start.4 = (f32[8,16,8]{1,2,0:T(8,128)S(1)}, f32[8,16,8]{1,2,0:T(8,128)}, u32[]{:S(2)}) copy-start(f32[8,16,8]{1,2,0:T(8,128)} %custom-call) | copy-start | bytes 12292
  54.7 1.9 %copy-start.5 = (f32[8,16,8]{1,2,0:T(8,128)S(1)}, f32[8,16,8]{1,2,0:T(8,128)}, u32[]{:S(2)}) copy-start(f32[8,16,8]{1,2,0:T(8,128)} %custom-call.1) | copy-start | bytes 12292
  78.2 9.8 %all-to-all-start = ((f32[16,1,64]{2,1,0:T(1,128)}), f32[16,1,64]{2,1,0:T(1,128)S(1)}, u32[]{:S(2)}, u32[]{:S(2)}) async-start(f32[16,1,64]{2,1,0:T(1,128)} %copy.121), calls=%async_computation | async-start | bytes 16384 | tf_op jit(solution)/shard_map/all_to_all | solution.py:137
  83.9 0.7 copy-start.6
  83.9 0.9 copy-start.7
  83.9 1.0 copy-start.3
  84.9 0.7 copy-start.9
  88.0 10.9 %all-to-all-start.1 = ((f32[16,1,64]{2,1,0:T(1,128)}), f32[16,1,64]{2,1,0:T(1,128)S(1)}, u32[]{:S(2)}, u32[]{:S(2)}) async-start(f32[16,1,64]{2,1,0:T(1,128)} %copy.125), calls=%async_computation.1 | async-start | bytes 16384 | tf_op jit(solution)/shard_map/all_to_all | solution.py:138
  99.0 14.1 %all-to-all-start.2 = ((bf16[16,2,4096]{2,1,0:T(2,128)(2,1)}), bf16[16,2,4096]{2,1,0:T(2,128)(2,1)S(1)}, u32[]{:S(2)}, u32[]{:S(2)}) async-start(bf16[16,2,4096]{2,1,0:T(2,128)(2,1)} %reshape.294), calls=%async_computation.2 | async-start | bytes 524288 | tf_op jit(solution)/shard_map/all_to_all | solution.py:140
where the time goes:
time: 116 us; the launch traced here: 115 us
  blocking collectives  42.3 us (36%)
  local copies, waits for them, and re-layouts  18.6 us (16%)
  matrix products  15 us (13%)
  waiting for transfers between devices  13.3 us (11%)
  other arithmetic  13.2 us (11%)
  starting transfers between devices  12 us (10%)
    all_gather x1, blocking collectives, per_device(): gathered = lax.all_gather(queries, 'seq', axis=0, tiled=True)  24.8 us
    all_gather x1, blocking collectives, per_device(): every_list = lax.all_gather(keep_lists, 'seq', axis=0, tiled=True)  17.4 us
    unnamed x33, local copies, waits for them, and re-layouts  11.3 us
    dot_general x9, matrix products, block_terms(): jnp.einsum(form, weights.astype(jnp.bfloat16), value_rows, preferred_elem...  10.7 us
    all_to_all x1, waiting for transfers between devices, per_device(): lax.all_to_all(units.reshape(devices, 1, HEADS * HD), 'seq', split_axis=0...  9.94 us
    reduce_sum x9, other arithmetic, block_terms(): block_sum = jnp.sum(weights, axis=-1)  5.2 us
    all_to_all x1, starting transfers between devices, per_device(): lax.all_to_all(span_sum[:, None, :], 'seq', split_axis=0, concat_axis=1,...  4.56 us
    all_to_all x1, starting transfers between devices, per_device(): lax.all_to_all(units.reshape(devices, 1, HEADS * HD), 'seq', split_axis=0...  4.05 us
  transfers between devices with their start and end apart: 3, of which 3 were waited for; matrix products, arithmetic and copies ran while one was open for 8% of the time, Pallas kernels for 0%

commit v1 on v0

v1 whole, which is shorter than its diff:
```python
import functools
import math

import jax
import jax.numpy as jnp
from jax import lax
from jax.experimental import pallas as pl
from jax.experimental.pallas import tpu as pltpu
from jax.sharding import PartitionSpec as P

HEADS = 64
KVH = 8
HD = 128
BLOCK = 128
GROUPS = HEADS // KVH
LANES = 128
SLOTS = 8

NEG_BIG = -1e30
NEG_SAFE = -5e29
EXP2_SCALE = HD**-0.5 * math.log2(math.e)

VMEM = pltpu.VMEM
SMEM = pltpu.SMEM


def pack_kernel(flag_rows, list_ref, q_ref, out_ref):
    q = q_ref[...].astype(jnp.float32)
    rows = [q[:, h * HD : (h + 1) * HD] for h in range(HEADS)]
    out_ref[0:HEADS, :] = jnp.concatenate(rows, axis=0).astype(jnp.bfloat16)
    ids = (
        lax.broadcasted_iota(jnp.int32, (flag_rows, LANES), 0) * LANES
        + lax.broadcasted_iota(jnp.int32, (flag_rows, LANES), 1)
    )

    def mark(k, found):
        return jnp.where(ids == list_ref[0, k], 1.0, found)

    found = lax.fori_loop(
        0, list_ref.shape[1], mark, jnp.zeros((flag_rows, LANES), jnp.float32), unroll=8
    )
    out_ref[HEADS : HEADS + flag_rows, :] = found.astype(jnp.bfloat16)


def lane_dot(a, b):
    return lax.dot_general(a, b, (((1,), (1,)), ((), ())), preferred_element_type=jnp.float32)


def partial_softmax(scores):
    top = jnp.max(scores, axis=-1, keepdims=True)
    weights = jnp.exp2((scores - jnp.maximum(top, NEG_SAFE)) * EXP2_SCALE)
    return top, jnp.sum(weights, axis=-1, keepdims=True), weights.astype(jnp.bfloat16)


def attend_kernel(
    flag_rows,
    me_ref,
    len_ref,
    near_ref,
    far_ref,
    dk_ref,
    dv_ref,
    sk_ref,
    sv_ref,
    nk_ref,
    nv_ref,
    out_ref,
    bias_ref,
):
    half_tokens = near_ref.shape[0]
    span = dk_ref.shape[0]
    suffix = sk_ref.shape[0]
    blocks_here = span // BLOCK
    me = me_ref[0]
    parity = lax.rem(me, 2)
    live_left = len_ref[lax.div(me, 2)] - parity * suffix
    first_block = me * blocks_here
    flag_row = lax.div(first_block, LANES)
    flag_lane = lax.rem(first_block, LANES)
    row_ids = lax.broadcasted_iota(jnp.int32, (1, flag_rows, LANES), 1)
    pick = (
        lax.broadcasted_iota(jnp.int32, (LANES, span), 0)
        == flag_lane + lax.broadcasted_iota(jnp.int32, (LANES, span), 1) // BLOCK
    ).astype(jnp.float32).astype(jnp.bfloat16)
    lane_ids = lax.broadcasted_iota(jnp.int32, (2 * SLOTS * GROUPS, LANES), 1)

    def do_chunk(chunk, local):
        start = chunk * SLOTS
        flags = near_ref[pl.ds(start, SLOTS), HEADS:, :].astype(jnp.float32) + far_ref[
            pl.ds(start, SLOTS), HEADS:, :
        ].astype(jnp.float32)
        flags = jnp.sum(jnp.where(row_ids == flag_row, flags, 0.0), axis=1)
        count = jnp.dot(flags.astype(jnp.bfloat16), pick, preferred_element_type=jnp.float32)
        bias = jnp.where(count > 0.5, 0.0, NEG_BIG)
        for s in range(SLOTS):
            bias_ref[s * GROUPS : (s + 1) * GROUPS, :] = jnp.broadcast_to(
                bias[s : s + 1, :], (GROUPS, span)
            )
        chunk_mask = chunk * (2 * SLOTS)
        folded = chunk
        for shift in (8, 4, 2, 1):
            folded = folded ^ (folded >> shift)
        chunk_mask = chunk_mask ^ (folded & 1)
        stats = jnp.zeros((2 * SLOTS * GROUPS, LANES), jnp.float32)
        for head in range(KVH):
            rows = slice(head * GROUPS, (head + 1) * GROUPS)
            cols = slice(head * HD, (head + 1) * HD)
            q = jnp.concatenate(
                [
                    ref[pl.ds(start, SLOTS), rows, :].astype(jnp.float32).reshape(SLOTS * GROUPS, HD)
                    for ref in (near_ref, far_ref)
                ],
                axis=0,
            ).astype(jnp.bfloat16)
            scores = lane_dot(q, dk_ref[:, cols])
            bias = bias_ref[...]
            scores = scores + jnp.concatenate([bias, bias], axis=0)
            top, total, weights = partial_softmax(scores)
            out = jnp.dot(weights, dv_ref[:, cols], preferred_element_type=jnp.float32)
            if local:
                pick_rows = lambda x: jnp.concatenate(
                    [x[0:GROUPS], x[SLOTS * GROUPS : (SLOTS + 1) * GROUPS]], axis=0
                )
                q_own = pick_rows(q.astype(jnp.float32))
                s_scores = lane_dot(q_own.astype(jnp.bfloat16), sk_ref[:, cols])
                position = lax.broadcasted_iota(jnp.int32, s_scores.shape, 1)
                s_scores = jnp.where(position < live_left, s_scores, NEG_BIG)
                s_top, s_total, s_weights = partial_softmax(s_scores)
                s_out = jnp.dot(s_weights, sv_ref[:, cols], preferred_element_type=jnp.float32)
                n_top = jnp.sum(
                    q_own * nk_ref[:, cols].astype(jnp.float32), axis=-1, keepdims=True
                )
                hidden = (lax.broadcasted_iota(jnp.int32, n_top.shape, 0) >= GROUPS) & (parity == 1)
                n_top = jnp.where(hidden, NEG_BIG, n_top)
                d_top, d_total, d_out = pick_rows(top), pick_rows(total), pick_rows(out)
                new_top = jnp.maximum(jnp.maximum(d_top, s_top), n_top)
                base = jnp.maximum(new_top, NEG_SAFE)
                d_scale = jnp.exp2((d_top - base) * EXP2_SCALE)
                s_scale = jnp.exp2((s_top - base) * EXP2_SCALE)
                n_scale = jnp.exp2((n_top - base) * EXP2_SCALE)
                new_total = d_scale * d_total + s_scale * s_total + n_scale
                new_out = (
                    d_scale * d_out
                    + s_scale * s_out
                    + n_scale * nv_ref[:, cols].astype(jnp.float32)
                )
                put_rows = lambda x, y: jnp.concatenate(
                    [
                        y[0:GROUPS],
                        x[GROUPS : SLOTS * GROUPS],
                        y[GROUPS:],
                        x[(SLOTS + 1) * GROUPS :],
                    ],
                    axis=0,
                )
                top, total, out = put_rows(top, new_top), put_rows(total, new_total), put_rows(
                    out, new_out
                )
            units = (out / jnp.maximum(total, 1.0)).astype(jnp.bfloat16)
            stats = jnp.where(lane_ids == head, top * EXP2_SCALE, stats)
            stats = jnp.where(lane_ids == KVH + head, total, stats)
            for s in range(2 * SLOTS):
                own = s % SLOTS
                mask = (own << 1) | (bin(own).count("1") & 1) ^ (s // SLOTS)
                out_ref[me ^ mask ^ chunk_mask, rows, :] = units[s * GROUPS : (s + 1) * GROUPS]
        high = stats.astype(jnp.bfloat16).astype(jnp.float32)
        rest = stats - high
        middle = rest.astype(jnp.bfloat16).astype(jnp.float32)
        low = rest - middle
        packed = high + pltpu.roll(middle, 2 * KVH, 1) + pltpu.roll(low, 4 * KVH, 1)
        packed = packed.astype(jnp.bfloat16)
        for s in range(2 * SLOTS):
            own = s % SLOTS
            mask = (own << 1) | (bin(own).count("1") & 1) ^ (s // SLOTS)
            out_ref[me ^ mask ^ chunk_mask, HEADS : HEADS + GROUPS, :] = packed[
                s * GROUPS : (s + 1) * GROUPS
            ]

    do_chunk(0, True)
    chunks = half_tokens // SLOTS
    if chunks > 1:
        lax.fori_loop(1, chunks, lambda c, _: do_chunk(c, False), None)


def combine_kernel(parts_ref, out_ref):
    packed = parts_ref[:, HEADS : HEADS + GROUPS, :].astype(jnp.float32)
    stats = (
        packed
        + pltpu.roll(packed, LANES - 2 * KVH, 2)
        + pltpu.roll(packed, LANES - 4 * KVH, 2)
    )
    live = lax.broadcasted_iota(jnp.int32, stats.shape, 2) < KVH
    top = jnp.where(live, stats, 0.0)
    total = jnp.where(live, pltpu.roll(stats, LANES - KVH, 2), 1.0)
    weight = jnp.exp2(top - jnp.max(top, axis=0, keepdims=True)) * total
    weight = weight / jnp.sum(weight, axis=0, keepdims=True)
    for head in range(KVH):
        rows = slice(head * GROUPS, (head + 1) * GROUPS)
        units = parts_ref[:, rows, :].astype(jnp.float32)
        mixed = jnp.sum(units * weight[:, :, head : head + 1], axis=0)
        for g in range(GROUPS):
            h = head * GROUPS + g
            out_ref[:, h * HD : (h + 1) * HD] = mixed[g : g + 1, :].astype(jnp.bfloat16)


def whole(space=VMEM):
    return pl.BlockSpec(memory_space=space)


def per_device(
    queries,
    new_keys,
    new_values,
    doc_keys,
    doc_values,
    suffix_keys,
    suffix_values,
    keep_lists,
    suffix_lengths,
):
    devices = lax.axis_size("seq")
    me = lax.axis_index("seq")
    blocks = devices * doc_keys.shape[0] // BLOCK
    flag_rows = 8 * pl.cdiv(blocks, 8 * LANES)
    packed = pl.pallas_call(
        functools.partial(pack_kernel, flag_rows),
        out_shape=jax.ShapeDtypeStruct((HEADS + flag_rows, HD), jnp.bfloat16),
        in_specs=[whole(SMEM), whole()],
        out_specs=whole(),
        name="pack",
    )(keep_lists, queries)
    near = packed[None]
    step = 2
    while step < devices:
        pairs = [(i, i ^ (step | 1)) for i in range(devices)]
        near = jnp.concatenate([near, lax.ppermute(near, "seq", pairs)], axis=0)
        step *= 2
    far = lax.ppermute(near, "seq", [(i, i ^ 1) for i in range(devices)])
    spread = pl.pallas_call(
        functools.partial(attend_kernel, flag_rows),
        out_shape=jax.ShapeDtypeStruct((devices, HEADS + GROUPS, HD), jnp.bfloat16),
        in_specs=[whole(SMEM), whole(SMEM)] + [whole()] * 8,
        out_specs=whole(),
        scratch_shapes=[VMEM((SLOTS * GROUPS, doc_keys.shape[0]), jnp.float32)],
        name="attend",
    )(
        me.astype(jnp.int32).reshape(1),
        suffix_lengths,
        near,
        far,
        doc_keys,
        doc_values,
        suffix_keys,
        suffix_values,
        new_keys,
        new_values,
    )
    parts = lax.all_to_all(spread, "seq", split_axis=0, concat_axis=0, tiled=True)
    return pl.pallas_call(
        combine_kernel,
        out_shape=jax.ShapeDtypeStruct((1, HEADS * HD), jnp.bfloat16),
        in_specs=[whole()],
        out_specs=whole(),
        name="combine",
    )(parts)


def solution(mesh):
    split = P(("parts", "seq"), None)
    return jax.shard_map(
        per_device,
        mesh=mesh,
        in_specs=(split,) * 8 + (P("parts"),),
        out_specs=split,
        check_vma=False,
    )
```

time: 116 us -> 50.3 us (0.43)
  blocking collectives: 42.3 us -> 17.3 us
  local copies, waits for them, and re-layouts: 18.6 us -> 0.66 us
  matrix products: 15 us -> 0 us
  Pallas kernels: 0 us -> 13.5 us
  other arithmetic: 13.2 us -> 2.2 us
  waiting for transfers between devices: 13.3 us -> 6.7 us
  starting transfers between devices: 12 us -> 9.49 us
    all_gather x2 -> x0, blocking collectives: 42.3 us -> none  [the longest x1 24.8 us: per_device(): gathered = lax.all_gather(queries, 'seq', axis=0, tiled=True)]
    all_to_all x0 -> x1, blocking collectives: none -> 17.3 us  [per_device(): lax.all_to_all(spread, 'seq', split_axis=0, concat_axis=0, tiled=True)]
    dot_general x19 -> x0, matrix products: 15 us -> none  [the longest x9 10.7 us: block_terms(): jnp.einsum(form, weights.astype(jnp.bfloat16), value_rows, preferred_elem...]
    pallas_call x0 -> x3, Pallas kernels: none -> 13.5 us  [the longest x1 10.1 us: per_device(): pl.pallas_call(functools.partial(attend_kernel, flag_rows), out_shape=jax...]
    all_to_all x3 -> x0, waiting for transfers between devices: 13.3 us -> none  [the longest x1 9.94 us: per_device(): lax.all_to_all(units.reshape(devices, 1, HEADS * HD), 'seq', split_axis=0...]
    all_to_all x3 -> x0, starting transfers between devices: 12 us -> none  [the longest x1 4.56 us: per_device(): lax.all_to_all(span_sum[:, None, :], 'seq', split_axis=0, concat_axis=1,...]
    unnamed x33 -> x4, local copies, waits for them, and re-layouts: 11.3 us -> 0.66 us
    ppermute x0 -> x4, starting transfers between devices: none -> 9.49 us  [the longest x3 7.56 us: per_device(): near = jnp.concatenate([near, lax.ppermute(near, 'seq', pairs)], axis=0)]
  transfers between devices with their start and end apart: 3 -> 4, of which waited for: 3 -> 4; matrix products, arithmetic and copies ran while one was open for 8% -> 0% of each run, Pallas kernels for 0% -> 0%
where the time goes in v1:
time: 50.3 us; the launch traced here: 49.9 us
  blocking collectives  17.3 us (34%)
  Pallas kernels  13.5 us (27%)
  starting transfers between devices  9.49 us (19%)
  waiting for transfers between devices  6.7 us (13%)
  other arithmetic  2.2 us (4%)
  local copies, waits for them, and re-layouts  0.66 us (1%)
    all_to_all x1, blocking collectives, per_device(): lax.all_to_all(spread, 'seq', split_axis=0, concat_axis=0, tiled=True)  17.3 us
    pallas_call x1, Pallas kernels, per_device(): pl.pallas_call(functools.partial(attend_kernel, flag_rows), out_shape=jax...  10.1 us
    ppermute x3, starting transfers between devices, per_device(): near = jnp.concatenate([near, lax.ppermute(near, 'seq', pairs)], axis=0)  7.56 us
    ppermute x3, waiting for transfers between devices, per_device(): near = jnp.concatenate([near, lax.ppermute(near, 'seq', pairs)], axis=0)  5.69 us
    concatenate x3, other arithmetic, per_device(): near = jnp.concatenate([near, lax.ppermute(near, 'seq', pairs)], axis=0)  2.2 us
    pallas_call x1, Pallas kernels, per_device(): pl.pallas_call(combine_kernel, out_shape=jax.ShapeDtypeStruct((1, HEADS *...  1.98 us
    ppermute x1, starting transfers between devices, per_device(): far = lax.ppermute(near, 'seq', [(i, i ^ 1) for i in range(devices)])  1.93 us
    pallas_call x1, Pallas kernels, per_device(): pl.pallas_call(functools.partial(pack_kernel, flag_rows), out_shape=jax.S...  1.43 us
  transfers between devices with their start and end apart: 4, of which 4 were waited for; matrix products, arithmetic and copies ran while one was open for 0% of the time, Pallas kernels for 0%

profile of v1, /device:TPU:0, one launch (start us, length us, event | category | flops | bytes accessed | tf_op | source)
XLA Modules:
  0.0 49.9 jit_solution(4188348974783662522)
XLA Ops:
  0.0 1.4 %pack.1 = bf16[72,128]{1,0:T(8,128)(2,1)} custom-call(s32[1,32]{1,0:T(1,128)} %list_ref.1, bf16[1,8192]{1,0:T(2,128)(2,1)} %q_ref.1), custom_call_target="tpu_custom_call" | custom-call | tf_op jit(solution)/shard_map/pack/pallas_call | solution.py:225
  1.4 2.4 %collective-permute-start = (bf16[1,72,128]{2,1,0:T(8,128)(2,1)}, bf16[1,72,128]{2,1,0:T(8,128)(2,1)S(1)}, u32[]{:S(2)}, u32[]{:S(2)}) collective-permute-start(bf16[1,72,128]{2,1,0:T(8,128)(2,1)} %bitcast.2), channel_id=1, source_target_pairs={{0,3},{1,2},{2,1},{3,0},{4,7},{5,6},{6,5},{7,4},{8,11},{9,10},{10,... | collective-permute-start | bytes 55304 | tf_op jit(solution)/shard_map/ppermute | solution.py:236
  3.8 1.7 %collective-permute-done = bf16[1,72,128]{2,1,0:T(8,128)(2,1)S(1)} collective-permute-done((bf16[1,72,128]{2,1,0:T(8,128)(2,1)}, bf16[1,72,128]{2,1,0:T(8,128)(2,1)S(1)}, u32[]{:S(2)}, u32[]{:S(2)}) %collective-permute-start) | collective-permute-done | bytes 18464 | tf_op jit(solution)/shard_map/ppermute | solution.py:236
  5.5 0.7 %pad_maximum_fusion.2 = bf16[2,72,128]{2,1,0:T(8,128)(2,1)S(1)} fusion(bf16[1,72,128]{2,1,0:T(8,128)(2,1)S(1)} %collective-permute-done, bf16[1,72,128]{2,1,0:T(8,128)(2,1)} %bitcast.3), kind=kLoop, calls=%fused_computation.2 | loop fusion | flops 18432 | bytes 73728 | tf_op jit(solution)/shard_map/concatenate | solution.py:236
  6.3 2.2 %collective-permute-start.1 = (bf16[2,72,128]{2,1,0:T(8,128)(2,1)S(1)}, bf16[2,72,128]{2,1,0:T(8,128)(2,1)S(1)}, u32[]{:S(2)}, u32[]{:S(2)}) collective-permute-start(bf16[2,72,128]{2,1,0:T(8,128)(2,1)S(1)} %pad_maximum_fusion.2), channel_id=1, source_target_pairs={{0,5},{1,4},{2,7},{3,6},{4,1},{5,0},{6,3},{7,2},{8,13},{9,12},{10,... | collective-permute-start | bytes 110600 | tf_op jit(solution)/shard_map/ppermute | solution.py:236
  8.5 1.6 %collective-permute-done.1 = bf16[2,72,128]{2,1,0:T(8,128)(2,1)S(1)} collective-permute-done((bf16[2,72,128]{2,1,0:T(8,128)(2,1)S(1)}, bf16[2,72,128]{2,1,0:T(8,128)(2,1)S(1)}, u32[]{:S(2)}, u32[]{:S(2)}) %collective-permute-start.1) | collective-permute-done | bytes 36896 | tf_op jit(solution)/shard_map/ppermute | solution.py:236
  10.1 0.7 %pad_maximum_fusion.1 = bf16[4,72,128]{2,1,0:T(8,128)(2,1)S(1)} fusion(bf16[2,72,128]{2,1,0:T(8,128)(2,1)S(1)} %collective-permute-done.1, bf16[1,72,128]{2,1,0:T(8,128)(2,1)S(1)} %collective-permute-done, bf16[1,72,128]{2,1,0:T(8,128)(2,1)} %bitcast.4), kind=kLoop, calls=%fused_computation.1 | loop fusion | flops 73728 | bytes 147456 | tf_op jit(solution)/shard_map/concatenate | solution.py:236
  10.9 2.9 %collective-permute-start.2 = (bf16[4,72,128]{2,1,0:T(8,128)(2,1)S(1)}, bf16[4,72,128]{2,1,0:T(8,128)(2,1)S(1)}, u32[]{:S(2)}, u32[]{:S(2)}) collective-permute-start(bf16[4,72,128]{2,1,0:T(8,128)(2,1)S(1)} %pad_maximum_fusion.1), channel_id=1, source_target_pairs={{0,9},{1,8},{2,11},{3,10},{4,13},{5,12},{6,15},{7,14},{8,1},{9,0},... | collective-permute-start | bytes 221192 | tf_op jit(solution)/shard_map/ppermute | solution.py:236
  13.8 2.4 %collective-permute-done.2 = bf16[4,72,128]{2,1,0:T(8,128)(2,1)S(1)} collective-permute-done((bf16[4,72,128]{2,1,0:T(8,128)(2,1)S(1)}, bf16[4,72,128]{2,1,0:T(8,128)(2,1)S(1)}, u32[]{:S(2)}, u32[]{:S(2)}) %collective-permute-start.2) | collective-permute-done | bytes 73760 | tf_op jit(solution)/shard_map/ppermute | solution.py:236
  16.1 0.7 %pad_maximum_fusion.near_ref = bf16[8,72,128]{2,1,0:T(8,128)(2,1)S(1)} fusion(bf16[4,72,128]{2,1,0:T(8,128)(2,1)S(1)} %collective-permute-done.2, bf16[2,72,128]{2,1,0:T(8,128)(2,1)S(1)} %collective-permute-done.1, bf16[1,72,128]{2,1,0:T(8,128)(2,1)S(1)} %collective-permute-done, bf16[1,72,128]{2,1,0:T(8,128)(2,1)} %bitcast.5), kind=kLoop, calls=%fused_computation | loop fusion | flops 221184 | bytes 294912 | tf_op jit(solution)/shard_map/concatenate | solution.py:236
  16.9 0.0 copy-start
  16.9 1.9 %collective-permute-start.3 = (bf16[8,72,128]{2,1,0:T(8,128)(2,1)S(1)}, bf16[8,72,128]{2,1,0:T(8,128)(2,1)S(1)}, u32[]{:S(2)}, u32[]{:S(2)}) collective-permute-start(bf16[8,72,128]{2,1,0:T(8,128)(2,1)S(1)} %pad_maximum_fusion.near_ref), channel_id=1, source_target_pairs={{0,1},{1,0},{2,3},{3,2},{4,5},{5,4},{6,7},{7,6},{8,9},{9,8},{10,11... | collective-permute-start | bytes 442376 | tf_op jit(solution)/shard_map/ppermute | solution.py:238
  18.8 1.0 %collective-permute-done.3.far_ref = bf16[8,72,128]{2,1,0:T(8,128)(2,1)S(1)} collective-permute-done((bf16[8,72,128]{2,1,0:T(8,128)(2,1)S(1)}, bf16[8,72,128]{2,1,0:T(8,128)(2,1)S(1)}, u32[]{:S(2)}, u32[]{:S(2)}) %collective-permute-start.3) | collective-permute-done | bytes 147488 | tf_op jit(solution)/shard_map/ppermute | solution.py:238
  19.8 0.0 copy-start.1
  19.8 0.0 copy-done
  19.8 0.7 %copy-done.1 = bf16[8,72,128]{2,1,0:T(8,128)(2,1)} copy-done((bf16[8,72,128]{2,1,0:T(8,128)(2,1)}, bf16[8,72,128]{2,1,0:T(8,128)(2,1)S(1)}, u32[]{:S(2)}) %copy-start.1) | copy-done | bytes 147480
  20.5 10.1 %attend.1 = bf16[16,72,128]{2,1,0:T(8,128)(2,1)} custom-call(s32[1]{0:T(128)} %bitcast.me_ref, s32[8]{0:T(128)} %len_ref.1, bf16[8,72,128]{2,1,0:T(8,128)(2,1)} %copy-done, bf16[8,72,128]{2,1,0:T(8,128)(2,1)} %copy-done.1, bf16[1024,1024]{1,0:T(8,128)(2,1)} %dk_ref.1, bf16[1024,1024]{1,0:T(8,128)(2,1)} %dv_ref.1, bf16[1024,1024]{1,0:T(8,128)(2,1)} %sk_ref.1, ...), custom_call_target="tpu_custom_call" | custom-call | tf_op jit(solution)/shard_map/attend/pallas_call | solution.py:239
  30.6 17.3 %all_to_all.5.parts_ref = bf16[16,72,128]{2,1,0:T(8,128)(2,1)} all-to-all(bf16[16,72,128]{2,1,0:T(8,128)(2,1)} %attend.1), channel_id=1, replica_groups=mesh['parts'=2,'seq'=16] {'seq'}, dimensions={0} | all-to-all | bytes 589824 | tf_op jit(solution)/shard_map/all_to_all | solution.py:258
  47.9 2.0 %combine.1 = bf16[1,8192]{1,0:T(2,128)(2,1)} custom-call(bf16[16,72,128]{2,1,0:T(8,128)(2,1)} %all_to_all.5.parts_ref), custom_call_target="tpu_custom_call" | custom-call | tf_op jit(solution)/shard_map/combine/pallas_call | solution.py:259
Async XLA Ops:
  1.4 4.1 %collective-permute-start = (bf16[1,72,128]{2,1,0:T(8,128)(2,1)}, bf16[1,72,128]{2,1,0:T(8,128)(2,1)S(1)}, u32[]{:S(2)}, u32[]{:S(2)}) collective-permute-start(bf16[1,72,128]{2,1,0:T(8,128)(2,1)} %bitcast.2), channel_id=1, source_target_pairs={{0,3},{1,2},{2,1},{3,0},{4,7},{5,6},{6,5},{7,4},{8,11},{9,10},{10,... | collective-permute-start | bytes 55304 | tf_op jit(solution)/shard_map/ppermute | solution.py:236
  6.3 3.9 %collective-permute-start.1 = (bf16[2,72,128]{2,1,0:T(8,128)(2,1)S(1)}, bf16[2,72,128]{2,1,0:T(8,128)(2,1)S(1)}, u32[]{:S(2)}, u32[]{:S(2)}) collective-permute-start(bf16[2,72,128]{2,1,0:T(8,128)(2,1)S(1)} %pad_maximum_fusion.2), channel_id=1, source_target_pairs={{0,5},{1,4},{2,7},{3,6},{4,1},{5,0},{6,3},{7,2},{8,13},{9,12},{10,... | collective-permute-start | bytes 110600 | tf_op jit(solution)/shard_map/ppermute | solution.py:236
  10.9 5.3 %collective-permute-start.2 = (bf16[4,72,128]{2,1,0:T(8,128)(2,1)S(1)}, bf16[4,72,128]{2,1,0:T(8,128)(2,1)S(1)}, u32[]{:S(2)}, u32[]{:S(2)}) collective-permute-start(bf16[4,72,128]{2,1,0:T(8,128)(2,1)S(1)} %pad_maximum_fusion.1), channel_id=1, source_target_pairs={{0,9},{1,8},{2,11},{3,10},{4,13},{5,12},{6,15},{7,14},{8,1},{9,0},... | collective-permute-start | bytes 221192 | tf_op jit(solution)/shard_map/ppermute | solution.py:236
  16.9 3.0 %copy-start = (bf16[8,72,128]{2,1,0:T(8,128)(2,1)}, bf16[8,72,128]{2,1,0:T(8,128)(2,1)S(1)}, u32[]{:S(2)}) copy-start(bf16[8,72,128]{2,1,0:T(8,128)(2,1)S(1)} %pad_maximum_fusion.near_ref) | copy-start | bytes 442372
  16.9 2.9 %collective-permute-start.3 = (bf16[8,72,128]{2,1,0:T(8,128)(2,1)S(1)}, bf16[8,72,128]{2,1,0:T(8,128)(2,1)S(1)}, u32[]{:S(2)}, u32[]{:S(2)}) collective-permute-start(bf16[8,72,128]{2,1,0:T(8,128)(2,1)S(1)} %pad_maximum_fusion.near_ref), channel_id=1, source_target_pairs={{0,1},{1,0},{2,3},{3,2},{4,5},{5,4},{6,7},{7,6},{8,9},{9,8},{10,11... | collective-permute-start | bytes 442376 | tf_op jit(solution)/shard_map/ppermute | solution.py:238
  19.8 0.7 %copy-start.1 = (bf16[8,72,128]{2,1,0:T(8,128)(2,1)}, bf16[8,72,128]{2,1,0:T(8,128)(2,1)S(1)}, u32[]{:S(2)}) copy-start(bf16[8,72,128]{2,1,0:T(8,128)(2,1)S(1)} %collective-permute-done.3.far_ref) | copy-start | bytes 442372

commit v2 on v1

v2 whole, which is shorter than its diff:
```python
import functools
import math

import jax
import jax.numpy as jnp
from jax import lax
from jax.experimental import pallas as pl
from jax.experimental.pallas import tpu as pltpu
from jax.sharding import PartitionSpec as P


HEADS = 64
KVH = 8
HD = 128
BLOCK = 128
GROUPS = HEADS // KVH
LANES = 128
SLOTS = 8

NEG_BIG = -1e30
NEG_SAFE = -5e29
EXP2_SCALE = HD**-0.5 * math.log2(math.e)

VMEM = pltpu.VMEM
SMEM = pltpu.SMEM


def pack_kernel(flag_rows, list_ref, q_ref, out_ref):
    q = q_ref[...].astype(jnp.float32)
    rows = [q[:, h * HD : (h + 1) * HD] for h in range(HEADS)]
    out_ref[0:HEADS, :] = jnp.concatenate(rows, axis=0).astype(jnp.bfloat16)
    ids = (
        lax.broadcasted_iota(jnp.int32, (flag_rows, LANES), 0) * LANES
        + lax.broadcasted_iota(jnp.int32, (flag_rows, LANES), 1)
    )

    def mark(k, found):
        return jnp.where(ids == list_ref[0, k], 1.0, found)

    found = lax.fori_loop(
        0, list_ref.shape[1], mark, jnp.zeros((flag_rows, LANES), jnp.float32), unroll=8
    )
    out_ref[HEADS : HEADS + flag_rows, :] = found.astype(jnp.bfloat16)


def lane_dot(a, b):
    return lax.dot_general(a, b, (((1,), (1,)), ((), ())), preferred_element_type=jnp.float32)


def partial_softmax(scores):
    top = jnp.max(scores, axis=-1, keepdims=True)
    weights = jnp.exp2((scores - jnp.maximum(top, NEG_SAFE)) * EXP2_SCALE)
    return top, jnp.sum(weights, axis=-1, keepdims=True), weights.astype(jnp.bfloat16)


def fetch_kernel(count, *refs):
    sources, targets, sem = refs[:count], refs[count : 2 * count], refs[-1]
    copies = [
        pltpu.make_async_copy(source, target, sem.at[i])
        for i, (source, target) in enumerate(zip(sources, targets))
    ]
    for copy in copies:
        copy.start()
    for copy in copies:
        copy.wait()


def suffix_kernel(
    me_ref, len_ref, own_ref, pair_ref, sk_ref, sv_ref, nk_ref, nv_ref, top_ref, total_ref, out_ref
):
    me = me_ref[0]
    parity = lax.rem(me, 2)
    live_left = len_ref[lax.div(me, 2)] - parity * sk_ref.shape[0]
    for head in range(KVH):
        rows = slice(head * GROUPS, (head + 1) * GROUPS)
        cols = slice(head * HD, (head + 1) * HD)
        q = jnp.concatenate(
            [ref[0, rows, :].astype(jnp.float32) for ref in (own_ref, pair_ref)], axis=0
        )
        scores = lane_dot(q.astype(jnp.bfloat16), sk_ref[:, cols])
        position = lax.broadcasted_iota(jnp.int32, scores.shape, 1)
        scores = jnp.where(position < live_left, scores, NEG_BIG)
        s_top, s_total, weights = partial_softmax(scores)
        s_out = jnp.dot(weights, sv_ref[:, cols], preferred_element_type=jnp.float32)
        n_top = jnp.sum(q * nk_ref[:, cols].astype(jnp.float32), axis=-1, keepdims=True)
        hidden = (lax.broadcasted_iota(jnp.int32, n_top.shape, 0) >= GROUPS) & (parity == 1)
        n_top = jnp.where(hidden, NEG_BIG, n_top)
        top = jnp.maximum(s_top, n_top)
        base = jnp.maximum(top, NEG_SAFE)
        s_scale = jnp.exp2((s_top - base) * EXP2_SCALE)
        n_scale = jnp.exp2((n_top - base) * EXP2_SCALE)
        top_ref[head] = jnp.broadcast_to(top, (2 * GROUPS, LANES))
        total_ref[head] = jnp.broadcast_to(s_scale * s_total + n_scale, (2 * GROUPS, LANES))
        out_ref[head] = s_scale * s_out + n_scale * nv_ref[:, cols].astype(jnp.float32)


def split_stats(stats, axis):
    high = stats.astype(jnp.bfloat16).astype(jnp.float32)
    rest = stats - high
    middle = rest.astype(jnp.bfloat16).astype(jnp.float32)
    low = rest - middle
    packed = high + pltpu.roll(middle, 2 * KVH, axis) + pltpu.roll(low, 4 * KVH, axis)
    return packed.astype(jnp.bfloat16)


def join_stats(packed, axis):
    packed = packed.astype(jnp.float32)
    stats = (
        packed
        + pltpu.roll(packed, LANES - 2 * KVH, axis)
        + pltpu.roll(packed, LANES - 4 * KVH, axis)
    )
    live = lax.broadcasted_iota(jnp.int32, stats.shape, axis) < KVH
    top = jnp.where(live, stats, 0.0)
    total = jnp.where(live, pltpu.roll(stats, LANES - KVH, axis), 0.0)
    return top, total


def attend_kernel(
    flag_rows,
    me_ref,
    near_ref,
    far_ref,
    dk_ref,
    dv_ref,
    top_ref,
    total_ref,
    extra_ref,
    near_out_ref,
    far_out_ref,
    bias_ref,
):
    half_tokens = near_ref.shape[0]
    span = dk_ref.shape[0]
    half = SLOTS * GROUPS
    first_block = me_ref[0] * (span // BLOCK)
    flag_row = lax.div(first_block, LANES)
    flag_lane = lax.rem(first_block, LANES)
    row_ids = lax.broadcasted_iota(jnp.int32, (1, flag_rows, LANES), 1)
    pick = (
        lax.broadcasted_iota(jnp.int32, (LANES, span), 0)
        == flag_lane + lax.broadcasted_iota(jnp.int32, (LANES, span), 1) // BLOCK
    ).astype(jnp.float32).astype(jnp.bfloat16)
    lane_ids = lax.broadcasted_iota(jnp.int32, (2 * half, LANES), 1)

    def do_chunk(chunk, local):
        start = chunk * SLOTS
        slots = pl.ds(start, SLOTS)
        flags = near_ref[slots, HEADS:, :].astype(jnp.float32) + far_ref[slots, HEADS:, :].astype(
            jnp.float32
        )
        flags = jnp.sum(jnp.where(row_ids == flag_row, flags, 0.0), axis=1)
        count = jnp.dot(flags.astype(jnp.bfloat16), pick, preferred_element_type=jnp.float32)
        bias = jnp.where(count > 0.5, 0.0, NEG_BIG)
        for s in range(SLOTS):
            bias_ref[s * GROUPS : (s + 1) * GROUPS, :] = jnp.broadcast_to(
                bias[s : s + 1, :], (GROUPS, span)
            )

        def scores_of(head):
            rows = slice(head * GROUPS, (head + 1) * GROUPS)
            q = jnp.concatenate(
                [
                    ref[slots, rows, :].astype(jnp.float32).reshape(half, HD)
                    for ref in (near_ref, far_ref)
                ],
                axis=0,
            ).astype(jnp.bfloat16)
            scores = lane_dot(q, dk_ref[:, head * HD : (head + 1) * HD])
            bias = bias_ref[...]
            return scores + jnp.concatenate([bias, bias], axis=0)

        stats = jnp.zeros((2 * half, LANES), jnp.float32)
        upcoming = scores_of(0)
        for head in range(KVH):
            rows = slice(head * GROUPS, (head + 1) * GROUPS)
            cols = slice(head * HD, (head + 1) * HD)
            scores = upcoming
            if head + 1 < KVH:
                upcoming = scores_of(head + 1)
            top, total, weights = partial_softmax(scores)
            out = jnp.dot(weights, dv_ref[:, cols], preferred_element_type=jnp.float32)
            if local:

                def joined(at, x_top, x_total, x_out):
                    own = slice(at * GROUPS, (at + 1) * GROUPS)
                    y_top = top_ref[head, own, 0:1]
                    new_top = jnp.maximum(x_top, y_top)
                    base = jnp.maximum(new_top, NEG_SAFE)
                    x_scale = jnp.exp2((x_top - base) * EXP2_SCALE)
                    y_scale = jnp.exp2((y_top - base) * EXP2_SCALE)
                    return (
                        new_top,
                        x_scale * x_total + y_scale * total_ref[head, own, 0:1],
                        x_scale * x_out + y_scale * extra_ref[head, own, :],
                    )

                pieces = []
                for at in range(2):
                    lo = at * half
                    first = slice(lo, lo + GROUPS)
                    others = slice(lo + GROUPS, lo + half)
                    new = joined(at, top[first], total[first], out[first])
                    pieces.append(new)
                    pieces.append((top[others], total[others], out[others]))
                top, total, out = [jnp.concatenate(p, axis=0) for p in zip(*pieces)]
            units = (out / jnp.maximum(total, 1.0)).astype(jnp.bfloat16)
            stats = jnp.where(lane_ids == head, top * EXP2_SCALE, stats)
            stats = jnp.where(lane_ids == KVH + head, total, stats)
            near_out_ref[slots, rows, :] = units[:half].reshape(SLOTS, GROUPS, HD)
            far_out_ref[slots, rows, :] = units[half:].reshape(SLOTS, GROUPS, HD)
        packed = split_stats(stats, 1)
        rows = slice(HEADS, HEADS + GROUPS)
        near_out_ref[slots, rows, :] = packed[:half].reshape(SLOTS, GROUPS, LANES)
        far_out_ref[slots, rows, :] = packed[half:].reshape(SLOTS, GROUPS, LANES)

    do_chunk(0, True)
    chunks = half_tokens // SLOTS
    if chunks > 1:
        lax.fori_loop(1, chunks, lambda c, _: do_chunk(c, False), None)


def mix_weights(mine_ref, theirs_ref):
    rows = slice(HEADS, HEADS + GROUPS)
    a_top, a_total = join_stats(mine_ref[:, rows, :], 2)
    b_top, b_total = join_stats(theirs_ref[:, rows, :], 2)
    top = jnp.maximum(a_top, b_top)
    a_weight = jnp.exp2(a_top - top) * a_total
    b_weight = jnp.exp2(b_top - top) * b_total
    total = a_weight + b_weight
    scale = 1.0 / jnp.maximum(total, 1.0)
    return top, total, a_weight * scale, b_weight * scale


def mixed_units(head, mine_ref, theirs_ref, a_weight, b_weight):
    rows = slice(head * GROUPS, (head + 1) * GROUPS)
    one = slice(head, head + 1)
    return mine_ref[:, rows, :].astype(jnp.float32) * a_weight[:, :, one] + theirs_ref[
        :, rows, :
    ].astype(jnp.float32) * b_weight[:, :, one]


def merge_kernel(mine_ref, theirs_ref, keep_ref, send_ref):
    half = keep_ref.shape[0]
    top, total, a_weight, b_weight = mix_weights(mine_ref, theirs_ref)
    for head in range(KVH):
        rows = slice(head * GROUPS, (head + 1) * GROUPS)
        units = mixed_units(head, mine_ref, theirs_ref, a_weight, b_weight).astype(jnp.bfloat16)
        keep_ref[:, rows, :] = units[:half]
        send_ref[:, rows, :] = units[half:]
    packed = split_stats(top + pltpu.roll(total, KVH, 2), 2)
    keep_ref[:, HEADS : HEADS + GROUPS, :] = packed[:half]
    send_ref[:, HEADS : HEADS + GROUPS, :] = packed[half:]


def finish_kernel(mine_ref, theirs_ref, out_ref):
    _, _, a_weight, b_weight = mix_weights(mine_ref, theirs_ref)
    for head in range(KVH):
        units = mixed_units(head, mine_ref, theirs_ref, a_weight, b_weight)[0]
        for g in range(GROUPS):
            h = head * GROUPS + g
            out_ref[:, h * HD : (h + 1) * HD] = units[g : g + 1, :].astype(jnp.bfloat16)


def whole(space=VMEM):
    return pl.BlockSpec(memory_space=space)


def near_core(x):
    return pltpu.with_memory_space_constraint(x, VMEM)


def on_core(kernel, out_shape, operands, scalars=0, cost=None, **kwargs):
    in_specs = [whole(SMEM)] * scalars + [whole()] * (len(operands) - scalars)
    return pl.pallas_call(
        kernel,
        out_shape=out_shape,
        in_specs=kwargs.pop("in_specs", in_specs),
        out_specs=jax.tree.map(lambda _: whole(), out_shape),
        compiler_params=pltpu.CompilerParams(vmem_limit_bytes=16 << 20),
        cost_estimate=cost,
        **kwargs,
    )(*operands)


def swap(x, bits):
    devices = lax.axis_size("seq")
    return lax.ppermute(x, "seq", [(i, i ^ bits) for i in range(devices)])


def per_device(
    queries,
    new_keys,
    new_values,
    doc_keys,
    doc_values,
    suffix_keys,
    suffix_values,
    keep_lists,
    suffix_lengths,
):
    devices = lax.axis_size("seq")
    me = lax.axis_index("seq").astype(jnp.int32).reshape(1)
    blocks = devices * doc_keys.shape[0] // BLOCK
    flag_rows = 8 * pl.cdiv(blocks, 8 * LANES)
    strides = []
    while 2 ** (len(strides) + 1) < devices:
        strides.insert(0, 2 ** (len(strides) + 1) | 1)
    packed = on_core(
        functools.partial(pack_kernel, flag_rows),
        VMEM((HEADS + flag_rows, HD), jnp.bfloat16),
        (keep_lists, queries),
        scalars=1,
    )
    near = packed[None]
    own = near
    caches = (doc_keys, doc_values, suffix_keys, suffix_values)
    size = sum(c.size * 2 for c in caches)
    dk, dv, sk, sv = on_core(
        functools.partial(fetch_kernel, len(caches)),
        [VMEM(c.shape, c.dtype) for c in caches],
        [pltpu.with_memory_space_constraint(c, pltpu.HBM) for c in caches],
        in_specs=[whole(pltpu.HBM)] * len(caches),
        scratch_shapes=[pltpu.SemaphoreType.DMA((len(caches),))],
        cost=pl.CostEstimate(flops=0, bytes_accessed=size, transcendentals=0),
    )
    pair = swap(own, 1)
    stat = VMEM((KVH, 2 * GROUPS, LANES), jnp.float32)
    local = on_core(
        suffix_kernel,
        [stat, stat, VMEM((KVH, 2 * GROUPS, HD), jnp.float32)],
        (me, suffix_lengths, own, near_core(pair), sk, sv, new_keys, new_values),
        scalars=2,
        cost=pl.CostEstimate(flops=10**9, bytes_accessed=size // 2, transcendentals=10**6),
    )
    for bits in strides:
        arrived = swap(near, bits)
        near = jnp.concatenate([near, arrived], axis=0)
    far = swap(near, 1)
    tokens = lambda count: VMEM((count, HEADS + GROUPS, HD), jnp.bfloat16)
    keep, send = on_core(
        functools.partial(attend_kernel, flag_rows),
        [tokens(devices // 2)] * 2,
        (me, near_core(near), near_core(far), dk, dv, *local),
        scalars=1,
        scratch_shapes=[VMEM((SLOTS * GROUPS, doc_keys.shape[0]), jnp.float32)],
    )
    bits = 1
    while strides:
        count = keep.shape[0] // 2
        keep, send = on_core(merge_kernel, [tokens(count)] * 2, (keep, near_core(swap(send, bits))))
        bits = strides.pop()
    return on_core(
        finish_kernel,
        jax.ShapeDtypeStruct((1, HEADS * HD), jnp.bfloat16),
        (keep, near_core(swap(send, bits))),
    )


def solution(mesh):
    split = P(("parts", "seq"), None)
    return jax.shard_map(
        per_device,
        mesh=mesh,
        in_specs=(split,) * 8 + (P("parts"),),
        out_specs=split,
        check_vma=False,
    )
```

time: 50.3 us -> 41.6 us (0.83)
  blocking collectives: 17.3 us -> 0 us
  starting transfers between devices: 9.49 us -> 15.3 us
  waiting for transfers between devices: 6.7 us -> 12 us
  other arithmetic: 2.2 us -> 0.03 us
  Pallas kernels: 13.5 us -> 12.5 us
  local copies, waits for them, and re-layouts: 0.66 us -> 1.42 us
    all_to_all x1 -> x0, blocking collectives: 17.3 us -> none  [per_device(): lax.all_to_all(spread, 'seq', split_axis=0, concat_axis=0, tiled=True)]
    ppermute x4 -> x9, starting transfers between devices: 9.49 us -> 15.3 us  [swap(): return lax.ppermute(x, 'seq', [(i, i ^ bits) for i in range(devices)])]
    ppermute x4 -> x9, waiting for transfers between devices: 6.7 us -> 12 us  [swap(): return lax.ppermute(x, 'seq', [(i, i ^ bits) for i in range(devices)])]
    concatenate x3, other arithmetic: 2.2 us -> 0.03 us  [per_device(): near = jnp.concatenate([near, arrived], axis=0)]
    pallas_call x3 -> x8, Pallas kernels: 13.5 us -> 12.5 us  [on_core(): pl.pallas_call(kernel, out_shape=out_shape, in_specs=kwargs.pop('in_specs...]
    unnamed x4 -> x10, local copies, waits for them, and re-layouts: 0.66 us -> 1.42 us
  transfers between devices with their start and end apart: 4 -> 9, of which waited for: 4 -> 7; matrix products, arithmetic and copies ran while one was open for 0% -> 0% of each run, Pallas kernels for 0% -> 16%
where the time goes in v2:
time: 41.6 us; the launch traced here: 41.4 us
  starting transfers between devices  15.3 us (37%)
  Pallas kernels  12.5 us (30%)
  waiting for transfers between devices  12 us (29%)
  local copies, waits for them, and re-layouts  1.42 us (3%)
    ppermute x9, starting transfers between devices, swap(): return lax.ppermute(x, 'seq', [(i, i ^ bits) for i in range(devices)])  15.3 us
    pallas_call x8, Pallas kernels, on_core(): pl.pallas_call(kernel, out_shape=out_shape, in_specs=kwargs.pop('in_specs...  12.5 us
    ppermute x9, waiting for transfers between devices, swap(): return lax.ppermute(x, 'seq', [(i, i ^ bits) for i in range(devices)])  12 us
    unnamed x10, local copies, waits for them, and re-layouts  1.42 us
  transfers between devices with their start and end apart: 9, of which 7 were waited for; matrix products, arithmetic and copies ran while one was open for 0% of the time, Pallas kernels for 16%

profile of v2, /device:TPU:0, one launch (start us, length us, event | category | flops | bytes accessed | tf_op | source)
XLA Modules:
  0.0 41.4 jit_solution(4347367974676719866)
XLA Ops:
  0.0 0.8 %copy-done = bf16[1,8192]{1,0:T(2,128)(2,1)S(1)} copy-done((bf16[1,8192]{1,0:T(2,128)(2,1)S(1)}, bf16[1,8192]{1,0:T(2,128)(2,1)}, u32[]{:S(2)}) %copy-start) | copy-done | bytes 16408
  0.8 0.7 %copy-done.3 = s32[1,32]{1,0:T(1,128)S(1)} copy-done((s32[1,32]{1,0:T(1,128)S(1)}, s32[1,32]{1,0:T(1,128)}, u32[]{:S(2)}) %copy-start.3) | copy-done | bytes 152
  1.4 0.6 %shard_map.91 = bf16[72,128]{1,0:T(8,128)(2,1)S(1)} custom-call(s32[1,32]{1,0:T(1,128)S(1)} %copy-done.3, bf16[1,8192]{1,0:T(2,128)(2,1)S(1)} %copy-done), custom_call_target="tpu_custom_call" | custom-call | tf_op jit(solution)/shard_map/pallas_call | solution.py:275
  2.0 3.6 %collective-permute-start = (bf16[1,72,128]{2,1,0:T(8,128)(2,1)S(1)}, bf16[1,72,128]{2,1,0:T(8,128)(2,1)S(1)}, u32[]{:S(2)}, u32[]{:S(2)}) collective-permute-start(bf16[1,72,128]{2,1,0:T(8,128)(2,1)S(1)} %bitcast.2), channel_id=1, source_target_pairs={{0,9},{1,8},{2,11},{3,10},{4,13},{5,12},{6,15},{7,14},{8,1},{9,0},... | collective-permute-start | bytes 55304 | tf_op jit(solution)/shard_map/ppermute | solution.py:288
  5.6 1.5 %collective-permute-done = bf16[1,72,128]{2,1,0:T(8,128)(2,1)S(1)} collective-permute-done((bf16[1,72,128]{2,1,0:T(8,128)(2,1)S(1)}, bf16[1,72,128]{2,1,0:T(8,128)(2,1)S(1)}, u32[]{:S(2)}, u32[]{:S(2)}) %collective-permute-start) | collective-permute-done | bytes 18464 | tf_op jit(solution)/shard_map/ppermute | solution.py:288
  7.1 1.9 %collective-permute-start.1 = (bf16[2,72,128]{2,1,0:T(8,128)(2,1)S(1)}, bf16[2,72,128]{2,1,0:T(8,128)(2,1)S(1)}, u32[]{:S(2)}, u32[]{:S(2)}) collective-permute-start(bf16[2,72,128]{2,1,0:T(8,128)(2,1)S(1)} %pad_maximum_fusion.2), channel_id=1, source_target_pairs={{0,5},{1,4},{2,7},{3,6},{4,1},{5,0},{6,3},{7,2},{8,13},{9,12},{10,... | collective-permute-start | bytes 110600 | tf_op jit(solution)/shard_map/ppermute | solution.py:288
  9.0 1.6 %collective-permute-done.1 = bf16[2,72,128]{2,1,0:T(8,128)(2,1)S(1)} collective-permute-done((bf16[2,72,128]{2,1,0:T(8,128)(2,1)S(1)}, bf16[2,72,128]{2,1,0:T(8,128)(2,1)S(1)}, u32[]{:S(2)}, u32[]{:S(2)}) %collective-permute-start.1) | collective-permute-done | bytes 36896 | tf_op jit(solution)/shard_map/ppermute | solution.py:288
  10.6 1.8 %collective-permute-start.2 = (bf16[4,72,128]{2,1,0:T(8,128)(2,1)S(1)}, bf16[4,72,128]{2,1,0:T(8,128)(2,1)S(1)}, u32[]{:S(2)}, u32[]{:S(2)}) collective-permute-start(bf16[4,72,128]{2,1,0:T(8,128)(2,1)S(1)} %pad_maximum_fusion.1), channel_id=1, source_target_pairs={{0,3},{1,2},{2,1},{3,0},{4,7},{5,6},{6,5},{7,4},{8,11},{9,10},{10,... | collective-permute-start | bytes 221192 | tf_op jit(solution)/shard_map/ppermute | solution.py:288
  12.4 2.4 %collective-permute-done.2 = bf16[4,72,128]{2,1,0:T(8,128)(2,1)S(1)} collective-permute-done((bf16[4,72,128]{2,1,0:T(8,128)(2,1)S(1)}, bf16[4,72,128]{2,1,0:T(8,128)(2,1)S(1)}, u32[]{:S(2)}, u32[]{:S(2)}) %collective-permute-start.2) | collective-permute-done | bytes 73760 | tf_op jit(solution)/shard_map/ppermute | solution.py:288
  14.8 0.3 collective-permute-start.3
  15.4 3.5 %shard_map.92 = (bf16[1024,1024]{1,0:T(8,128)(2,1)S(1)}, bf16[1024,1024]{1,0:T(8,128)(2,1)S(1)}, bf16[1024,1024]{1,0:T(8,128)(2,1)S(1)}, bf16[1024,1024]{1,0:T(8,128)(2,1)S(1)}) custom-call(bf16[1024,1024]{1,0:T(8,128)(2,1)} %refs_0_.1, bf16[1024,1024]{1,0:T(8,128)(2,1)} %refs_1_.1, bf16[1024,1024]{1,0:T(8,128)(2,1)} %refs_2_.1, bf16[1024,1024]{1,0:T(8,128)(2,1)} %refs_3_.1), custom_call_target="tpu_custom_call" | custom-call | bytes 8388608 | tf_op jit(solution)/shard_map/pallas_call | solution.py:275
  19.0 3.1 %shard_map.93 = (f32[8,16,128]{2,1,0:T(8,128)S(1)}, f32[8,16,128]{2,1,0:T(8,128)S(1)}, f32[8,16,128]{2,1,0:T(8,128)S(1)}) custom-call(s32[1]{0:T(128)} %bitcast.me_ref, s32[8]{0:T(128)S(1)} %copy-done.4, bf16[1,72,128]{2,1,0:T(8,128)(2,1)S(1)} %bitcast.7, bf16[1,72,128]{2,1,0:T(8,128)(2,1)S(1)} %collective-permute-done.4.pair_ref, ...), custom_call_target="tpu_custom_call" | custom-call | flops 1000000000 | bytes 4194304 | tf_op jit(solution)/shard_map/pallas_call | solution.py:275
  22.1 3.4 %shard_map.94 = (bf16[8,72,128]{2,1,0:T(8,128)(2,1)S(1)}, bf16[8,72,128]{2,1,0:T(8,128)(2,1)S(1)}) custom-call(s32[1]{0:T(128)} %bitcast.me_ref, bf16[8,72,128]{2,1,0:T(8,128)(2,1)S(1)} %pad_maximum_fusion.near_ref, bf16[8,72,128]{2,1,0:T(8,128)(2,1)S(1)} %collective-permute-done.3.far_ref, bf16[1024,1024]{1,0:T(8,128)(2,1)S(1)} %get-tuple-element.20.dk_ref, ...), custom_call_target="tpu_custom_call" | custom-call | tf_op jit(solution)/shard_map/pallas_call | solution.py:275
  25.4 0.3 collective-permute-start.5
  25.8 1.1 %collective-permute-done.5.theirs_ref = bf16[8,72,128]{2,1,0:T(8,128)(2,1)S(1)} collective-permute-done((bf16[8,72,128]{2,1,0:T(8,128)(2,1)S(1)}, bf16[8,72,128]{2,1,0:T(8,128)(2,1)S(1)}, u32[]{:S(2)}, u32[]{:S(2)}) %collective-permute-start.5) | collective-permute-done | bytes 147488 | tf_op jit(solution)/shard_map/ppermute | solution.py:288
  26.9 0.4 %shard_map.95 = (bf16[4,72,128]{2,1,0:T(8,128)(2,1)S(1)}, bf16[4,72,128]{2,1,0:T(8,128)(2,1)S(1)}) custom-call(bf16[8,72,128]{2,1,0:T(8,128)(2,1)S(1)} %get-tuple-element.27.mine_ref, bf16[8,72,128]{2,1,0:T(8,128)(2,1)S(1)} %collective-permute-done.5.theirs_ref), custom_call_target="tpu_custom_call" | custom-call | tf_op jit(solution)/shard_map/pallas_call | solution.py:275
  27.3 2.0 %collective-permute-start.6 = (bf16[4,72,128]{2,1,0:T(8,128)(2,1)S(1)}, bf16[4,72,128]{2,1,0:T(8,128)(2,1)S(1)}, u32[]{:S(2)}, u32[]{:S(2)}) collective-permute-start(bf16[4,72,128]{2,1,0:T(8,128)(2,1)S(1)} %get-tuple-element.30), channel_id=1, source_target_pairs={{0,3},{1,2},{2,1},{3,0},{4,7},{5,6},{6,5},{7,4},{8,11},{9,10},{10,... | collective-permute-start | bytes 221192 | tf_op jit(solution)/shard_map/ppermute | solution.py:288
  29.3 2.3 %collective-permute-done.6.theirs_ref = bf16[4,72,128]{2,1,0:T(8,128)(2,1)S(1)} collective-permute-done((bf16[4,72,128]{2,1,0:T(8,128)(2,1)S(1)}, bf16[4,72,128]{2,1,0:T(8,128)(2,1)S(1)}, u32[]{:S(2)}, u32[]{:S(2)}) %collective-permute-start.6) | collective-permute-done | bytes 73760 | tf_op jit(solution)/shard_map/ppermute | solution.py:288
  31.7 0.3 shard_map.96
  32.0 2.1 %collective-permute-start.7 = (bf16[2,72,128]{2,1,0:T(8,128)(2,1)S(1)}, bf16[2,72,128]{2,1,0:T(8,128)(2,1)S(1)}, u32[]{:S(2)}, u32[]{:S(2)}) collective-permute-start(bf16[2,72,128]{2,1,0:T(8,128)(2,1)S(1)} %get-tuple-element.32), channel_id=1, source_target_pairs={{0,5},{1,4},{2,7},{3,6},{4,1},{5,0},{6,3},{7,2},{8,13},{9,12},{10,... | collective-permute-start | bytes 110600 | tf_op jit(solution)/shard_map/ppermute | solution.py:288
  34.0 1.6 %collective-permute-done.7.theirs_ref = bf16[2,72,128]{2,1,0:T(8,128)(2,1)S(1)} collective-permute-done((bf16[2,72,128]{2,1,0:T(8,128)(2,1)S(1)}, bf16[2,72,128]{2,1,0:T(8,128)(2,1)S(1)}, u32[]{:S(2)}, u32[]{:S(2)}) %collective-permute-start.7) | collective-permute-done | bytes 36896 | tf_op jit(solution)/shard_map/ppermute | solution.py:288
  36.0 3.1 %collective-permute-start.8 = (bf16[1,72,128]{2,1,0:T(8,128)(2,1)S(1)}, bf16[1,72,128]{2,1,0:T(8,128)(2,1)S(1)}, u32[]{:S(2)}, u32[]{:S(2)}) collective-permute-start(bf16[1,72,128]{2,1,0:T(8,128)(2,1)S(1)} %get-tuple-element.34), channel_id=1, source_target_pairs={{0,9},{1,8},{2,11},{3,10},{4,13},{5,12},{6,15},{7,14},{8,1},{9,0},... | collective-permute-start | bytes 55304 | tf_op jit(solution)/shard_map/ppermute | solution.py:288
  39.0 1.5 %collective-permute-done.8.theirs_ref = bf16[1,72,128]{2,1,0:T(8,128)(2,1)S(1)} collective-permute-done((bf16[1,72,128]{2,1,0:T(8,128)(2,1)S(1)}, bf16[1,72,128]{2,1,0:T(8,128)(2,1)S(1)}, u32[]{:S(2)}, u32[]{:S(2)}) %collective-permute-start.8) | collective-permute-done | bytes 18464 | tf_op jit(solution)/shard_map/ppermute | solution.py:288
  40.5 0.9 %shard_map.98 = bf16[1,8192]{1,0:T(2,128)(2,1)} custom-call(bf16[1,72,128]{2,1,0:T(8,128)(2,1)S(1)} %get-tuple-element.33.mine_ref, bf16[1,72,128]{2,1,0:T(8,128)(2,1)S(1)} %collective-permute-done.8.theirs_ref), custom_call_target="tpu_custom_call" | custom-call | tf_op jit(solution)/shard_map/pallas_call | solution.py:275
  (15 shorter events, 0.6 us)
Async XLA Ops:
  0.0 0.8 %copy-start = (bf16[1,8192]{1,0:T(2,128)(2,1)S(1)}, bf16[1,8192]{1,0:T(2,128)(2,1)}, u32[]{:S(2)}) copy-start(bf16[1,8192]{1,0:T(2,128)(2,1)} %q_ref.1) | copy-start | bytes 49156
  0.8 0.7 %copy-start.3 = (s32[1,32]{1,0:T(1,128)S(1)}, s32[1,32]{1,0:T(1,128)}, u32[]{:S(2)}) copy-start(s32[1,32]{1,0:T(1,128)} %list_ref.1) | copy-start | bytes 388
  2.0 5.0 %collective-permute-start = (bf16[1,72,128]{2,1,0:T(8,128)(2,1)S(1)}, bf16[1,72,128]{2,1,0:T(8,128)(2,1)S(1)}, u32[]{:S(2)}, u32[]{:S(2)}) collective-permute-start(bf16[1,72,128]{2,1,0:T(8,128)(2,1)S(1)} %bitcast.2), channel_id=1, source_target_pairs={{0,9},{1,8},{2,11},{3,10},{4,13},{5,12},{6,15},{7,14},{8,1},{9,0},... | collective-permute-start | bytes 55304 | tf_op jit(solution)/shard_map/ppermute | solution.py:288
  7.1 3.5 %collective-permute-start.1 = (bf16[2,72,128]{2,1,0:T(8,128)(2,1)S(1)}, bf16[2,72,128]{2,1,0:T(8,128)(2,1)S(1)}, u32[]{:S(2)}, u32[]{:S(2)}) collective-permute-start(bf16[2,72,128]{2,1,0:T(8,128)(2,1)S(1)} %pad_maximum_fusion.2), channel_id=1, source_target_pairs={{0,5},{1,4},{2,7},{3,6},{4,1},{5,0},{6,3},{7,2},{8,13},{9,12},{10,... | collective-permute-start | bytes 110600 | tf_op jit(solution)/shard_map/ppermute | solution.py:288
  10.6 4.2 %collective-permute-start.2 = (bf16[4,72,128]{2,1,0:T(8,128)(2,1)S(1)}, bf16[4,72,128]{2,1,0:T(8,128)(2,1)S(1)}, u32[]{:S(2)}, u32[]{:S(2)}) collective-permute-start(bf16[4,72,128]{2,1,0:T(8,128)(2,1)S(1)} %pad_maximum_fusion.1), channel_id=1, source_target_pairs={{0,3},{1,2},{2,1},{3,0},{4,7},{5,6},{6,5},{7,4},{8,11},{9,10},{10,... | collective-permute-start | bytes 221192 | tf_op jit(solution)/shard_map/ppermute | solution.py:288
  14.8 7.2 %collective-permute-start.3 = (bf16[8,72,128]{2,1,0:T(8,128)(2,1)S(1)}, bf16[8,72,128]{2,1,0:T(8,128)(2,1)S(1)}, u32[]{:S(2)}, u32[]{:S(2)}) collective-permute-start(bf16[8,72,128]{2,1,0:T(8,128)(2,1)S(1)} %pad_maximum_fusion.near_ref), channel_id=1, source_target_pairs={{0,1},{1,0},{2,3},{3,2},{4,5},{5,4},{6,7},{7,6},{8,9},{9,8},{10,11... | collective-permute-start | bytes 442376 | tf_op jit(solution)/shard_map/ppermute | solution.py:288
  15.2 3.8 %collective-permute-start.4 = (bf16[1,72,128]{2,1,0:T(8,128)(2,1)S(1)}, bf16[1,72,128]{2,1,0:T(8,128)(2,1)S(1)}, u32[]{:S(2)}, u32[]{:S(2)}) collective-permute-start(bf16[1,72,128]{2,1,0:T(8,128)(2,1)S(1)} %bitcast.6), channel_id=1, source_target_pairs={{0,1},{1,0},{2,3},{3,2},{4,5},{5,4},{6,7},{7,6},{8,9},{9,8},{10,11... | collective-permute-start | bytes 55304 | tf_op jit(solution)/shard_map/ppermute | solution.py:288
  15.4 3.6 %copy-start.1 = (bf16[1,1024]{1,0:T(2,128)(2,1)S(1)}, bf16[1,1024]{1,0:T(2,128)(2,1)}, u32[]{:S(2)}) copy-start(bf16[1,1024]{1,0:T(2,128)(2,1)} %nk_ref.1) | copy-start | bytes 6148
  15.4 3.6 %copy-start.2 = (bf16[1,1024]{1,0:T(2,128)(2,1)S(1)}, bf16[1,1024]{1,0:T(2,128)(2,1)}, u32[]{:S(2)}) copy-start(bf16[1,1024]{1,0:T(2,128)(2,1)} %nv_ref.1) | copy-start | bytes 6148
  15.4 3.6 %copy-start.4 = (s32[8]{0:T(128)S(1)}, s32[8]{0:T(128)}, u32[]{:S(2)}) copy-start(s32[8]{0:T(128)} %len_ref.1) | copy-start | bytes 100
  25.4 1.4 %collective-permute-start.5 = (bf16[8,72,128]{2,1,0:T(8,128)(2,1)S(1)}, bf16[8,72,128]{2,1,0:T(8,128)(2,1)S(1)}, u32[]{:S(2)}, u32[]{:S(2)}) collective-permute-start(bf16[8,72,128]{2,1,0:T(8,128)(2,1)S(1)} %get-tuple-element.28), channel_id=1, source_target_pairs={{0,1},{1,0},{2,3},{3,2},{4,5},{5,4},{6,7},{7,6},{8,9},{9,8},{10,11... | collective-permute-start | bytes 442376 | tf_op jit(solution)/shard_map/ppermute | solution.py:288
  27.3 4.3 %collective-permute-start.6 = (bf16[4,72,128]{2,1,0:T(8,128)(2,1)S(1)}, bf16[4,72,128]{2,1,0:T(8,128)(2,1)S(1)}, u32[]{:S(2)}, u32[]{:S(2)}) collective-permute-start(bf16[4,72,128]{2,1,0:T(8,128)(2,1)S(1)} %get-tuple-element.30), channel_id=1, source_target_pairs={{0,3},{1,2},{2,1},{3,0},{4,7},{5,6},{6,5},{7,4},{8,11},{9,10},{10,... | collective-permute-start | bytes 221192 | tf_op jit(solution)/shard_map/ppermute | solution.py:288
  32.0 3.7 %collective-permute-start.7 = (bf16[2,72,128]{2,1,0:T(8,128)(2,1)S(1)}, bf16[2,72,128]{2,1,0:T(8,128)(2,1)S(1)}, u32[]{:S(2)}, u32[]{:S(2)}) collective-permute-start(bf16[2,72,128]{2,1,0:T(8,128)(2,1)S(1)} %get-tuple-element.32), channel_id=1, source_target_pairs={{0,5},{1,4},{2,7},{3,6},{4,1},{5,0},{6,3},{7,2},{8,13},{9,12},{10,... | collective-permute-start | bytes 110600 | tf_op jit(solution)/shard_map/ppermute | solution.py:288
  36.0 4.5 %collective-permute-start.8 = (bf16[1,72,128]{2,1,0:T(8,128)(2,1)S(1)}, bf16[1,72,128]{2,1,0:T(8,128)(2,1)S(1)}, u32[]{:S(2)}, u32[]{:S(2)}) collective-permute-start(bf16[1,72,128]{2,1,0:T(8,128)(2,1)S(1)} %get-tuple-element.34), channel_id=1, source_target_pairs={{0,9},{1,8},{2,11},{3,10},{4,13},{5,12},{6,15},{7,14},{8,1},{9,0},... | collective-permute-start | bytes 55304 | tf_op jit(solution)/shard_map/ppermute | solution.py:288

commit v3 on v2

v3 whole, which is shorter than its diff:
```python
import functools
import math

import jax
import jax.numpy as jnp
from jax import lax
from jax.experimental import pallas as pl
from jax.experimental.pallas import tpu as pltpu
from jax.sharding import PartitionSpec as P


HEADS = 64
KVH = 8
HD = 128
BLOCK = 128
GROUPS = HEADS // KVH
LANES = 128
SLOTS = 8

NEG_BIG = -1e30
NEG_SAFE = -5e29
AHEAD = 2
EXP2_SCALE = HD**-0.5 * math.log2(math.e)

VMEM = pltpu.VMEM


def pack_kernel(list_ref, q_ref, out_ref):
    q = q_ref[...].astype(jnp.float32)
    rows = [q[:, h * HD : (h + 1) * HD] for h in range(HEADS)]
    out_ref[0:HEADS, :] = jnp.concatenate(rows, axis=0).astype(jnp.bfloat16)
    entries = list_ref.shape[1]
    ids = list_ref[...].astype(jnp.float32)
    diagonal = lax.broadcasted_iota(jnp.int32, (entries, entries), 0) == lax.broadcasted_iota(
        jnp.int32, (entries, entries), 1
    )
    column = jnp.sum(jnp.where(diagonal, ids, 0.0), axis=1, keepdims=True)
    lanes = lax.broadcasted_iota(jnp.int32, (entries, LANES), 1).astype(jnp.float32)
    found = [
        jnp.max(jnp.where(column == lanes + float(i * LANES), 1.0, 0.0), axis=0, keepdims=True)
        for i in range(out_ref.shape[0] - HEADS)
    ]
    out_ref[HEADS:, :] = jnp.concatenate(found, axis=0).astype(jnp.bfloat16)


def lane_dot(a, b):
    return lax.dot_general(a, b, (((1,), (1,)), ((), ())), preferred_element_type=jnp.float32)


def partial_softmax(scores):
    top = jnp.max(scores, axis=-1, keepdims=True)
    weights = jnp.exp2((scores - jnp.maximum(top, NEG_SAFE)) * EXP2_SCALE)
    return top, jnp.sum(weights, axis=-1, keepdims=True), weights.astype(jnp.bfloat16)


def head_copies(source, target, sem):
    return [
        pltpu.make_async_copy(source.at[:, pl.ds(head * HD, HD)], target.at[head], sem.at[head])
        for head in range(KVH)
    ]


def fetch_kernel(sk_hbm, sv_hbm, sk_ref, sv_ref, sk_sem, sv_sem):
    copies = head_copies(sk_hbm, sk_ref, sk_sem) + head_copies(sv_hbm, sv_ref, sv_sem)
    for copy in copies:
        copy.start()
    for copy in copies:
        copy.wait()


def suffix_kernel(
    len_ref,
    own_ref,
    pair_ref,
    sk_ref,
    sv_ref,
    nk_ref,
    nv_ref,
    dk_hbm,
    dv_hbm,
    top_ref,
    total_ref,
    out_ref,
    dk_ref,
    dv_ref,
    dk_sem,
    dv_sem,
):
    copies = head_copies(dk_hbm, dk_ref, dk_sem) + head_copies(dv_hbm, dv_ref, dv_sem)
    for copy in copies:
        copy.start()
    me = lax.axis_index("seq")
    parity = lax.rem(me, 2)
    mine = lax.broadcasted_iota(jnp.int32, len_ref.shape, 1) == lax.div(me, 2)
    length = jnp.sum(
        jnp.where(mine, len_ref[...].astype(jnp.float32), 0.0), axis=1, keepdims=True
    )
    live_left = length.astype(jnp.int32) - parity * sk_ref.shape[1]

    def scores_of(head):
        rows = slice(head * GROUPS, (head + 1) * GROUPS)
        cols = slice(head * HD, (head + 1) * HD)
        q = jnp.concatenate(
            [ref[0, rows, :].astype(jnp.float32) for ref in (own_ref, pair_ref)], axis=0
        )
        scores = lane_dot(q.astype(jnp.bfloat16), sk_ref[head])
        position = lax.broadcasted_iota(jnp.int32, scores.shape, 1)
        scores = jnp.where(position < live_left, scores, NEG_BIG)
        n_top = jnp.sum(q * nk_ref[:, cols].astype(jnp.float32), axis=-1, keepdims=True)
        hidden = (lax.broadcasted_iota(jnp.int32, n_top.shape, 0) >= GROUPS) & (parity == 1)
        return scores, jnp.where(hidden, NEG_BIG, n_top)

    ready = [scores_of(head) for head in range(AHEAD)]
    for head in range(KVH):
        cols = slice(head * HD, (head + 1) * HD)
        scores, n_top = ready.pop(0)
        if head + AHEAD < KVH:
            ready.append(scores_of(head + AHEAD))
        top = jnp.maximum(jnp.max(scores, axis=-1, keepdims=True), n_top)
        base = jnp.maximum(top, NEG_SAFE)
        weights = jnp.exp2((scores - base) * EXP2_SCALE)
        n_scale = jnp.exp2((n_top - base) * EXP2_SCALE)
        total = jnp.sum(weights, axis=-1, keepdims=True) + n_scale
        out = jnp.dot(
            weights.astype(jnp.bfloat16), sv_ref[head], preferred_element_type=jnp.float32
        )
        top_ref[head] = jnp.broadcast_to(top, (2 * GROUPS, LANES))
        total_ref[head] = jnp.broadcast_to(total, (2 * GROUPS, LANES))
        out_ref[head] = out + n_scale * nv_ref[:, cols].astype(jnp.float32)
    for copy in copies:
        copy.wait()


def split_stats(stats, axis):
    high = stats.astype(jnp.bfloat16).astype(jnp.float32)
    rest = stats - high
    middle = rest.astype(jnp.bfloat16).astype(jnp.float32)
    low = rest - middle
    packed = high + pltpu.roll(middle, 2 * KVH, axis) + pltpu.roll(low, 4 * KVH, axis)
    return packed.astype(jnp.bfloat16)


def join_stats(packed, axis):
    packed = packed.astype(jnp.float32)
    shifted = lambda by: pltpu.roll(packed, LANES - by * KVH, axis)
    live = lax.broadcasted_iota(jnp.int32, packed.shape, axis) < KVH
    top = jnp.where(live, packed + shifted(2) + shifted(4), 0.0)
    total = jnp.where(live, shifted(1) + shifted(3) + shifted(5), 0.0)
    return top, total


def attend_kernel(
    flag_rows,
    near_ref,
    far_ref,
    dk_ref,
    dv_ref,
    top_ref,
    total_ref,
    extra_ref,
    near_out_ref,
    far_out_ref,
    bias_ref,
):
    half_tokens = near_ref.shape[0]
    span = dk_ref.shape[1]
    half = SLOTS * GROUPS
    first_block = lax.axis_index("seq") * (span // BLOCK)
    flag_row = lax.div(first_block, LANES)
    flag_lane = lax.rem(first_block, LANES)
    row_ids = lax.broadcasted_iota(jnp.int32, (1, flag_rows, LANES), 1)
    pick = (
        lax.broadcasted_iota(jnp.int32, (LANES, span), 0)
        == flag_lane + lax.broadcasted_iota(jnp.int32, (LANES, span), 1) // BLOCK
    ).astype(jnp.float32).astype(jnp.bfloat16)
    lane_ids = lax.broadcasted_iota(jnp.int32, (2 * half, LANES), 1)

    def do_chunk(chunk, local):
        start = chunk * SLOTS
        slots = pl.ds(start, SLOTS)
        flags = near_ref[slots, HEADS:, :].astype(jnp.float32) + far_ref[slots, HEADS:, :].astype(
            jnp.float32
        )
        flags = jnp.sum(jnp.where(row_ids == flag_row, flags, 0.0), axis=1)
        count = jnp.dot(flags.astype(jnp.bfloat16), pick, preferred_element_type=jnp.float32)
        bias = jnp.where(count > 0.5, 0.0, NEG_BIG)
        for s in range(SLOTS):
            bias_ref[s * GROUPS : (s + 1) * GROUPS, :] = jnp.broadcast_to(
                bias[s : s + 1, :], (GROUPS, span)
            )

        def scores_of(head):
            rows = slice(head * GROUPS, (head + 1) * GROUPS)
            q = jnp.concatenate(
                [
                    ref[slots, rows, :].astype(jnp.float32).reshape(half, HD)
                    for ref in (near_ref, far_ref)
                ],
                axis=0,
            ).astype(jnp.bfloat16)
            scores = lane_dot(q, dk_ref[head])
            bias = bias_ref[...]
            return scores + jnp.concatenate([bias, bias], axis=0)

        stats = jnp.zeros((2 * half, LANES), jnp.float32)
        upcoming = scores_of(0)
        for head in range(KVH):
            rows = slice(head * GROUPS, (head + 1) * GROUPS)
            scores = upcoming
            if head + 1 < KVH:
                upcoming = scores_of(head + 1)
            top, total, weights = partial_softmax(scores)
            out = jnp.dot(weights, dv_ref[head], preferred_element_type=jnp.float32)
            if local:

                def joined(at, x_top, x_total, x_out):
                    own = slice(at * GROUPS, (at + 1) * GROUPS)
                    y_top = top_ref[head, own, 0:1]
                    new_top = jnp.maximum(x_top, y_top)
                    base = jnp.maximum(new_top, NEG_SAFE)
                    x_scale = jnp.exp2((x_top - base) * EXP2_SCALE)
                    y_scale = jnp.exp2((y_top - base) * EXP2_SCALE)
                    return (
                        new_top,
                        x_scale * x_total + y_scale * total_ref[head, own, 0:1],
                        x_scale * x_out + y_scale * extra_ref[head, own, :],
                    )

                pieces = []
                for at in range(2):
                    lo = at * half
                    first = slice(lo, lo + GROUPS)
                    others = slice(lo + GROUPS, lo + half)
                    new = joined(at, top[first], total[first], out[first])
                    pieces.append(new)
                    pieces.append((top[others], total[others], out[others]))
                top, total, out = [jnp.concatenate(p, axis=0) for p in zip(*pieces)]
            units = (out / jnp.maximum(total, 1.0)).astype(jnp.bfloat16)
            stats = jnp.where(lane_ids == head, top * EXP2_SCALE, stats)
            stats = jnp.where(lane_ids == KVH + head, total, stats)
            near_out_ref[slots, rows, :] = units[:half].reshape(SLOTS, GROUPS, HD)
            far_out_ref[slots, rows, :] = units[half:].reshape(SLOTS, GROUPS, HD)
        packed = split_stats(stats, 1)
        rows = slice(HEADS, HEADS + GROUPS)
        near_out_ref[slots, rows, :] = packed[:half].reshape(SLOTS, GROUPS, LANES)
        far_out_ref[slots, rows, :] = packed[half:].reshape(SLOTS, GROUPS, LANES)

    do_chunk(0, True)
    chunks = half_tokens // SLOTS
    if chunks > 1:
        lax.fori_loop(1, chunks, lambda c, _: do_chunk(c, False), None)


def mix_weights(refs):
    rows = slice(HEADS, HEADS + GROUPS)
    stats = [join_stats(ref[:, rows, :], 2) for ref in refs]
    top = functools.reduce(jnp.maximum, [t for t, _ in stats])
    weights = [jnp.exp2(t - top) * total for t, total in stats]
    total = functools.reduce(jnp.add, weights)
    scale = 1.0 / jnp.maximum(total, 1.0)
    return top, total, [w * scale for w in weights]


def mixed_units(head, refs, weights):
    rows = slice(head * GROUPS, (head + 1) * GROUPS)
    return functools.reduce(
        jnp.add,
        [
            ref[:, rows, :].astype(jnp.float32) * w[:, :, head : head + 1]
            for ref, w in zip(refs, weights)
        ],
    )


def merge_kernel(count, *refs):
    sources, targets = refs[:count], refs[count:]
    top, total, weights = mix_weights(sources)
    size = targets[0].shape[0]
    for head in range(KVH):
        rows = slice(head * GROUPS, (head + 1) * GROUPS)
        units = mixed_units(head, sources, weights).astype(jnp.bfloat16)
        for i, target in enumerate(targets):
            target[:, rows, :] = units[i * size : (i + 1) * size]
    packed = split_stats(top + pltpu.roll(total, KVH, 2), 2)
    for i, target in enumerate(targets):
        target[:, HEADS : HEADS + GROUPS, :] = packed[i * size : (i + 1) * size]


def finish_kernel(count, *refs):
    sources, out_ref = refs[:count], refs[count]
    _, _, weights = mix_weights(sources)
    for head in range(KVH):
        units = mixed_units(head, sources, weights)[0]
        for g in range(GROUPS):
            h = head * GROUPS + g
            out_ref[:, h * HD : (h + 1) * HD] = units[g : g + 1, :].astype(jnp.bfloat16)


def whole(space=VMEM):
    return pl.BlockSpec(memory_space=space)


def near_core(x):
    return pltpu.with_memory_space_constraint(x, VMEM)


def on_core(kernel, out_shape, operands, cost=None, **kwargs):
    return pl.pallas_call(
        kernel,
        out_shape=out_shape,
        in_specs=kwargs.pop("in_specs", [whole()] * len(operands)),
        out_specs=jax.tree.map(lambda _: whole(), out_shape),
        compiler_params=pltpu.CompilerParams(vmem_limit_bytes=16 << 20),
        cost_estimate=cost,
        **kwargs,
    )(*operands)


def in_hbm(x):
    return pltpu.with_memory_space_constraint(x, pltpu.HBM)


def swap(x, bits):
    devices = lax.axis_size("seq")
    return lax.ppermute(x, "seq", [(i, i ^ bits) for i in range(devices)])


def stages_of(devices):
    far_bits = []
    while 2 ** (len(far_bits) + 3) < devices:
        far_bits.insert(0, (2 ** (len(far_bits) + 3) | 1,))
    return far_bits + [(3, 5, 7)[: devices // 2 - 1]]


def per_device(
    queries,
    new_keys,
    new_values,
    doc_keys,
    doc_values,
    suffix_keys,
    suffix_values,
    keep_lists,
    suffix_lengths,
):
    devices = lax.axis_size("seq")
    blocks = devices * doc_keys.shape[0] // BLOCK
    flag_rows = 8 * pl.cdiv(blocks, 8 * LANES)
    stages = stages_of(devices)
    packed = on_core(
        pack_kernel,
        VMEM((HEADS + flag_rows, HD), jnp.bfloat16),
        (in_hbm(keep_lists), in_hbm(queries)),
    )
    near = packed[None]
    own = near
    by_head = lambda x: VMEM((KVH, x.shape[0], HD), x.dtype)
    sems = pltpu.SemaphoreType.DMA((KVH,))
    hbm = whole(pltpu.HBM)
    size = 2 * (suffix_keys.size + suffix_values.size)
    sk, sv = on_core(
        fetch_kernel,
        [by_head(suffix_keys), by_head(suffix_values)],
        (in_hbm(suffix_keys), in_hbm(suffix_values)),
        in_specs=[hbm] * 2,
        scratch_shapes=[sems, sems],
        cost=pl.CostEstimate(flops=0, bytes_accessed=size, transcendentals=0),
    )
    pair = swap(own, 1)
    stat = VMEM((KVH, 2 * GROUPS, LANES), jnp.float32)
    *local, dk, dv = on_core(
        suffix_kernel,
        [stat, stat, VMEM((KVH, 2 * GROUPS, HD), jnp.float32)] + [by_head(doc_keys), by_head(doc_values)],
        (
            near_core(suffix_lengths[None]),
            own,
            near_core(pair),
            sk,
            sv,
            new_keys,
            new_values,
            in_hbm(doc_keys),
            in_hbm(doc_values),
        ),
        in_specs=[whole()] * 7 + [hbm] * 2,
        scratch_shapes=[sems, sems],
        cost=pl.CostEstimate(flops=10**9, bytes_accessed=size, transcendentals=10**6),
    )
    for step, stage in enumerate(stages):
        arrived = []
        for bits in stage:
            arrived.append(swap(near, bits))
        near = jnp.concatenate([near] + arrived, axis=0)
    far = swap(near, 1)
    tokens = lambda count: VMEM((count, HEADS + GROUPS, HD), jnp.bfloat16)
    parts = on_core(
        functools.partial(attend_kernel, flag_rows),
        [tokens(devices // 2)] * 2,
        (near_core(near), near_core(far), dk, dv, *local),
        scratch_shapes=[VMEM((SLOTS * GROUPS, doc_keys.shape[0]), jnp.float32)],
    )
    step = len(stages)
    stages.append((1,))
    while stages:
        stage = stages.pop()
        sources = [parts[0]]
        for bits, part in zip(stage, parts[1:]):
            sources.append(near_core(swap(part, bits)))
        step -= 1
        if stages:
            pieces = len(stages[-1]) + 1
            parts = on_core(
                functools.partial(merge_kernel, len(sources)),
                [tokens(sources[0].shape[0] // pieces)] * pieces,
                sources,
            )
    return on_core(
        functools.partial(finish_kernel, len(sources)),
        jax.ShapeDtypeStruct((1, HEADS * HD), jnp.bfloat16),
        sources,
    )


def solution(mesh):
    split = P(("parts", "seq"), None)
    return jax.shard_map(
        per_device,
        mesh=mesh,
        in_specs=(split,) * 8 + (P("parts"),),
        out_specs=split,
        check_vma=False,
    )
```

time: 41.6 us -> 36.5 us (0.88)
  starting transfers between devices: 15.3 us -> 13.7 us
  Pallas kernels: 12.5 us -> 11 us
  local copies, waits for them, and re-layouts: 1.42 us -> 0.06 us
  waiting for transfers between devices: 12 us -> 11.4 us
    ppermute x9 -> x11, starting transfers between devices: 15.3 us -> 13.7 us  [swap(): return lax.ppermute(x, 'seq', [(i, i ^ bits) for i in range(devices)])]
    pallas_call x8 -> x7, Pallas kernels: 12.5 us -> 11 us  [on_core(): pl.pallas_call(kernel, out_shape=out_shape, in_specs=kwargs.pop('in_specs...]
    unnamed x10, local copies, waits for them, and re-layouts: 1.42 us -> 0.05 us
    ppermute x9 -> x11, waiting for transfers between devices: 12 us -> 11.4 us  [swap(): return lax.ppermute(x, 'seq', [(i, i ^ bits) for i in range(devices)])]
  transfers between devices with their start and end apart: 9 -> 11, of which waited for: 7 -> 7; matrix products, arithmetic and copies ran while one was open for 0% -> 0% of each run, Pallas kernels for 16% -> 15%
where the time goes in v3:
time: 36.5 us; the launch traced here: 36.3 us
  starting transfers between devices  13.7 us (38%)
  waiting for transfers between devices  11.4 us (31%)
  Pallas kernels  11 us (30%)
    ppermute x11, starting transfers between devices, swap(): return lax.ppermute(x, 'seq', [(i, i ^ bits) for i in range(devices)])  13.7 us
    ppermute x11, waiting for transfers between devices, swap(): return lax.ppermute(x, 'seq', [(i, i ^ bits) for i in range(devices)])  11.4 us
    pallas_call x7, Pallas kernels, on_core(): pl.pallas_call(kernel, out_shape=out_shape, in_specs=kwargs.pop('in_specs...  11 us
  transfers between devices with their start and end apart: 11, of which 7 were waited for; matrix products, arithmetic and copies ran while one was open for 0% of the time, Pallas kernels for 15%

profile of v3, /device:TPU:0, one launch (start us, length us, event | category | flops | bytes accessed | tf_op | source)
XLA Modules:
  0.0 36.3 jit_solution(4873883730538640111)
XLA Ops:
  0.0 0.9 %shard_map.91 = bf16[72,128]{1,0:T(8,128)(2,1)S(1)} custom-call(s32[1,32]{1,0:T(1,128)} %list_ref.1, bf16[1,8192]{1,0:T(2,128)(2,1)} %q_ref.1), custom_call_target="tpu_custom_call" | custom-call | tf_op jit(solution)/shard_map/pallas_call | solution.py:308
  0.9 3.6 %collective-permute-start = (bf16[1,72,128]{2,1,0:T(8,128)(2,1)S(1)}, bf16[1,72,128]{2,1,0:T(8,128)(2,1)S(1)}, u32[]{:S(2)}, u32[]{:S(2)}) collective-permute-start(bf16[1,72,128]{2,1,0:T(8,128)(2,1)S(1)} %bitcast.3), channel_id=1, source_target_pairs={{0,9},{1,8},{2,11},{3,10},{4,13},{5,12},{6,15},{7,14},{8,1},{9,0},... | collective-permute-start | bytes 55304 | tf_op jit(solution)/shard_map/ppermute | solution.py:325
  4.5 1.5 %collective-permute-done = bf16[1,72,128]{2,1,0:T(8,128)(2,1)S(1)} collective-permute-done((bf16[1,72,128]{2,1,0:T(8,128)(2,1)S(1)}, bf16[1,72,128]{2,1,0:T(8,128)(2,1)S(1)}, u32[]{:S(2)}, u32[]{:S(2)}) %collective-permute-start) | collective-permute-done | bytes 18464 | tf_op jit(solution)/shard_map/ppermute | solution.py:325
  5.9 2.8 %collective-permute-start.3 = (bf16[2,72,128]{2,1,0:T(8,128)(2,1)S(1)}, bf16[2,72,128]{2,1,0:T(8,128)(2,1)S(1)}, u32[]{:S(2)}, u32[]{:S(2)}) collective-permute-start(bf16[2,72,128]{2,1,0:T(8,128)(2,1)S(1)} %pad_maximum_fusion), channel_id=1, source_target_pairs={{0,7},{1,6},{2,5},{3,4},{4,3},{5,2},{6,1},{7,0},{8,15},{9,14},{10,... | collective-permute-start | bytes 110600 | tf_op jit(solution)/shard_map/ppermute | solution.py:325
  8.8 0.4 %collective-permute-start.2 = (bf16[2,72,128]{2,1,0:T(8,128)(2,1)S(1)}, bf16[2,72,128]{2,1,0:T(8,128)(2,1)S(1)}, u32[]{:S(2)}, u32[]{:S(2)}) collective-permute-start(bf16[2,72,128]{2,1,0:T(8,128)(2,1)S(1)} %pad_maximum_fusion), channel_id=1, source_target_pairs={{0,5},{1,4},{2,7},{3,6},{4,1},{5,0},{6,3},{7,2},{8,13},{9,12},{10,... | collective-permute-start | bytes 110600 | tf_op jit(solution)/shard_map/ppermute | solution.py:325
  9.2 0.2 collective-permute-start.1
  9.4 3.3 %collective-permute-done.1 = bf16[2,72,128]{2,1,0:T(8,128)(2,1)S(1)} collective-permute-done((bf16[2,72,128]{2,1,0:T(8,128)(2,1)S(1)}, bf16[2,72,128]{2,1,0:T(8,128)(2,1)S(1)}, u32[]{:S(2)}, u32[]{:S(2)}) %collective-permute-start.1) | collective-permute-done | bytes 36896 | tf_op jit(solution)/shard_map/ppermute | solution.py:325
  12.8 0.2 collective-permute-start.4
  13.0 0.4 %collective-permute-start.5 = (bf16[1,72,128]{2,1,0:T(8,128)(2,1)S(1)}, bf16[1,72,128]{2,1,0:T(8,128)(2,1)S(1)}, u32[]{:S(2)}, u32[]{:S(2)}) collective-permute-start(bf16[1,72,128]{2,1,0:T(8,128)(2,1)S(1)} %bitcast.5), channel_id=1, source_target_pairs={{0,1},{1,0},{2,3},{3,2},{4,5},{5,4},{6,7},{7,6},{8,9},{9,8},{10,11... | collective-permute-start | bytes 55304 | tf_op jit(solution)/shard_map/ppermute | solution.py:325
  13.4 2.4 %shard_map.92 = (bf16[8,1024,128]{2,1,0:T(8,128)(2,1)S(1)}, bf16[8,1024,128]{2,1,0:T(8,128)(2,1)S(1)}) custom-call(bf16[1024,1024]{1,0:T(8,128)(2,1)} %sk_hbm.1, bf16[1024,1024]{1,0:T(8,128)(2,1)} %sv_hbm.1), custom_call_target="tpu_custom_call" | custom-call | bytes 4194304 | tf_op jit(solution)/shard_map/pallas_call | solution.py:308
  15.8 3.0 %shard_map.93 = (f32[8,16,128]{2,1,0:T(8,128)S(1)}, f32[8,16,128]{2,1,0:T(8,128)S(1)}, f32[8,16,128]{2,1,0:T(8,128)S(1)}, bf16[8,1024,128]{2,1,0:T(8,128)(2,1)S(1)}, bf16[8,1024,128]{2,1,0:T(8,128)(2,1)S(1)}) custom-call(s32[1,8]{1,0:T(1,128)S(1)} %bitcast.7, bf16[1,72,128]{2,1,0:T(8,128)(2,1)S(1)} %bitcast.6, ...), custom_call_target="tpu_custom_call" | custom-call | flops 1000000000 | bytes 4194304 | tf_op jit(solution)/shard_map/pallas_call | solution.py:308
  18.8 3.3 %shard_map.94 = (bf16[8,72,128]{2,1,0:T(8,128)(2,1)S(1)}, bf16[8,72,128]{2,1,0:T(8,128)(2,1)S(1)}) custom-call(bf16[8,72,128]{2,1,0:T(8,128)(2,1)S(1)} %constant_dynamic-update-slice_fusion.near_ref, bf16[8,72,128]{2,1,0:T(8,128)(2,1)S(1)} %collective-permute-done.4.far_ref, bf16[8,1024,128]{2,1,0:T(8,128)(2,1)S(1)} %get-tuple-element.22.dk_ref, ...), custom_call_target="tpu_custom_call" | custom-call | tf_op jit(solution)/shard_map/pallas_call | solution.py:308
  22.3 1.3 %collective-permute-done.6.refs_1_ = bf16[8,72,128]{2,1,0:T(8,128)(2,1)S(1)} collective-permute-done((bf16[8,72,128]{2,1,0:T(8,128)(2,1)S(1)}, bf16[8,72,128]{2,1,0:T(8,128)(2,1)S(1)}, u32[]{:S(2)}, u32[]{:S(2)}) %collective-permute-start.6) | collective-permute-done | bytes 147488 | tf_op jit(solution)/shard_map/ppermute | solution.py:325
  23.5 0.4 %shard_map.95 = (bf16[2,72,128]{2,1,0:T(8,128)(2,1)S(1)}, bf16[2,72,128]{2,1,0:T(8,128)(2,1)S(1)}, bf16[2,72,128]{2,1,0:T(8,128)(2,1)S(1)}, bf16[2,72,128]{2,1,0:T(8,128)(2,1)S(1)}) custom-call(bf16[8,72,128]{2,1,0:T(8,128)(2,1)S(1)} %get-tuple-element.27.refs_0_, bf16[8,72,128]{2,1,0:T(8,128)(2,1)S(1)} %collective-permute-done.6.refs_1_), custom_call_target="tpu_custom_call" | custom-call | tf_op jit(solution)/shard_map/pallas_call | solution.py:308
  23.9 0.3 collective-permute-start.7
  24.3 1.8 %collective-permute-start.8 = (bf16[2,72,128]{2,1,0:T(8,128)(2,1)S(1)}, bf16[2,72,128]{2,1,0:T(8,128)(2,1)S(1)}, u32[]{:S(2)}, u32[]{:S(2)}) collective-permute-start(bf16[2,72,128]{2,1,0:T(8,128)(2,1)S(1)} %get-tuple-element.31), channel_id=1, source_target_pairs={{0,5},{1,4},{2,7},{3,6},{4,1},{5,0},{6,3},{7,2},{8,13},{9,12},{10,... | collective-permute-start | bytes 110600 | tf_op jit(solution)/shard_map/ppermute | solution.py:325
  26.1 0.9 %collective-permute-start.9 = (bf16[2,72,128]{2,1,0:T(8,128)(2,1)S(1)}, bf16[2,72,128]{2,1,0:T(8,128)(2,1)S(1)}, u32[]{:S(2)}, u32[]{:S(2)}) collective-permute-start(bf16[2,72,128]{2,1,0:T(8,128)(2,1)S(1)} %get-tuple-element.32), channel_id=1, source_target_pairs={{0,7},{1,6},{2,5},{3,4},{4,3},{5,2},{6,1},{7,0},{8,15},{9,14},{10,... | collective-permute-start | bytes 110600 | tf_op jit(solution)/shard_map/ppermute | solution.py:325
  27.0 0.5 %collective-permute-done.7.refs_1_ = bf16[2,72,128]{2,1,0:T(8,128)(2,1)S(1)} collective-permute-done((bf16[2,72,128]{2,1,0:T(8,128)(2,1)S(1)}, bf16[2,72,128]{2,1,0:T(8,128)(2,1)S(1)}, u32[]{:S(2)}, u32[]{:S(2)}) %collective-permute-start.7) | collective-permute-done | bytes 36896 | tf_op jit(solution)/shard_map/ppermute | solution.py:325
  27.5 0.3 collective-permute-done.8.refs_2_
  27.7 2.7 %collective-permute-done.9.refs_3_ = bf16[2,72,128]{2,1,0:T(8,128)(2,1)S(1)} collective-permute-done((bf16[2,72,128]{2,1,0:T(8,128)(2,1)S(1)}, bf16[2,72,128]{2,1,0:T(8,128)(2,1)S(1)}, u32[]{:S(2)}, u32[]{:S(2)}) %collective-permute-start.9) | collective-permute-done | bytes 36896 | tf_op jit(solution)/shard_map/ppermute | solution.py:325
  30.5 0.3 shard_map.96
  30.7 2.9 %collective-permute-start.10 = (bf16[1,72,128]{2,1,0:T(8,128)(2,1)S(1)}, bf16[1,72,128]{2,1,0:T(8,128)(2,1)S(1)}, u32[]{:S(2)}, u32[]{:S(2)}) collective-permute-start(bf16[1,72,128]{2,1,0:T(8,128)(2,1)S(1)} %get-tuple-element.34), channel_id=1, source_target_pairs={{0,9},{1,8},{2,11},{3,10},{4,13},{5,12},{6,15},{7,14},{8,1},{9,0},... | collective-permute-start | bytes 55304 | tf_op jit(solution)/shard_map/ppermute | solution.py:325
  33.6 1.9 %collective-permute-done.10.refs_1_ = bf16[1,72,128]{2,1,0:T(8,128)(2,1)S(1)} collective-permute-done((bf16[1,72,128]{2,1,0:T(8,128)(2,1)S(1)}, bf16[1,72,128]{2,1,0:T(8,128)(2,1)S(1)}, u32[]{:S(2)}, u32[]{:S(2)}) %collective-permute-start.10) | collective-permute-done | bytes 18464 | tf_op jit(solution)/shard_map/ppermute | solution.py:325
  35.5 0.8 %shard_map.97 = bf16[1,8192]{1,0:T(2,128)(2,1)} custom-call(bf16[1,72,128]{2,1,0:T(8,128)(2,1)S(1)} %get-tuple-element.33.refs_0_, bf16[1,72,128]{2,1,0:T(8,128)(2,1)S(1)} %collective-permute-done.10.refs_1_), custom_call_target="tpu_custom_call" | custom-call | tf_op jit(solution)/shard_map/pallas_call | solution.py:308
  (17 shorter events, 0.3 us)
Async XLA Ops:
  0.9 5.0 %collective-permute-start = (bf16[1,72,128]{2,1,0:T(8,128)(2,1)S(1)}, bf16[1,72,128]{2,1,0:T(8,128)(2,1)S(1)}, u32[]{:S(2)}, u32[]{:S(2)}) collective-permute-start(bf16[1,72,128]{2,1,0:T(8,128)(2,1)S(1)} %bitcast.3), channel_id=1, source_target_pairs={{0,9},{1,8},{2,11},{3,10},{4,13},{5,12},{6,15},{7,14},{8,1},{9,0},... | collective-permute-start | bytes 55304 | tf_op jit(solution)/shard_map/ppermute | solution.py:325
  5.9 6.8 %collective-permute-start.3 = (bf16[2,72,128]{2,1,0:T(8,128)(2,1)S(1)}, bf16[2,72,128]{2,1,0:T(8,128)(2,1)S(1)}, u32[]{:S(2)}, u32[]{:S(2)}) collective-permute-start(bf16[2,72,128]{2,1,0:T(8,128)(2,1)S(1)} %pad_maximum_fusion), channel_id=1, source_target_pairs={{0,7},{1,6},{2,5},{3,4},{4,3},{5,2},{6,1},{7,0},{8,15},{9,14},{10,... | collective-permute-start | bytes 110600 | tf_op jit(solution)/shard_map/ppermute | solution.py:325
  8.8 3.9 %collective-permute-start.2 = (bf16[2,72,128]{2,1,0:T(8,128)(2,1)S(1)}, bf16[2,72,128]{2,1,0:T(8,128)(2,1)S(1)}, u32[]{:S(2)}, u32[]{:S(2)}) collective-permute-start(bf16[2,72,128]{2,1,0:T(8,128)(2,1)S(1)} %pad_maximum_fusion), channel_id=1, source_target_pairs={{0,5},{1,4},{2,7},{3,6},{4,1},{5,0},{6,3},{7,2},{8,13},{9,12},{10,... | collective-permute-start | bytes 110600 | tf_op jit(solution)/shard_map/ppermute | solution.py:325
  9.2 3.5 %collective-permute-start.1 = (bf16[2,72,128]{2,1,0:T(8,128)(2,1)S(1)}, bf16[2,72,128]{2,1,0:T(8,128)(2,1)S(1)}, u32[]{:S(2)}, u32[]{:S(2)}) collective-permute-start(bf16[2,72,128]{2,1,0:T(8,128)(2,1)S(1)} %pad_maximum_fusion), channel_id=1, source_target_pairs={{0,3},{1,2},{2,1},{3,0},{4,7},{5,6},{6,5},{7,4},{8,11},{9,10},{10,... | collective-permute-start | bytes 110600 | tf_op jit(solution)/shard_map/ppermute | solution.py:325
  12.7 3.0 %copy-start = (bf16[1,1024]{1,0:T(2,128)(2,1)S(1)}, bf16[1,1024]{1,0:T(2,128)(2,1)}, u32[]{:S(2)}) copy-start(bf16[1,1024]{1,0:T(2,128)(2,1)} %nk_ref.1) | copy-start | bytes 6148
  12.8 3.0 %copy-start.1 = (bf16[1,1024]{1,0:T(2,128)(2,1)S(1)}, bf16[1,1024]{1,0:T(2,128)(2,1)}, u32[]{:S(2)}) copy-start(bf16[1,1024]{1,0:T(2,128)(2,1)} %nv_ref.1) | copy-start | bytes 6148
  12.8 3.0 %copy-start.2 = (s32[8]{0:T(128)S(1)}, s32[8]{0:T(128)}, u32[]{:S(2)}) copy-start(s32[8]{0:T(128)} %param.17) | copy-start | bytes 100
  12.8 6.1 %collective-permute-start.4 = (bf16[8,72,128]{2,1,0:T(8,128)(2,1)S(1)}, bf16[8,72,128]{2,1,0:T(8,128)(2,1)S(1)}, u32[]{:S(2)}, u32[]{:S(2)}) collective-permute-start(bf16[8,72,128]{2,1,0:T(8,128)(2,1)S(1)} %constant_dynamic-update-slice_fusion.near_ref), channel_id=1, source_target_pairs={{0,1},{1,0},{2,3},{3,2},{4,5},{5,4},{6,7},{7,6},{8,9},{9,8},{10,11... | collective-permute-start | bytes 442376 | tf_op jit(solution)/shard_map/ppermute | solution.py:325
  13.0 2.8 %collective-permute-start.5 = (bf16[1,72,128]{2,1,0:T(8,128)(2,1)S(1)}, bf16[1,72,128]{2,1,0:T(8,128)(2,1)S(1)}, u32[]{:S(2)}, u32[]{:S(2)}) collective-permute-start(bf16[1,72,128]{2,1,0:T(8,128)(2,1)S(1)} %bitcast.5), channel_id=1, source_target_pairs={{0,1},{1,0},{2,3},{3,2},{4,5},{5,4},{6,7},{7,6},{8,9},{9,8},{10,11... | collective-permute-start | bytes 55304 | tf_op jit(solution)/shard_map/ppermute | solution.py:325
  22.1 1.4 %collective-permute-start.6 = (bf16[8,72,128]{2,1,0:T(8,128)(2,1)S(1)}, bf16[8,72,128]{2,1,0:T(8,128)(2,1)S(1)}, u32[]{:S(2)}, u32[]{:S(2)}) collective-permute-start(bf16[8,72,128]{2,1,0:T(8,128)(2,1)S(1)} %get-tuple-element.28), channel_id=1, source_target_pairs={{0,1},{1,0},{2,3},{3,2},{4,5},{5,4},{6,7},{7,6},{8,9},{9,8},{10,11... | collective-permute-start | bytes 442376 | tf_op jit(solution)/shard_map/ppermute | solution.py:325
  23.9 3.5 %collective-permute-start.7 = (bf16[2,72,128]{2,1,0:T(8,128)(2,1)S(1)}, bf16[2,72,128]{2,1,0:T(8,128)(2,1)S(1)}, u32[]{:S(2)}, u32[]{:S(2)}) collective-permute-start(bf16[2,72,128]{2,1,0:T(8,128)(2,1)S(1)} %get-tuple-element.30), channel_id=1, source_target_pairs={{0,3},{1,2},{2,1},{3,0},{4,7},{5,6},{6,5},{7,4},{8,11},{9,10},{10,... | collective-permute-start | bytes 110600 | tf_op jit(solution)/shard_map/ppermute | solution.py:325
  24.3 3.5 %collective-permute-start.8 = (bf16[2,72,128]{2,1,0:T(8,128)(2,1)S(1)}, bf16[2,72,128]{2,1,0:T(8,128)(2,1)S(1)}, u32[]{:S(2)}, u32[]{:S(2)}) collective-permute-start(bf16[2,72,128]{2,1,0:T(8,128)(2,1)S(1)} %get-tuple-element.31), channel_id=1, source_target_pairs={{0,5},{1,4},{2,7},{3,6},{4,1},{5,0},{6,3},{7,2},{8,13},{9,12},{10,... | collective-permute-start | bytes 110600 | tf_op jit(solution)/shard_map/ppermute | solution.py:325
  26.1 4.3 %collective-permute-start.9 = (bf16[2,72,128]{2,1,0:T(8,128)(2,1)S(1)}, bf16[2,72,128]{2,1,0:T(8,128)(2,1)S(1)}, u32[]{:S(2)}, u32[]{:S(2)}) collective-permute-start(bf16[2,72,128]{2,1,0:T(8,128)(2,1)S(1)} %get-tuple-element.32), channel_id=1, source_target_pairs={{0,7},{1,6},{2,5},{3,4},{4,3},{5,2},{6,1},{7,0},{8,15},{9,14},{10,... | collective-permute-start | bytes 110600 | tf_op jit(solution)/shard_map/ppermute | solution.py:325
  30.7 4.8 %collective-permute-start.10 = (bf16[1,72,128]{2,1,0:T(8,128)(2,1)S(1)}, bf16[1,72,128]{2,1,0:T(8,128)(2,1)S(1)}, u32[]{:S(2)}, u32[]{:S(2)}) collective-permute-start(bf16[1,72,128]{2,1,0:T(8,128)(2,1)S(1)} %get-tuple-element.34), channel_id=1, source_target_pairs={{0,9},{1,8},{2,11},{3,10},{4,13},{5,12},{6,15},{7,14},{8,1},{9,0},... | collective-permute-start | bytes 55304 | tf_op jit(solution)/shard_map/ppermute | solution.py:325

commit v4 on v3

--- a/solution.py
+++ b/solution.py
@@ -20,6 +20,7 @@
 NEG_BIG = -1e30
 NEG_SAFE = -5e29
 AHEAD = 2
+DOC_AHEAD = 2
 EXP2_SCALE = HD**-0.5 * math.log2(math.e)
 
 VMEM = pltpu.VMEM
@@ -60,8 +61,8 @@
     ]
 
 
-def fetch_kernel(sk_hbm, sv_hbm, sk_ref, sv_ref, sk_sem, sv_sem):
-    copies = head_copies(sk_hbm, sk_ref, sk_sem) + head_copies(sv_hbm, sv_ref, sv_sem)
+def fetch_kernel(source, target, sem):
+    copies = head_copies(source, target, sem)
     for copy in copies:
         copy.start()
     for copy in copies:
@@ -73,9 +74,9 @@
     own_ref,
     pair_ref,
     sk_ref,
-    sv_ref,
     nk_ref,
     nv_ref,
+    sv_hbm,
     dk_hbm,
     dv_hbm,
     top_ref,
@@ -83,11 +84,14 @@
     out_ref,
     dk_ref,
     dv_ref,
+    sv_ref,
+    sv_sem,
     dk_sem,
     dv_sem,
 ):
+    arriving = head_copies(sv_hbm, sv_ref, sv_sem)
     copies = head_copies(dk_hbm, dk_ref, dk_sem) + head_copies(dv_hbm, dv_ref, dv_sem)
-    for copy in copies:
+    for copy in arriving + copies:
         copy.start()
     me = lax.axis_index("seq")
     parity = lax.rem(me, 2)
@@ -121,6 +125,7 @@
         weights = jnp.exp2((scores - base) * EXP2_SCALE)
         n_scale = jnp.exp2((n_top - base) * EXP2_SCALE)
         total = jnp.sum(weights, axis=-1, keepdims=True) + n_scale
+        arriving[head].wait()
         out = jnp.dot(
             weights.astype(jnp.bfloat16), sv_ref[head], preferred_element_type=jnp.float32
         )
@@ -151,20 +156,20 @@
 
 def attend_kernel(
     flag_rows,
-    near_ref,
-    far_ref,
+    which,
+    token_ref,
+    other_ref,
     dk_ref,
     dv_ref,
     top_ref,
     total_ref,
     extra_ref,
-    near_out_ref,
-    far_out_ref,
+    out_ref,
     bias_ref,
 ):
-    half_tokens = near_ref.shape[0]
+    tokens = token_ref.shape[0]
     span = dk_ref.shape[1]
-    half = SLOTS * GROUPS
+    rows_here = SLOTS * GROUPS
     first_block = lax.axis_index("seq") * (span // BLOCK)
     flag_row = lax.div(first_block, LANES)
     flag_lane = lax.rem(first_block, LANES)
@@ -173,14 +178,14 @@
         lax.broadcasted_iota(jnp.int32, (LANES, span), 0)
         == flag_lane + lax.broadcasted_iota(jnp.int32, (LANES, span), 1) // BLOCK
     ).astype(jnp.float32).astype(jnp.bfloat16)
-    lane_ids = lax.broadcasted_iota(jnp.int32, (2 * half, LANES), 1)
+    lane_ids = lax.broadcasted_iota(jnp.int32, (rows_here, LANES), 1)
+    own = slice(which * GROUPS, (which + 1) * GROUPS)
 
     def do_chunk(chunk, local):
-        start = chunk * SLOTS
-        slots = pl.ds(start, SLOTS)
-        flags = near_ref[slots, HEADS:, :].astype(jnp.float32) + far_ref[slots, HEADS:, :].astype(
-            jnp.float32
-        )
+        slots = pl.ds(chunk * SLOTS, SLOTS)
+        flags = token_ref[slots, HEADS:, :].astype(jnp.float32) + other_ref[
+            slots, HEADS:, :
+        ].astype(jnp.float32)
         flags = jnp.sum(jnp.where(row_ids == flag_row, flags, 0.0), axis=1)
         count = jnp.dot(flags.astype(jnp.bfloat16), pick, preferred_element_type=jnp.float32)
         bias = jnp.where(count > 0.5, 0.0, NEG_BIG)
@@ -191,62 +196,38 @@
 
         def scores_of(head):
             rows = slice(head * GROUPS, (head + 1) * GROUPS)
-            q = jnp.concatenate(
-                [
-                    ref[slots, rows, :].astype(jnp.float32).reshape(half, HD)
-                    for ref in (near_ref, far_ref)
-                ],
-                axis=0,
-            ).astype(jnp.bfloat16)
-            scores = lane_dot(q, dk_ref[head])
-            bias = bias_ref[...]
-            return scores + jnp.concatenate([bias, bias], axis=0)
-
-        stats = jnp.zeros((2 * half, LANES), jnp.float32)
-        upcoming = scores_of(0)
+            q = token_ref[slots, rows, :].astype(jnp.float32).reshape(rows_here, HD)
+            return lane_dot(q.astype(jnp.bfloat16), dk_ref[head]) + bias_ref[...]
+
+        stats = jnp.zeros((rows_here, LANES), jnp.float32)
+        ready = [scores_of(head) for head in range(DOC_AHEAD)]
         for head in range(KVH):
             rows = slice(head * GROUPS, (head + 1) * GROUPS)
-            scores = upcoming
-            if head + 1 < KVH:
-                upcoming = scores_of(head + 1)
+            scores = ready.pop(0)
+            if head + DOC_AHEAD < KVH:
+                ready.append(scores_of(head + DOC_AHEAD))
             top, total, weights = partial_softmax(scores)
             out = jnp.dot(weights, dv_ref[head], preferred_element_type=jnp.float32)
             if local:
-
-                def joined(at, x_top, x_total, x_out):
-                    own = slice(at * GROUPS, (at + 1) * GROUPS)
-                    y_top = top_ref[head, own, 0:1]
-                    new_top = jnp.maximum(x_top, y_top)
-                    base = jnp.maximum(new_top, NEG_SAFE)
-                    x_scale = jnp.exp2((x_top - base) * EXP2_SCALE)
-                    y_scale = jnp.exp2((y_top - base) * EXP2_SCALE)
-                    return (
-                        new_top,
-                        x_scale * x_total + y_scale * total_ref[head, own, 0:1],
-                        x_scale * x_out + y_scale * extra_ref[head, own, :],
-                    )
-
-                pieces = []
-                for at in range(2):
-                    lo = at * half
-                    first = slice(lo, lo + GROUPS)
-                    others = slice(lo + GROUPS, lo + half)
-                    new = joined(at, top[first], total[first], out[first])
-                    pieces.append(new)
-                    pieces.append((top[others], total[others], out[others]))
-                top, total, out = [jnp.concatenate(p, axis=0) for p in zip(*pieces)]
+                x_top, y_top = top[:GROUPS], top_ref[head, own, 0:1]
+                new_top = jnp.maximum(x_top, y_top)
+                base = jnp.maximum(new_top, NEG_SAFE)
+                x_scale = jnp.exp2((x_top - base) * EXP2_SCALE)
+                y_scale = jnp.exp2((y_top - base) * EXP2_SCALE)
+                new_total = x_scale * total[:GROUPS] + y_scale * total_ref[head, own, 0:1]
+                new_out = x_scale * out[:GROUPS] + y_scale * extra_ref[head, own, :]
+                top = jnp.concatenate([new_top, top[GROUPS:]], axis=0)
+                total = jnp.concatenate([new_total, total[GROUPS:]], axis=0)
+                out = jnp.concatenate([new_out, out[GROUPS:]], axis=0)
             units = (out / jnp.maximum(total, 1.0)).astype(jnp.bfloat16)
             stats = jnp.where(lane_ids == head, top * EXP2_SCALE, stats)
             stats = jnp.where(lane_ids == KVH + head, total, stats)
-            near_out_ref[slots, rows, :] = units[:half].reshape(SLOTS, GROUPS, HD)
-            far_out_ref[slots, rows, :] = units[half:].reshape(SLOTS, GROUPS, HD)
-        packed = split_stats(stats, 1)
+            out_ref[slots, rows, :] = units.reshape(SLOTS, GROUPS, HD)
         rows = slice(HEADS, HEADS + GROUPS)
-        near_out_ref[slots, rows, :] = packed[:half].reshape(SLOTS, GROUPS, LANES)
-        far_out_ref[slots, rows, :] = packed[half:].reshape(SLOTS, GROUPS, LANES)
+        out_ref[slots, rows, :] = split_stats(stats, 1).reshape(SLOTS, GROUPS, LANES)
 
     do_chunk(0, True)
-    chunks = half_tokens // SLOTS
+    chunks = tokens // SLOTS
     if chunks > 1:
         lax.fori_loop(1, chunks, lambda c, _: do_chunk(c, False), None)
 
@@ -357,13 +338,13 @@
     by_head = lambda x: VMEM((KVH, x.shape[0], HD), x.dtype)
     sems = pltpu.SemaphoreType.DMA((KVH,))
     hbm = whole(pltpu.HBM)
-    size = 2 * (suffix_keys.size + suffix_values.size)
-    sk, sv = on_core(
+    size = 2 * suffix_keys.size
+    sk = on_core(
         fetch_kernel,
-        [by_head(suffix_keys), by_head(suffix_values)],
-        (in_hbm(suffix_keys), in_hbm(suffix_values)),
-        in_specs=[hbm] * 2,
-        scratch_shapes=[sems, sems],
+        by_head(suffix_keys),
+        (in_hbm(suffix_keys),),
+        in_specs=[hbm],
+        scratch_shapes=[sems],
         cost=pl.CostEstimate(flops=0, bytes_accessed=size, transcendentals=0),
     )
     pair = swap(own, 1)
@@ -376,15 +357,15 @@
             own,
             near_core(pair),
             sk,
-            sv,
             new_keys,
             new_values,
+            in_hbm(suffix_values),
             in_hbm(doc_keys),
             in_hbm(doc_values),
         ),
-        in_specs=[whole()] * 7 + [hbm] * 2,
-        scratch_shapes=[sems, sems],
-        cost=pl.CostEstimate(flops=10**9, bytes_accessed=size, transcendentals=10**6),
+        in_specs=[whole()] * 6 + [hbm] * 3,
+        scratch_shapes=[by_head(suffix_values), sems, sems, sems],
+        cost=pl.CostEstimate(flops=10**9, bytes_accessed=3 * size, transcendentals=10**6),
     )
     for step, stage in enumerate(stages):
         arrived = []
@@ -393,12 +374,17 @@
         near = jnp.concatenate([near] + arrived, axis=0)
     far = swap(near, 1)
     tokens = lambda count: VMEM((count, HEADS + GROUPS, HD), jnp.bfloat16)
-    parts = on_core(
-        functools.partial(attend_kernel, flag_rows),
-        [tokens(devices // 2)] * 2,
-        (near_core(near), near_core(far), dk, dv, *local),
-        scratch_shapes=[VMEM((SLOTS * GROUPS, doc_keys.shape[0]), jnp.float32)],
-    )
+    near, far = near_core(near), near_core(far)
+    parts = [
+        on_core(
+            functools.partial(attend_kernel, flag_rows, which),
+            tokens(devices // 2),
+            (mine, other, dk, dv, *local),
+            scratch_shapes=[VMEM((SLOTS * GROUPS, doc_keys.shape[0]), jnp.float32)],
+            cost=pl.CostEstimate(flops=10**9, bytes_accessed=2 * size, transcendentals=10**6),
+        )
+        for which, mine, other in ((0, near, far), (1, far, near))
+    ]
     step = len(stages)
     stages.append((1,))
     while stages:

time: 36.5 us -> 34.7 us (0.951)
  waiting for transfers between devices: 11.4 us -> 9.38 us
  starting transfers between devices: 13.7 us -> 14.2 us
    ppermute x11, waiting for transfers between devices: 11.4 us -> 9.38 us  [swap(): return lax.ppermute(x, 'seq', [(i, i ^ bits) for i in range(devices)])]
    ppermute x11, starting transfers between devices: 13.7 us -> 14.2 us  [swap(): return lax.ppermute(x, 'seq', [(i, i ^ bits) for i in range(devices)])]
    pallas_call x7 -> x8, Pallas kernels: 11 us -> 10.7 us  [on_core(): pl.pallas_call(kernel, out_shape=out_shape, in_specs=kwargs.pop('in_specs...]
  transfers between devices with their start and end apart: 11 -> 11, of which waited for: 7 -> 6; matrix products, arithmetic and copies ran while one was open for 0% -> 0% of each run, Pallas kernels for 15% -> 19%
where the time goes in v4:
time: 34.7 us; the launch traced here: 34.5 us
  starting transfers between devices  14.2 us (41%)
  Pallas kernels  10.7 us (31%)
  waiting for transfers between devices  9.38 us (27%)
    ppermute x11, starting transfers between devices, swap(): return lax.ppermute(x, 'seq', [(i, i ^ bits) for i in range(devices)])  14.2 us
    pallas_call x8, Pallas kernels, on_core(): pl.pallas_call(kernel, out_shape=out_shape, in_specs=kwargs.pop('in_specs...  10.7 us
    ppermute x11, waiting for transfers between devices, swap(): return lax.ppermute(x, 'seq', [(i, i ^ bits) for i in range(devices)])  9.38 us
  transfers between devices with their start and end apart: 11, of which 6 were waited for; matrix products, arithmetic and copies ran while one was open for 0% of the time, Pallas kernels for 19%

profile of v4, /device:TPU:0, one launch (start us, length us, event | category | flops | bytes accessed | tf_op | source)
XLA Modules:
  0.0 34.5 jit_solution(14544044802723428096)
XLA Ops:
  0.0 0.9 %shard_map.91 = bf16[72,128]{1,0:T(8,128)(2,1)S(1)} custom-call(s32[1,32]{1,0:T(1,128)} %list_ref.1, bf16[1,8192]{1,0:T(2,128)(2,1)} %q_ref.1), custom_call_target="tpu_custom_call" | custom-call | tf_op jit(solution)/shard_map/pallas_call | solution.py:289
  0.9 3.6 %collective-permute-start = (bf16[1,72,128]{2,1,0:T(8,128)(2,1)S(1)}, bf16[1,72,128]{2,1,0:T(8,128)(2,1)S(1)}, u32[]{:S(2)}, u32[]{:S(2)}) collective-permute-start(bf16[1,72,128]{2,1,0:T(8,128)(2,1)S(1)} %bitcast.3), channel_id=1, source_target_pairs={{0,9},{1,8},{2,11},{3,10},{4,13},{5,12},{6,15},{7,14},{8,1},{9,0},... | collective-permute-start | bytes 55304 | tf_op jit(solution)/shard_map/ppermute | solution.py:306
  4.5 1.5 %collective-permute-done = bf16[1,72,128]{2,1,0:T(8,128)(2,1)S(1)} collective-permute-done((bf16[1,72,128]{2,1,0:T(8,128)(2,1)S(1)}, bf16[1,72,128]{2,1,0:T(8,128)(2,1)S(1)}, u32[]{:S(2)}, u32[]{:S(2)}) %collective-permute-start) | collective-permute-done | bytes 18464 | tf_op jit(solution)/shard_map/ppermute | solution.py:306
  5.9 2.8 %collective-permute-start.3 = (bf16[2,72,128]{2,1,0:T(8,128)(2,1)S(1)}, bf16[2,72,128]{2,1,0:T(8,128)(2,1)S(1)}, u32[]{:S(2)}, u32[]{:S(2)}) collective-permute-start(bf16[2,72,128]{2,1,0:T(8,128)(2,1)S(1)} %pad_maximum_fusion), channel_id=1, source_target_pairs={{0,7},{1,6},{2,5},{3,4},{4,3},{5,2},{6,1},{7,0},{8,15},{9,14},{10,... | collective-permute-start | bytes 110600 | tf_op jit(solution)/shard_map/ppermute | solution.py:306
  8.8 0.4 %collective-permute-start.2 = (bf16[2,72,128]{2,1,0:T(8,128)(2,1)S(1)}, bf16[2,72,128]{2,1,0:T(8,128)(2,1)S(1)}, u32[]{:S(2)}, u32[]{:S(2)}) collective-permute-start(bf16[2,72,128]{2,1,0:T(8,128)(2,1)S(1)} %pad_maximum_fusion), channel_id=1, source_target_pairs={{0,5},{1,4},{2,7},{3,6},{4,1},{5,0},{6,3},{7,2},{8,13},{9,12},{10,... | collective-permute-start | bytes 110600 | tf_op jit(solution)/shard_map/ppermute | solution.py:306
  9.2 0.2 collective-permute-start.1
  9.4 3.3 %collective-permute-done.1 = bf16[2,72,128]{2,1,0:T(8,128)(2,1)S(1)} collective-permute-done((bf16[2,72,128]{2,1,0:T(8,128)(2,1)S(1)}, bf16[2,72,128]{2,1,0:T(8,128)(2,1)S(1)}, u32[]{:S(2)}, u32[]{:S(2)}) %collective-permute-start.1) | collective-permute-done | bytes 36896 | tf_op jit(solution)/shard_map/ppermute | solution.py:306
  12.8 0.2 collective-permute-start.4
  13.0 0.4 %collective-permute-start.5 = (bf16[1,72,128]{2,1,0:T(8,128)(2,1)S(1)}, bf16[1,72,128]{2,1,0:T(8,128)(2,1)S(1)}, u32[]{:S(2)}, u32[]{:S(2)}) collective-permute-start(bf16[1,72,128]{2,1,0:T(8,128)(2,1)S(1)} %bitcast.5), channel_id=1, source_target_pairs={{0,1},{1,0},{2,3},{3,2},{4,5},{5,4},{6,7},{7,6},{8,9},{9,8},{10,11... | collective-permute-start | bytes 55304 | tf_op jit(solution)/shard_map/ppermute | solution.py:306
  13.4 1.6 %shard_map.92.sk_ref = bf16[8,1024,128]{2,1,0:T(8,128)(2,1)S(1)} custom-call(bf16[1024,1024]{1,0:T(8,128)(2,1)} %source.1), custom_call_target="tpu_custom_call" | custom-call | bytes 2097152 | tf_op jit(solution)/shard_map/pallas_call | solution.py:289
  15.0 3.2 %shard_map.93 = (f32[8,16,128]{2,1,0:T(8,128)S(1)}, f32[8,16,128]{2,1,0:T(8,128)S(1)}, f32[8,16,128]{2,1,0:T(8,128)S(1)}, bf16[8,1024,128]{2,1,0:T(8,128)(2,1)S(1)}, bf16[8,1024,128]{2,1,0:T(8,128)(2,1)S(1)}) custom-call(s32[1,8]{1,0:T(1,128)S(1)} %bitcast.7, bf16[1,72,128]{2,1,0:T(8,128)(2,1)S(1)} %bitcast.6, ...), custom_call_target="tpu_custom_call" | custom-call | flops 1000000000 | bytes 6291456 | tf_op jit(solution)/shard_map/pallas_call | solution.py:289
  18.3 1.8 %shard_map.95 = bf16[8,72,128]{2,1,0:T(8,128)(2,1)S(1)} custom-call(bf16[8,72,128]{2,1,0:T(8,128)(2,1)S(1)} %collective-permute-done.4.other_ref.token_ref, bf16[8,72,128]{2,1,0:T(8,128)(2,1)S(1)} %constant_dynamic-update-slice_fusion.token_ref.other_ref, bf16[8,1024,128]{2,1,0:T(8,128)(2,1)S(1)} %get-tuple-element.16.dk_ref, ...), custom_call_target="tpu_custom_call" | custom-call | flops 1000000000 | bytes 4194304 | tf_op jit(solution)/shard_map/pallas_call | solution.py:289
  20.0 0.2 collective-permute-start.6
  20.2 1.8 %shard_map.94.refs_0_ = bf16[8,72,128]{2,1,0:T(8,128)(2,1)S(1)} custom-call(bf16[8,72,128]{2,1,0:T(8,128)(2,1)S(1)} %constant_dynamic-update-slice_fusion.token_ref.other_ref, bf16[8,72,128]{2,1,0:T(8,128)(2,1)S(1)} %collective-permute-done.4.other_ref.token_ref, bf16[8,1024,128]{2,1,0:T(8,128)(2,1)S(1)} %get-tuple-element.16.dk_ref, ...), custom_call_target="tpu_custom_call" | custom-call | flops 1000000000 | bytes 4194304 | tf_op jit(solution)/shard_map/pallas_call | solution.py:289
  22.0 0.4 %shard_map.96 = (bf16[2,72,128]{2,1,0:T(8,128)(2,1)S(1)}, bf16[2,72,128]{2,1,0:T(8,128)(2,1)S(1)}, bf16[2,72,128]{2,1,0:T(8,128)(2,1)S(1)}, bf16[2,72,128]{2,1,0:T(8,128)(2,1)S(1)}) custom-call(bf16[8,72,128]{2,1,0:T(8,128)(2,1)S(1)} %shard_map.94.refs_0_, bf16[8,72,128]{2,1,0:T(8,128)(2,1)S(1)} %collective-permute-done.6.refs_1_), custom_call_target="tpu_custom_call" | custom-call | tf_op jit(solution)/shard_map/pallas_call | solution.py:289
  22.4 0.6 %collective-permute-start.7 = (bf16[2,72,128]{2,1,0:T(8,128)(2,1)S(1)}, bf16[2,72,128]{2,1,0:T(8,128)(2,1)S(1)}, u32[]{:S(2)}, u32[]{:S(2)}) collective-permute-start(bf16[2,72,128]{2,1,0:T(8,128)(2,1)S(1)} %get-tuple-element.22), channel_id=1, source_target_pairs={{0,3},{1,2},{2,1},{3,0},{4,7},{5,6},{6,5},{7,4},{8,11},{9,10},{10,... | collective-permute-start | bytes 110600 | tf_op jit(solution)/shard_map/ppermute | solution.py:306
  23.0 1.6 %collective-permute-start.8 = (bf16[2,72,128]{2,1,0:T(8,128)(2,1)S(1)}, bf16[2,72,128]{2,1,0:T(8,128)(2,1)S(1)}, u32[]{:S(2)}, u32[]{:S(2)}) collective-permute-start(bf16[2,72,128]{2,1,0:T(8,128)(2,1)S(1)} %get-tuple-element.23), channel_id=1, source_target_pairs={{0,5},{1,4},{2,7},{3,6},{4,1},{5,0},{6,3},{7,2},{8,13},{9,12},{10,... | collective-permute-start | bytes 110600 | tf_op jit(solution)/shard_map/ppermute | solution.py:306
  24.5 1.1 %collective-permute-start.9 = (bf16[2,72,128]{2,1,0:T(8,128)(2,1)S(1)}, bf16[2,72,128]{2,1,0:T(8,128)(2,1)S(1)}, u32[]{:S(2)}, u32[]{:S(2)}) collective-permute-start(bf16[2,72,128]{2,1,0:T(8,128)(2,1)S(1)} %get-tuple-element.24), channel_id=1, source_target_pairs={{0,7},{1,6},{2,5},{3,4},{4,3},{5,2},{6,1},{7,0},{8,15},{9,14},{10,... | collective-permute-start | bytes 110600 | tf_op jit(solution)/shard_map/ppermute | solution.py:306
  25.8 0.5 %collective-permute-done.8.refs_2_ = bf16[2,72,128]{2,1,0:T(8,128)(2,1)S(1)} collective-permute-done((bf16[2,72,128]{2,1,0:T(8,128)(2,1)S(1)}, bf16[2,72,128]{2,1,0:T(8,128)(2,1)S(1)}, u32[]{:S(2)}, u32[]{:S(2)}) %collective-permute-start.8) | collective-permute-done | bytes 36896 | tf_op jit(solution)/shard_map/ppermute | solution.py:306
  26.4 2.5 %collective-permute-done.9.refs_3_ = bf16[2,72,128]{2,1,0:T(8,128)(2,1)S(1)} collective-permute-done((bf16[2,72,128]{2,1,0:T(8,128)(2,1)S(1)}, bf16[2,72,128]{2,1,0:T(8,128)(2,1)S(1)}, u32[]{:S(2)}, u32[]{:S(2)}) %collective-permute-start.9) | collective-permute-done | bytes 36896 | tf_op jit(solution)/shard_map/ppermute | solution.py:306
  28.8 0.3 shard_map.97
  29.1 3.1 %collective-permute-start.10 = (bf16[1,72,128]{2,1,0:T(8,128)(2,1)S(1)}, bf16[1,72,128]{2,1,0:T(8,128)(2,1)S(1)}, u32[]{:S(2)}, u32[]{:S(2)}) collective-permute-start(bf16[1,72,128]{2,1,0:T(8,128)(2,1)S(1)} %get-tuple-element.26), channel_id=1, source_target_pairs={{0,9},{1,8},{2,11},{3,10},{4,13},{5,12},{6,15},{7,14},{8,1},{9,0},... | collective-permute-start | bytes 55304 | tf_op jit(solution)/shard_map/ppermute | solution.py:306
  32.2 1.5 %collective-permute-done.10.refs_1_ = bf16[1,72,128]{2,1,0:T(8,128)(2,1)S(1)} collective-permute-done((bf16[1,72,128]{2,1,0:T(8,128)(2,1)S(1)}, bf16[1,72,128]{2,1,0:T(8,128)(2,1)S(1)}, u32[]{:S(2)}, u32[]{:S(2)}) %collective-permute-start.10) | collective-permute-done | bytes 18464 | tf_op jit(solution)/shard_map/ppermute | solution.py:306
  33.7 0.8 %shard_map.98 = bf16[1,8192]{1,0:T(2,128)(2,1)} custom-call(bf16[1,72,128]{2,1,0:T(8,128)(2,1)S(1)} %get-tuple-element.25.refs_0_, bf16[1,72,128]{2,1,0:T(8,128)(2,1)S(1)} %collective-permute-done.10.refs_1_), custom_call_target="tpu_custom_call" | custom-call | tf_op jit(solution)/shard_map/pallas_call | solution.py:289
  (18 shorter events, 0.3 us)
Async XLA Ops:
  0.9 5.0 %collective-permute-start = (bf16[1,72,128]{2,1,0:T(8,128)(2,1)S(1)}, bf16[1,72,128]{2,1,0:T(8,128)(2,1)S(1)}, u32[]{:S(2)}, u32[]{:S(2)}) collective-permute-start(bf16[1,72,128]{2,1,0:T(8,128)(2,1)S(1)} %bitcast.3), channel_id=1, source_target_pairs={{0,9},{1,8},{2,11},{3,10},{4,13},{5,12},{6,15},{7,14},{8,1},{9,0},... | collective-permute-start | bytes 55304 | tf_op jit(solution)/shard_map/ppermute | solution.py:306
  5.9 6.8 %collective-permute-start.3 = (bf16[2,72,128]{2,1,0:T(8,128)(2,1)S(1)}, bf16[2,72,128]{2,1,0:T(8,128)(2,1)S(1)}, u32[]{:S(2)}, u32[]{:S(2)}) collective-permute-start(bf16[2,72,128]{2,1,0:T(8,128)(2,1)S(1)} %pad_maximum_fusion), channel_id=1, source_target_pairs={{0,7},{1,6},{2,5},{3,4},{4,3},{5,2},{6,1},{7,0},{8,15},{9,14},{10,... | collective-permute-start | bytes 110600 | tf_op jit(solution)/shard_map/ppermute | solution.py:306
  8.8 3.9 %collective-permute-start.2 = (bf16[2,72,128]{2,1,0:T(8,128)(2,1)S(1)}, bf16[2,72,128]{2,1,0:T(8,128)(2,1)S(1)}, u32[]{:S(2)}, u32[]{:S(2)}) collective-permute-start(bf16[2,72,128]{2,1,0:T(8,128)(2,1)S(1)} %pad_maximum_fusion), channel_id=1, source_target_pairs={{0,5},{1,4},{2,7},{3,6},{4,1},{5,0},{6,3},{7,2},{8,13},{9,12},{10,... | collective-permute-start | bytes 110600 | tf_op jit(solution)/shard_map/ppermute | solution.py:306
  9.2 3.5 %collective-permute-start.1 = (bf16[2,72,128]{2,1,0:T(8,128)(2,1)S(1)}, bf16[2,72,128]{2,1,0:T(8,128)(2,1)S(1)}, u32[]{:S(2)}, u32[]{:S(2)}) collective-permute-start(bf16[2,72,128]{2,1,0:T(8,128)(2,1)S(1)} %pad_maximum_fusion), channel_id=1, source_target_pairs={{0,3},{1,2},{2,1},{3,0},{4,7},{5,6},{6,5},{7,4},{8,11},{9,10},{10,... | collective-permute-start | bytes 110600 | tf_op jit(solution)/shard_map/ppermute | solution.py:306
  12.7 2.3 %copy-start = (bf16[1,1024]{1,0:T(2,128)(2,1)S(1)}, bf16[1,1024]{1,0:T(2,128)(2,1)}, u32[]{:S(2)}) copy-start(bf16[1,1024]{1,0:T(2,128)(2,1)} %nk_ref.1) | copy-start | bytes 6148
  12.8 2.3 %copy-start.1 = (bf16[1,1024]{1,0:T(2,128)(2,1)S(1)}, bf16[1,1024]{1,0:T(2,128)(2,1)}, u32[]{:S(2)}) copy-start(bf16[1,1024]{1,0:T(2,128)(2,1)} %nv_ref.1) | copy-start | bytes 6148
  12.8 2.3 %copy-start.2 = (s32[8]{0:T(128)S(1)}, s32[8]{0:T(128)}, u32[]{:S(2)}) copy-start(s32[8]{0:T(128)} %param.17) | copy-start | bytes 100
  12.8 5.5 %collective-permute-start.4 = (bf16[8,72,128]{2,1,0:T(8,128)(2,1)S(1)}, bf16[8,72,128]{2,1,0:T(8,128)(2,1)S(1)}, u32[]{:S(2)}, u32[]{:S(2)}) collective-permute-start(bf16[8,72,128]{2,1,0:T(8,128)(2,1)S(1)} %constant_dynamic-update-slice_fusion.token_ref.other_ref), channel_id=1, source_target_pairs={{0,1},{1,0},{2,3},{3,2},{4,5},{5,4},{6,7},{7,6},{8,9},{9,8},{10,11... | collective-permute-start | bytes 442376 | tf_op jit(solution)/shard_map/ppermute | solution.py:306
  13.0 2.0 %collective-permute-start.5 = (bf16[1,72,128]{2,1,0:T(8,128)(2,1)S(1)}, bf16[1,72,128]{2,1,0:T(8,128)(2,1)S(1)}, u32[]{:S(2)}, u32[]{:S(2)}) collective-permute-start(bf16[1,72,128]{2,1,0:T(8,128)(2,1)S(1)} %bitcast.5), channel_id=1, source_target_pairs={{0,1},{1,0},{2,3},{3,2},{4,5},{5,4},{6,7},{7,6},{8,9},{9,8},{10,11... | collective-permute-start | bytes 55304 | tf_op jit(solution)/shard_map/ppermute | solution.py:306
  20.0 1.9 %collective-permute-start.6 = (bf16[8,72,128]{2,1,0:T(8,128)(2,1)S(1)}, bf16[8,72,128]{2,1,0:T(8,128)(2,1)S(1)}, u32[]{:S(2)}, u32[]{:S(2)}) collective-permute-start(bf16[8,72,128]{2,1,0:T(8,128)(2,1)S(1)} %shard_map.95), channel_id=1, source_target_pairs={{0,1},{1,0},{2,3},{3,2},{4,5},{5,4},{6,7},{7,6},{8,9},{9,8},{10,11... | collective-permute-start | bytes 442376 | tf_op jit(solution)/shard_map/ppermute | solution.py:306
  22.4 3.4 %collective-permute-start.7 = (bf16[2,72,128]{2,1,0:T(8,128)(2,1)S(1)}, bf16[2,72,128]{2,1,0:T(8,128)(2,1)S(1)}, u32[]{:S(2)}, u32[]{:S(2)}) collective-permute-start(bf16[2,72,128]{2,1,0:T(8,128)(2,1)S(1)} %get-tuple-element.22), channel_id=1, source_target_pairs={{0,3},{1,2},{2,1},{3,0},{4,7},{5,6},{6,5},{7,4},{8,11},{9,10},{10,... | collective-permute-start | bytes 110600 | tf_op jit(solution)/shard_map/ppermute | solution.py:306
  23.0 3.4 %collective-permute-start.8 = (bf16[2,72,128]{2,1,0:T(8,128)(2,1)S(1)}, bf16[2,72,128]{2,1,0:T(8,128)(2,1)S(1)}, u32[]{:S(2)}, u32[]{:S(2)}) collective-permute-start(bf16[2,72,128]{2,1,0:T(8,128)(2,1)S(1)} %get-tuple-element.23), channel_id=1, source_target_pairs={{0,5},{1,4},{2,7},{3,6},{4,1},{5,0},{6,3},{7,2},{8,13},{9,12},{10,... | collective-permute-start | bytes 110600 | tf_op jit(solution)/shard_map/ppermute | solution.py:306
  24.5 4.3 %collective-permute-start.9 = (bf16[2,72,128]{2,1,0:T(8,128)(2,1)S(1)}, bf16[2,72,128]{2,1,0:T(8,128)(2,1)S(1)}, u32[]{:S(2)}, u32[]{:S(2)}) collective-permute-start(bf16[2,72,128]{2,1,0:T(8,128)(2,1)S(1)} %get-tuple-element.24), channel_id=1, source_target_pairs={{0,7},{1,6},{2,5},{3,4},{4,3},{5,2},{6,1},{7,0},{8,15},{9,14},{10,... | collective-permute-start | bytes 110600 | tf_op jit(solution)/shard_map/ppermute | solution.py:306
  29.1 4.6 %collective-permute-start.10 = (bf16[1,72,128]{2,1,0:T(8,128)(2,1)S(1)}, bf16[1,72,128]{2,1,0:T(8,128)(2,1)S(1)}, u32[]{:S(2)}, u32[]{:S(2)}) collective-permute-start(bf16[1,72,128]{2,1,0:T(8,128)(2,1)S(1)} %get-tuple-element.26), channel_id=1, source_target_pairs={{0,9},{1,8},{2,11},{3,10},{4,13},{5,12},{6,15},{7,14},{8,1},{9,0},... | collective-permute-start | bytes 55304 | tf_op jit(solution)/shard_map/ppermute | solution.py:306

commit v5 on v4

--- a/solution.py
+++ b/solution.py
@@ -19,7 +19,7 @@
 
 NEG_BIG = -1e30
 NEG_SAFE = -5e29
-AHEAD = 2
+AHEAD = 4
 DOC_AHEAD = 2
 EXP2_SCALE = HD**-0.5 * math.log2(math.e)
 
@@ -54,52 +54,29 @@
     return top, jnp.sum(weights, axis=-1, keepdims=True), weights.astype(jnp.bfloat16)
 
 
-def head_copies(source, target, sem):
-    return [
-        pltpu.make_async_copy(source.at[:, pl.ds(head * HD, HD)], target.at[head], sem.at[head])
-        for head in range(KVH)
-    ]
-
-
-def fetch_kernel(source, target, sem):
-    copies = head_copies(source, target, sem)
-    for copy in copies:
-        copy.start()
-    for copy in copies:
-        copy.wait()
-
-
 def suffix_kernel(
     len_ref,
     own_ref,
     pair_ref,
     sk_ref,
+    sv_ref,
     nk_ref,
     nv_ref,
-    sv_hbm,
-    dk_hbm,
-    dv_hbm,
+    dk_ref,
+    dv_ref,
     top_ref,
     total_ref,
     out_ref,
-    dk_ref,
-    dv_ref,
-    sv_ref,
-    sv_sem,
-    dk_sem,
-    dv_sem,
+    dk_out_ref,
+    dv_out_ref,
 ):
-    arriving = head_copies(sv_hbm, sv_ref, sv_sem)
-    copies = head_copies(dk_hbm, dk_ref, dk_sem) + head_copies(dv_hbm, dv_ref, dv_sem)
-    for copy in arriving + copies:
-        copy.start()
     me = lax.axis_index("seq")
     parity = lax.rem(me, 2)
     mine = lax.broadcasted_iota(jnp.int32, len_ref.shape, 1) == lax.div(me, 2)
     length = jnp.sum(
         jnp.where(mine, len_ref[...].astype(jnp.float32), 0.0), axis=1, keepdims=True
     )
-    live_left = length.astype(jnp.int32) - parity * sk_ref.shape[1]
+    live_left = length.astype(jnp.int32) - parity * sv_ref.shape[0]
 
     def scores_of(head):
         rows = slice(head * GROUPS, (head + 1) * GROUPS)
@@ -107,7 +84,7 @@
         q = jnp.concatenate(
             [ref[0, rows, :].astype(jnp.float32) for ref in (own_ref, pair_ref)], axis=0
         )
-        scores = lane_dot(q.astype(jnp.bfloat16), sk_ref[head])
+        scores = lane_dot(q.astype(jnp.bfloat16), sk_ref[:, cols])
         position = lax.broadcasted_iota(jnp.int32, scores.shape, 1)
         scores = jnp.where(position < live_left, scores, NEG_BIG)
         n_top = jnp.sum(q * nk_ref[:, cols].astype(jnp.float32), axis=-1, keepdims=True)
@@ -125,15 +102,14 @@
         weights = jnp.exp2((scores - base) * EXP2_SCALE)
         n_scale = jnp.exp2((n_top - base) * EXP2_SCALE)
         total = jnp.sum(weights, axis=-1, keepdims=True) + n_scale
-        arriving[head].wait()
         out = jnp.dot(
-            weights.astype(jnp.bfloat16), sv_ref[head], preferred_element_type=jnp.float32
+            weights.astype(jnp.bfloat16), sv_ref[:, cols], preferred_element_type=jnp.float32
         )
         top_ref[head] = jnp.broadcast_to(top, (2 * GROUPS, LANES))
         total_ref[head] = jnp.broadcast_to(total, (2 * GROUPS, LANES))
         out_ref[head] = out + n_scale * nv_ref[:, cols].astype(jnp.float32)
-    for copy in copies:
-        copy.wait()
+        dk_out_ref[head] = dk_ref[:, cols]
+        dv_out_ref[head] = dv_ref[:, cols]
 
 
 def split_stats(stats, axis):
@@ -154,50 +130,45 @@
     return top, total
 
 
-def attend_kernel(
-    flag_rows,
-    which,
-    token_ref,
-    other_ref,
-    dk_ref,
-    dv_ref,
-    top_ref,
-    total_ref,
-    extra_ref,
-    out_ref,
-    bias_ref,
-):
+def attend_kernel(which, flag_rows, *refs):
+    if flag_rows:
+        token_ref, other_ref, *refs = refs
+    else:
+        token_ref, bias_ref, *refs = refs
+    dk_ref, dv_ref, top_ref, total_ref, extra_ref, out_ref, *refs = refs
+    if flag_rows:
+        (bias_ref,) = refs
     tokens = token_ref.shape[0]
     span = dk_ref.shape[1]
+    blocks_here = span // BLOCK
     rows_here = SLOTS * GROUPS
-    first_block = lax.axis_index("seq") * (span // BLOCK)
+    first_block = lax.axis_index("seq") * blocks_here
     flag_row = lax.div(first_block, LANES)
     flag_lane = lax.rem(first_block, LANES)
-    row_ids = lax.broadcasted_iota(jnp.int32, (1, flag_rows, LANES), 1)
-    pick = (
-        lax.broadcasted_iota(jnp.int32, (LANES, span), 0)
-        == flag_lane + lax.broadcasted_iota(jnp.int32, (LANES, span), 1) // BLOCK
-    ).astype(jnp.float32).astype(jnp.bfloat16)
     lane_ids = lax.broadcasted_iota(jnp.int32, (rows_here, LANES), 1)
     own = slice(which * GROUPS, (which + 1) * GROUPS)
 
     def do_chunk(chunk, local):
         slots = pl.ds(chunk * SLOTS, SLOTS)
-        flags = token_ref[slots, HEADS:, :].astype(jnp.float32) + other_ref[
-            slots, HEADS:, :
-        ].astype(jnp.float32)
-        flags = jnp.sum(jnp.where(row_ids == flag_row, flags, 0.0), axis=1)
-        count = jnp.dot(flags.astype(jnp.bfloat16), pick, preferred_element_type=jnp.float32)
-        bias = jnp.where(count > 0.5, 0.0, NEG_BIG)
-        for s in range(SLOTS):
-            bias_ref[s * GROUPS : (s + 1) * GROUPS, :] = jnp.broadcast_to(
-                bias[s : s + 1, :], (GROUPS, span)
-            )
+        here = pl.ds(chunk * rows_here, rows_here)
+        if flag_rows:
+            flags = token_ref[slots, HEADS:, :].astype(jnp.float32) + other_ref[
+                slots, HEADS:, :
+            ].astype(jnp.float32)
+            row_ids = lax.broadcasted_iota(jnp.int32, (1, flag_rows, LANES), 1)
+            flags = jnp.sum(jnp.where(row_ids == flag_row, flags, 0.0), axis=1)
+            flags = pltpu.roll(flags, LANES - flag_lane, 1)
+            bias = jnp.where(flags > 0.5, 0.0, NEG_BIG)
+            for b in range(blocks_here):
+                wide = jnp.broadcast_to(bias[:, b : b + 1], (SLOTS, BLOCK))
+                bias_ref[here, b * BLOCK : (b + 1) * BLOCK] = jnp.broadcast_to(
+                    wide[:, None, :], (SLOTS, GROUPS, BLOCK)
+                ).reshape(rows_here, BLOCK)
 
         def scores_of(head):
             rows = slice(head * GROUPS, (head + 1) * GROUPS)
             q = token_ref[slots, rows, :].astype(jnp.float32).reshape(rows_here, HD)
-            return lane_dot(q.astype(jnp.bfloat16), dk_ref[head]) + bias_ref[...]
+            return lane_dot(q.astype(jnp.bfloat16), dk_ref[head]) + bias_ref[here, :]
 
         stats = jnp.zeros((rows_here, LANES), jnp.float32)
         ready = [scores_of(head) for head in range(DOC_AHEAD)]
@@ -207,7 +178,9 @@
             if head + DOC_AHEAD < KVH:
                 ready.append(scores_of(head + DOC_AHEAD))
             top, total, weights = partial_softmax(scores)
-            out = jnp.dot(weights, dv_ref[head], preferred_element_type=jnp.float32)
+            out = jnp.dot(
+                weights, dv_ref[head], preferred_element_type=jnp.float32
+            )
             if local:
                 x_top, y_top = top[:GROUPS], top_ref[head, own, 0:1]
                 new_top = jnp.maximum(x_top, y_top)
@@ -239,18 +212,14 @@
     weights = [jnp.exp2(t - top) * total for t, total in stats]
     total = functools.reduce(jnp.add, weights)
     scale = 1.0 / jnp.maximum(total, 1.0)
-    return top, total, [w * scale for w in weights]
+    return top, total, [w * scale for w in weights[1:]]
 
 
 def mixed_units(head, refs, weights):
     rows = slice(head * GROUPS, (head + 1) * GROUPS)
-    return functools.reduce(
-        jnp.add,
-        [
-            ref[:, rows, :].astype(jnp.float32) * w[:, :, head : head + 1]
-            for ref, w in zip(refs, weights)
-        ],
-    )
+    first, *others = [ref[:, rows, :].astype(jnp.float32) for ref in refs]
+    steps = [(u - first) * w[:, :, head : head + 1] for u, w in zip(others, weights)]
+    return functools.reduce(jnp.add, steps, first)
 
 
 def merge_kernel(count, *refs):
@@ -332,39 +301,29 @@
         pack_kernel,
         VMEM((HEADS + flag_rows, HD), jnp.bfloat16),
         (in_hbm(keep_lists), in_hbm(queries)),
+        cost=pl.CostEstimate(flops=10**10, bytes_accessed=10**5, transcendentals=0),
     )
     near = packed[None]
     own = near
-    by_head = lambda x: VMEM((KVH, x.shape[0], HD), x.dtype)
-    sems = pltpu.SemaphoreType.DMA((KVH,))
-    hbm = whole(pltpu.HBM)
+    heads_of = lambda x: VMEM((KVH, x.shape[0], HD), x.dtype)
     size = 2 * suffix_keys.size
-    sk = on_core(
-        fetch_kernel,
-        by_head(suffix_keys),
-        (in_hbm(suffix_keys),),
-        in_specs=[hbm],
-        scratch_shapes=[sems],
-        cost=pl.CostEstimate(flops=0, bytes_accessed=size, transcendentals=0),
-    )
     pair = swap(own, 1)
     stat = VMEM((KVH, 2 * GROUPS, LANES), jnp.float32)
     *local, dk, dv = on_core(
         suffix_kernel,
-        [stat, stat, VMEM((KVH, 2 * GROUPS, HD), jnp.float32)] + [by_head(doc_keys), by_head(doc_values)],
+        [stat, stat, VMEM((KVH, 2 * GROUPS, HD), jnp.float32)]
+        + [heads_of(doc_keys), heads_of(doc_values)],
         (
             near_core(suffix_lengths[None]),
             own,
             near_core(pair),
-            sk,
+            suffix_keys,
+            suffix_values,
             new_keys,
             new_values,
-            in_hbm(suffix_values),
-            in_hbm(doc_keys),
-            in_hbm(doc_values),
+            doc_keys,
+            doc_values,
         ),
-        in_specs=[whole()] * 6 + [hbm] * 3,
-        scratch_shapes=[by_head(suffix_values), sems, sems, sems],
         cost=pl.CostEstimate(flops=10**9, bytes_accessed=3 * size, transcendentals=10**6),
     )
     for step, stage in enumerate(stages):
@@ -375,16 +334,18 @@
     far = swap(near, 1)
     tokens = lambda count: VMEM((count, HEADS + GROUPS, HD), jnp.bfloat16)
     near, far = near_core(near), near_core(far)
-    parts = [
-        on_core(
-            functools.partial(attend_kernel, flag_rows, which),
-            tokens(devices // 2),
-            (mine, other, dk, dv, *local),
-            scratch_shapes=[VMEM((SLOTS * GROUPS, doc_keys.shape[0]), jnp.float32)],
-            cost=pl.CostEstimate(flops=10**9, bytes_accessed=2 * size, transcendentals=10**6),
-        )
-        for which, mine, other in ((0, near, far), (1, far, near))
-    ]
+    half = tokens(devices // 2)
+    cost = pl.CostEstimate(flops=10**9, bytes_accessed=2 * size, transcendentals=10**6)
+    span = doc_keys.shape[0]
+    caches = (dk, dv, *local)
+    sent, bias = on_core(
+        functools.partial(attend_kernel, 1, flag_rows),
+        [half, VMEM((devices // 2 * GROUPS, span), jnp.float32)],
+        (far, near, *caches),
+        cost=cost,
+    )
+    kept = on_core(functools.partial(attend_kernel, 0, 0), half, (near, bias, *caches), cost=cost)
+    parts = [kept, sent]
     step = len(stages)
     stages.append((1,))
     while stages:

time: 34.7 us -> 32.9 us (0.948)
  Pallas kernels: 10.7 us -> 7.91 us
  waiting for transfers between devices: 9.38 us -> 10.6 us
    pallas_call x8 -> x7, Pallas kernels: 10.7 us -> 7.91 us  [on_core(): pl.pallas_call(kernel, out_shape=out_shape, in_specs=kwargs.pop('in_specs...]
    ppermute x11, waiting for transfers between devices: 9.38 us -> 10.6 us  [swap(): return lax.ppermute(x, 'seq', [(i, i ^ bits) for i in range(devices)])]
  transfers between devices with their start and end apart: 11 -> 11, of which waited for: 6 -> 7; matrix products, arithmetic and copies ran while one was open for 0% -> 0% of each run, Pallas kernels for 19% -> 12%
where the time goes in v5:
time: 32.9 us; the launch traced here: 32.8 us
  starting transfers between devices  14 us (43%)
  waiting for transfers between devices  10.6 us (32%)
  Pallas kernels  7.91 us (24%)
    ppermute x11, starting transfers between devices, swap(): return lax.ppermute(x, 'seq', [(i, i ^ bits) for i in range(devices)])  14 us
    ppermute x11, waiting for transfers between devices, swap(): return lax.ppermute(x, 'seq', [(i, i ^ bits) for i in range(devices)])  10.6 us
    pallas_call x7, Pallas kernels, on_core(): pl.pallas_call(kernel, out_shape=out_shape, in_specs=kwargs.pop('in_specs...  7.91 us
  transfers between devices with their start and end apart: 11, of which 7 were waited for; matrix products, arithmetic and copies ran while one was open for 0% of the time, Pallas kernels for 12%

profile of v5, /device:TPU:0, one launch (start us, length us, event | category | flops | bytes accessed | tf_op | source)
XLA Modules:
  0.0 32.8 jit_solution(15583043165360556277)
XLA Ops:
  0.0 1.0 %shard_map.91 = bf16[72,128]{1,0:T(8,128)(2,1)S(1)} custom-call(s32[1,32]{1,0:T(1,128)} %list_ref.1, bf16[1,8192]{1,0:T(2,128)(2,1)} %q_ref.1), custom_call_target="tpu_custom_call" | custom-call | flops 10000000000 | bytes 100000 | tf_op jit(solution)/shard_map/pallas_call | solution.py:258
  1.1 3.6 %collective-permute-start = (bf16[1,72,128]{2,1,0:T(8,128)(2,1)S(1)}, bf16[1,72,128]{2,1,0:T(8,128)(2,1)S(1)}, u32[]{:S(2)}, u32[]{:S(2)}) collective-permute-start(bf16[1,72,128]{2,1,0:T(8,128)(2,1)S(1)} %bitcast.3), channel_id=1, source_target_pairs={{0,9},{1,8},{2,11},{3,10},{4,13},{5,12},{6,15},{7,14},{8,1},{9,0},... | collective-permute-start | bytes 55304 | tf_op jit(solution)/shard_map/ppermute | solution.py:275
  4.7 1.5 %collective-permute-done = bf16[1,72,128]{2,1,0:T(8,128)(2,1)S(1)} collective-permute-done((bf16[1,72,128]{2,1,0:T(8,128)(2,1)S(1)}, bf16[1,72,128]{2,1,0:T(8,128)(2,1)S(1)}, u32[]{:S(2)}, u32[]{:S(2)}) %collective-permute-start) | collective-permute-done | bytes 18464 | tf_op jit(solution)/shard_map/ppermute | solution.py:275
  6.1 2.8 %collective-permute-start.3 = (bf16[2,72,128]{2,1,0:T(8,128)(2,1)S(1)}, bf16[2,72,128]{2,1,0:T(8,128)(2,1)S(1)}, u32[]{:S(2)}, u32[]{:S(2)}) collective-permute-start(bf16[2,72,128]{2,1,0:T(8,128)(2,1)S(1)} %pad_maximum_fusion), channel_id=1, source_target_pairs={{0,7},{1,6},{2,5},{3,4},{4,3},{5,2},{6,1},{7,0},{8,15},{9,14},{10,... | collective-permute-start | bytes 110600 | tf_op jit(solution)/shard_map/ppermute | solution.py:275
  9.0 0.4 %collective-permute-start.2 = (bf16[2,72,128]{2,1,0:T(8,128)(2,1)S(1)}, bf16[2,72,128]{2,1,0:T(8,128)(2,1)S(1)}, u32[]{:S(2)}, u32[]{:S(2)}) collective-permute-start(bf16[2,72,128]{2,1,0:T(8,128)(2,1)S(1)} %pad_maximum_fusion), channel_id=1, source_target_pairs={{0,5},{1,4},{2,7},{3,6},{4,1},{5,0},{6,3},{7,2},{8,13},{9,12},{10,... | collective-permute-start | bytes 110600 | tf_op jit(solution)/shard_map/ppermute | solution.py:275
  9.4 0.2 collective-permute-start.1
  9.6 3.3 %collective-permute-done.1 = bf16[2,72,128]{2,1,0:T(8,128)(2,1)S(1)} collective-permute-done((bf16[2,72,128]{2,1,0:T(8,128)(2,1)S(1)}, bf16[2,72,128]{2,1,0:T(8,128)(2,1)S(1)}, u32[]{:S(2)}, u32[]{:S(2)}) %collective-permute-start.1) | collective-permute-done | bytes 36896 | tf_op jit(solution)/shard_map/ppermute | solution.py:275
  13.1 0.4 %collective-permute-start.5 = (bf16[1,72,128]{2,1,0:T(8,128)(2,1)S(1)}, bf16[1,72,128]{2,1,0:T(8,128)(2,1)S(1)}, u32[]{:S(2)}, u32[]{:S(2)}) collective-permute-start(bf16[1,72,128]{2,1,0:T(8,128)(2,1)S(1)} %bitcast.5), channel_id=1, source_target_pairs={{0,1},{1,0},{2,3},{3,2},{4,5},{5,4},{6,7},{7,6},{8,9},{9,8},{10,11... | collective-permute-start | bytes 55304 | tf_op jit(solution)/shard_map/ppermute | solution.py:275
  13.5 0.9 %collective-permute-done.5.pair_ref = bf16[1,72,128]{2,1,0:T(8,128)(2,1)S(1)} collective-permute-done((bf16[1,72,128]{2,1,0:T(8,128)(2,1)S(1)}, bf16[1,72,128]{2,1,0:T(8,128)(2,1)S(1)}, u32[]{:S(2)}, u32[]{:S(2)}) %collective-permute-start.5) | collective-permute-done | bytes 18464 | tf_op jit(solution)/shard_map/ppermute | solution.py:275
  14.5 2.1 %shard_map.92 = (f32[8,16,128]{2,1,0:T(8,128)S(1)}, f32[8,16,128]{2,1,0:T(8,128)S(1)}, f32[8,16,128]{2,1,0:T(8,128)S(1)}, bf16[8,1024,128]{2,1,0:T(8,128)(2,1)S(1)}, bf16[8,1024,128]{2,1,0:T(8,128)(2,1)S(1)}) custom-call(s32[1,8]{1,0:T(1,128)S(1)} %bitcast.7, bf16[1,72,128]{2,1,0:T(8,128)(2,1)S(1)} %bitcast.6, ...), custom_call_target="tpu_custom_call" | custom-call | flops 1000000000 | bytes 6291456 | tf_op jit(solution)/shard_map/pallas_call | solution.py:258
  16.6 1.7 %shard_map.93 = (bf16[8,72,128]{2,1,0:T(8,128)(2,1)S(1)}, f32[64,1024]{1,0:T(8,128)S(1)}) custom-call(bf16[8,72,128]{2,1,0:T(8,128)(2,1)S(1)} %collective-permute-done.4.refs_0_, bf16[8,72,128]{2,1,0:T(8,128)(2,1)S(1)} %constant_dynamic-update-slice_fusion.refs_1_.refs_0_, bf16[8,1024,128]{2,1,0:T(8,128)(2,1)S(1)} %get-tuple-element.18.refs_2_, ...), custom_call_target="tpu_custom_call" | custom-call | flops 1000000000 | bytes 4194304 | tf_op jit(solution)/shard_map/pallas_call | solution.py:258
  18.2 0.4 %collective-permute-start.6 = (bf16[8,72,128]{2,1,0:T(8,128)(2,1)S(1)}, bf16[8,72,128]{2,1,0:T(8,128)(2,1)S(1)}, u32[]{:S(2)}, u32[]{:S(2)}) collective-permute-start(bf16[8,72,128]{2,1,0:T(8,128)(2,1)S(1)} %get-tuple-element.24), channel_id=1, source_target_pairs={{0,1},{1,0},{2,3},{3,2},{4,5},{5,4},{6,7},{7,6},{8,9},{9,8},{10,11... | collective-permute-start | bytes 442376 | tf_op jit(solution)/shard_map/ppermute | solution.py:275
  18.6 1.7 %shard_map.94.refs_0_ = bf16[8,72,128]{2,1,0:T(8,128)(2,1)S(1)} custom-call(bf16[8,72,128]{2,1,0:T(8,128)(2,1)S(1)} %constant_dynamic-update-slice_fusion.refs_1_.refs_0_, f32[64,1024]{1,0:T(8,128)S(1)} %get-tuple-element.23.refs_1_, bf16[8,1024,128]{2,1,0:T(8,128)(2,1)S(1)} %get-tuple-element.18.refs_2_, ...), custom_call_target="tpu_custom_call" | custom-call | flops 1000000000 | bytes 4194304 | tf_op jit(solution)/shard_map/pallas_call | solution.py:258
  20.3 0.3 shard_map.95
  20.7 0.4 %collective-permute-start.7 = (bf16[2,72,128]{2,1,0:T(8,128)(2,1)S(1)}, bf16[2,72,128]{2,1,0:T(8,128)(2,1)S(1)}, u32[]{:S(2)}, u32[]{:S(2)}) collective-permute-start(bf16[2,72,128]{2,1,0:T(8,128)(2,1)S(1)} %get-tuple-element.26), channel_id=1, source_target_pairs={{0,3},{1,2},{2,1},{3,0},{4,7},{5,6},{6,5},{7,4},{8,11},{9,10},{10,... | collective-permute-start | bytes 110600 | tf_op jit(solution)/shard_map/ppermute | solution.py:275
  21.1 1.7 %collective-permute-start.8 = (bf16[2,72,128]{2,1,0:T(8,128)(2,1)S(1)}, bf16[2,72,128]{2,1,0:T(8,128)(2,1)S(1)}, u32[]{:S(2)}, u32[]{:S(2)}) collective-permute-start(bf16[2,72,128]{2,1,0:T(8,128)(2,1)S(1)} %get-tuple-element.27), channel_id=1, source_target_pairs={{0,5},{1,4},{2,7},{3,6},{4,1},{5,0},{6,3},{7,2},{8,13},{9,12},{10,... | collective-permute-start | bytes 110600 | tf_op jit(solution)/shard_map/ppermute | solution.py:275
  22.8 0.9 %collective-permute-start.9 = (bf16[2,72,128]{2,1,0:T(8,128)(2,1)S(1)}, bf16[2,72,128]{2,1,0:T(8,128)(2,1)S(1)}, u32[]{:S(2)}, u32[]{:S(2)}) collective-permute-start(bf16[2,72,128]{2,1,0:T(8,128)(2,1)S(1)} %get-tuple-element.28), channel_id=1, source_target_pairs={{0,7},{1,6},{2,5},{3,4},{4,3},{5,2},{6,1},{7,0},{8,15},{9,14},{10,... | collective-permute-start | bytes 110600 | tf_op jit(solution)/shard_map/ppermute | solution.py:275
  23.8 0.4 %collective-permute-done.7.refs_1_ = bf16[2,72,128]{2,1,0:T(8,128)(2,1)S(1)} collective-permute-done((bf16[2,72,128]{2,1,0:T(8,128)(2,1)S(1)}, bf16[2,72,128]{2,1,0:T(8,128)(2,1)S(1)}, u32[]{:S(2)}, u32[]{:S(2)}) %collective-permute-start.7) | collective-permute-done | bytes 36896 | tf_op jit(solution)/shard_map/ppermute | solution.py:275
  24.1 0.4 %collective-permute-done.8.refs_2_ = bf16[2,72,128]{2,1,0:T(8,128)(2,1)S(1)} collective-permute-done((bf16[2,72,128]{2,1,0:T(8,128)(2,1)S(1)}, bf16[2,72,128]{2,1,0:T(8,128)(2,1)S(1)}, u32[]{:S(2)}, u32[]{:S(2)}) %collective-permute-start.8) | collective-permute-done | bytes 36896 | tf_op jit(solution)/shard_map/ppermute | solution.py:275
  24.5 2.6 %collective-permute-done.9.refs_3_ = bf16[2,72,128]{2,1,0:T(8,128)(2,1)S(1)} collective-permute-done((bf16[2,72,128]{2,1,0:T(8,128)(2,1)S(1)}, bf16[2,72,128]{2,1,0:T(8,128)(2,1)S(1)}, u32[]{:S(2)}, u32[]{:S(2)}) %collective-permute-start.9) | collective-permute-done | bytes 36896 | tf_op jit(solution)/shard_map/ppermute | solution.py:275
  27.1 0.2 shard_map.96
  27.4 3.0 %collective-permute-start.10 = (bf16[1,72,128]{2,1,0:T(8,128)(2,1)S(1)}, bf16[1,72,128]{2,1,0:T(8,128)(2,1)S(1)}, u32[]{:S(2)}, u32[]{:S(2)}) collective-permute-start(bf16[1,72,128]{2,1,0:T(8,128)(2,1)S(1)} %get-tuple-element.30), channel_id=1, source_target_pairs={{0,9},{1,8},{2,11},{3,10},{4,13},{5,12},{6,15},{7,14},{8,1},{9,0},... | collective-permute-start | bytes 55304 | tf_op jit(solution)/shard_map/ppermute | solution.py:275
  30.3 1.6 %collective-permute-done.10.refs_1_ = bf16[1,72,128]{2,1,0:T(8,128)(2,1)S(1)} collective-permute-done((bf16[1,72,128]{2,1,0:T(8,128)(2,1)S(1)}, bf16[1,72,128]{2,1,0:T(8,128)(2,1)S(1)}, u32[]{:S(2)}, u32[]{:S(2)}) %collective-permute-start.10) | collective-permute-done | bytes 18464 | tf_op jit(solution)/shard_map/ppermute | solution.py:275
  32.0 0.8 %shard_map.97 = bf16[1,8192]{1,0:T(2,128)(2,1)} custom-call(bf16[1,72,128]{2,1,0:T(8,128)(2,1)S(1)} %get-tuple-element.29.refs_0_, bf16[1,72,128]{2,1,0:T(8,128)(2,1)S(1)} %collective-permute-done.10.refs_1_), custom_call_target="tpu_custom_call" | custom-call | tf_op jit(solution)/shard_map/pallas_call | solution.py:258
  (25 shorter events, 0.3 us)
Async XLA Ops:
  0.0 14.4 %copy-start.6 = (s32[8]{0:T(128)S(1)}, s32[8]{0:T(128)}, u32[]{:S(2)}) copy-start(s32[8]{0:T(128)} %param.17) | copy-start | bytes 100
  0.0 14.4 %copy-start.1 = (bf16[1024,1024]{1,0:T(8,128)(2,1)S(1)}, bf16[1024,1024]{1,0:T(8,128)(2,1)}, u32[]{:S(2)}) copy-start(bf16[1024,1024]{1,0:T(8,128)(2,1)} %sv_ref.1) | copy-start | bytes 6291460
  0.0 14.4 %copy-start = (bf16[1024,1024]{1,0:T(8,128)(2,1)S(1)}, bf16[1024,1024]{1,0:T(8,128)(2,1)}, u32[]{:S(2)}) copy-start(bf16[1024,1024]{1,0:T(8,128)(2,1)} %sk_ref.1) | copy-start | bytes 6291460
  0.0 14.4 %copy-start.3 = (bf16[1024,1024]{1,0:T(8,128)(2,1)S(1)}, bf16[1024,1024]{1,0:T(8,128)(2,1)}, u32[]{:S(2)}) copy-start(bf16[1024,1024]{1,0:T(8,128)(2,1)} %dv_ref.1) | copy-start | bytes 6291460
  0.0 14.4 %copy-start.2 = (bf16[1024,1024]{1,0:T(8,128)(2,1)S(1)}, bf16[1024,1024]{1,0:T(8,128)(2,1)}, u32[]{:S(2)}) copy-start(bf16[1024,1024]{1,0:T(8,128)(2,1)} %dk_ref.1) | copy-start | bytes 6291460
  0.0 14.4 %copy-start.5 = (bf16[1,1024]{1,0:T(2,128)(2,1)S(1)}, bf16[1,1024]{1,0:T(2,128)(2,1)}, u32[]{:S(2)}) copy-start(bf16[1,1024]{1,0:T(2,128)(2,1)} %nv_ref.1) | copy-start | bytes 6148
  0.0 14.4 %copy-start.4 = (bf16[1,1024]{1,0:T(2,128)(2,1)S(1)}, bf16[1,1024]{1,0:T(2,128)(2,1)}, u32[]{:S(2)}) copy-start(bf16[1,1024]{1,0:T(2,128)(2,1)} %nk_ref.1) | copy-start | bytes 6148
  1.1 5.1 %collective-permute-start = (bf16[1,72,128]{2,1,0:T(8,128)(2,1)S(1)}, bf16[1,72,128]{2,1,0:T(8,128)(2,1)S(1)}, u32[]{:S(2)}, u32[]{:S(2)}) collective-permute-start(bf16[1,72,128]{2,1,0:T(8,128)(2,1)S(1)} %bitcast.3), channel_id=1, source_target_pairs={{0,9},{1,8},{2,11},{3,10},{4,13},{5,12},{6,15},{7,14},{8,1},{9,0},... | collective-permute-start | bytes 55304 | tf_op jit(solution)/shard_map/ppermute | solution.py:275
  6.1 6.8 %collective-permute-start.3 = (bf16[2,72,128]{2,1,0:T(8,128)(2,1)S(1)}, bf16[2,72,128]{2,1,0:T(8,128)(2,1)S(1)}, u32[]{:S(2)}, u32[]{:S(2)}) collective-permute-start(bf16[2,72,128]{2,1,0:T(8,128)(2,1)S(1)} %pad_maximum_fusion), channel_id=1, source_target_pairs={{0,7},{1,6},{2,5},{3,4},{4,3},{5,2},{6,1},{7,0},{8,15},{9,14},{10,... | collective-permute-start | bytes 110600 | tf_op jit(solution)/shard_map/ppermute | solution.py:275
  9.0 3.9 %collective-permute-start.2 = (bf16[2,72,128]{2,1,0:T(8,128)(2,1)S(1)}, bf16[2,72,128]{2,1,0:T(8,128)(2,1)S(1)}, u32[]{:S(2)}, u32[]{:S(2)}) collective-permute-start(bf16[2,72,128]{2,1,0:T(8,128)(2,1)S(1)} %pad_maximum_fusion), channel_id=1, source_target_pairs={{0,5},{1,4},{2,7},{3,6},{4,1},{5,0},{6,3},{7,2},{8,13},{9,12},{10,... | collective-permute-start | bytes 110600 | tf_op jit(solution)/shard_map/ppermute | solution.py:275
  9.4 3.5 %collective-permute-start.1 = (bf16[2,72,128]{2,1,0:T(8,128)(2,1)S(1)}, bf16[2,72,128]{2,1,0:T(8,128)(2,1)S(1)}, u32[]{:S(2)}, u32[]{:S(2)}) collective-permute-start(bf16[2,72,128]{2,1,0:T(8,128)(2,1)S(1)} %pad_maximum_fusion), channel_id=1, source_target_pairs={{0,3},{1,2},{2,1},{3,0},{4,7},{5,6},{6,5},{7,4},{8,11},{9,10},{10,... | collective-permute-start | bytes 110600 | tf_op jit(solution)/shard_map/ppermute | solution.py:275
  12.9 3.6 %collective-permute-start.4 = (bf16[8,72,128]{2,1,0:T(8,128)(2,1)S(1)}, bf16[8,72,128]{2,1,0:T(8,128)(2,1)S(1)}, u32[]{:S(2)}, u32[]{:S(2)}) collective-permute-start(bf16[8,72,128]{2,1,0:T(8,128)(2,1)S(1)} %constant_dynamic-update-slice_fusion.refs_1_.refs_0_), channel_id=1, source_target_pairs={{0,1},{1,0},{2,3},{3,2},{4,5},{5,4},{6,7},{7,6},{8,9},{9,8},{10,11... | collective-permute-start | bytes 442376 | tf_op jit(solution)/shard_map/ppermute | solution.py:275
  13.1 1.3 %collective-permute-start.5 = (bf16[1,72,128]{2,1,0:T(8,128)(2,1)S(1)}, bf16[1,72,128]{2,1,0:T(8,128)(2,1)S(1)}, u32[]{:S(2)}, u32[]{:S(2)}) collective-permute-start(bf16[1,72,128]{2,1,0:T(8,128)(2,1)S(1)} %bitcast.5), channel_id=1, source_target_pairs={{0,1},{1,0},{2,3},{3,2},{4,5},{5,4},{6,7},{7,6},{8,9},{9,8},{10,11... | collective-permute-start | bytes 55304 | tf_op jit(solution)/shard_map/ppermute | solution.py:275
  18.2 2.1 %collective-permute-start.6 = (bf16[8,72,128]{2,1,0:T(8,128)(2,1)S(1)}, bf16[8,72,128]{2,1,0:T(8,128)(2,1)S(1)}, u32[]{:S(2)}, u32[]{:S(2)}) collective-permute-start(bf16[8,72,128]{2,1,0:T(8,128)(2,1)S(1)} %get-tuple-element.24), channel_id=1, source_target_pairs={{0,1},{1,0},{2,3},{3,2},{4,5},{5,4},{6,7},{7,6},{8,9},{9,8},{10,11... | collective-permute-start | bytes 442376 | tf_op jit(solution)/shard_map/ppermute | solution.py:275
  20.7 3.4 %collective-permute-start.7 = (bf16[2,72,128]{2,1,0:T(8,128)(2,1)S(1)}, bf16[2,72,128]{2,1,0:T(8,128)(2,1)S(1)}, u32[]{:S(2)}, u32[]{:S(2)}) collective-permute-start(bf16[2,72,128]{2,1,0:T(8,128)(2,1)S(1)} %get-tuple-element.26), channel_id=1, source_target_pairs={{0,3},{1,2},{2,1},{3,0},{4,7},{5,6},{6,5},{7,4},{8,11},{9,10},{10,... | collective-permute-start | bytes 110600 | tf_op jit(solution)/shard_map/ppermute | solution.py:275
  21.1 3.4 %collective-permute-start.8 = (bf16[2,72,128]{2,1,0:T(8,128)(2,1)S(1)}, bf16[2,72,128]{2,1,0:T(8,128)(2,1)S(1)}, u32[]{:S(2)}, u32[]{:S(2)}) collective-permute-start(bf16[2,72,128]{2,1,0:T(8,128)(2,1)S(1)} %get-tuple-element.27), channel_id=1, source_target_pairs={{0,5},{1,4},{2,7},{3,6},{4,1},{5,0},{6,3},{7,2},{8,13},{9,12},{10,... | collective-permute-start | bytes 110600 | tf_op jit(solution)/shard_map/ppermute | solution.py:275
  22.8 4.3 %collective-permute-start.9 = (bf16[2,72,128]{2,1,0:T(8,128)(2,1)S(1)}, bf16[2,72,128]{2,1,0:T(8,128)(2,1)S(1)}, u32[]{:S(2)}, u32[]{:S(2)}) collective-permute-start(bf16[2,72,128]{2,1,0:T(8,128)(2,1)S(1)} %get-tuple-element.28), channel_id=1, source_target_pairs={{0,7},{1,6},{2,5},{3,4},{4,3},{5,2},{6,1},{7,0},{8,15},{9,14},{10,... | collective-permute-start | bytes 110600 | tf_op jit(solution)/shard_map/ppermute | solution.py:275
  27.4 4.6 %collective-permute-start.10 = (bf16[1,72,128]{2,1,0:T(8,128)(2,1)S(1)}, bf16[1,72,128]{2,1,0:T(8,128)(2,1)S(1)}, u32[]{:S(2)}, u32[]{:S(2)}) collective-permute-start(bf16[1,72,128]{2,1,0:T(8,128)(2,1)S(1)} %get-tuple-element.30), channel_id=1, source_target_pairs={{0,9},{1,8},{2,11},{3,10},{4,13},{5,12},{6,15},{7,14},{8,1},{9,0},... | collective-permute-start | bytes 55304 | tf_op jit(solution)/shard_map/ppermute | solution.py:275

commit v6 on v5

--- a/solution.py
+++ b/solution.py
@@ -130,14 +130,34 @@
     return top, total
 
 
-def attend_kernel(which, flag_rows, *refs):
+def head_queries(ref, slots, head):
+    q = ref[slots, head * GROUPS : (head + 1) * GROUPS, :].astype(jnp.float32)
+    return q.reshape(SLOTS * GROUPS, HD).astype(jnp.bfloat16)
+
+
+def score_kernel(token_ref, dk_ref, score_ref, peak_ref):
+    rows_here = SLOTS * GROUPS
+    lane_ids = lax.broadcasted_iota(jnp.int32, (rows_here, LANES), 1)
+    for head in range(KVH):
+        scores = lane_dot(head_queries(token_ref, pl.ds(0, SLOTS), head), dk_ref[head])
+        score_ref[head] = scores
+        peaks = jnp.full((rows_here, LANES), NEG_BIG, jnp.float32)
+        for b in range(scores.shape[1] // BLOCK):
+            block = scores[:, b * BLOCK : (b + 1) * BLOCK]
+            peaks = jnp.where(lane_ids == b, jnp.max(block, axis=-1, keepdims=True), peaks)
+        peak_ref[head] = peaks
+
+
+def attend_kernel(which, flag_rows, scored, *refs):
     if flag_rows:
         token_ref, other_ref, *refs = refs
+    elif scored:
+        token_ref, score_ref, peak_ref, bias_ref, mark_ref, *refs = refs
     else:
-        token_ref, bias_ref, *refs = refs
+        token_ref, bias_ref, mark_ref, *refs = refs
     dk_ref, dv_ref, top_ref, total_ref, extra_ref, out_ref, *refs = refs
     if flag_rows:
-        (bias_ref,) = refs
+        bias_ref, mark_ref = refs
     tokens = token_ref.shape[0]
     span = dk_ref.shape[1]
     blocks_here = span // BLOCK
@@ -159,6 +179,9 @@
             flags = jnp.sum(jnp.where(row_ids == flag_row, flags, 0.0), axis=1)
             flags = pltpu.roll(flags, LANES - flag_lane, 1)
             bias = jnp.where(flags > 0.5, 0.0, NEG_BIG)
+            mark_ref[here, :] = jnp.broadcast_to(
+                bias[:, None, :], (SLOTS, GROUPS, LANES)
+            ).reshape(rows_here, LANES)
             for b in range(blocks_here):
                 wide = jnp.broadcast_to(bias[:, b : b + 1], (SLOTS, BLOCK))
                 bias_ref[here, b * BLOCK : (b + 1) * BLOCK] = jnp.broadcast_to(
@@ -166,9 +189,18 @@
                 ).reshape(rows_here, BLOCK)
 
         def scores_of(head):
-            rows = slice(head * GROUPS, (head + 1) * GROUPS)
-            q = token_ref[slots, rows, :].astype(jnp.float32).reshape(rows_here, HD)
-            return lane_dot(q.astype(jnp.bfloat16), dk_ref[head]) + bias_ref[here, :]
+            if scored:
+                return None
+            q = head_queries(token_ref, slots, head)
+            return lane_dot(q, dk_ref[head]) + bias_ref[here, :]
+
+        def softmax_of(head, scores):
+            if not scored:
+                return partial_softmax(scores)
+            top = jnp.max(peak_ref[head] + mark_ref[here, :], axis=-1, keepdims=True)
+            shifted = score_ref[head] + bias_ref[here, :] - jnp.maximum(top, NEG_SAFE)
+            weights = jnp.exp2(shifted * EXP2_SCALE)
+            return top, jnp.sum(weights, axis=-1, keepdims=True), weights.astype(jnp.bfloat16)
 
         stats = jnp.zeros((rows_here, LANES), jnp.float32)
         ready = [scores_of(head) for head in range(DOC_AHEAD)]
@@ -177,10 +209,8 @@
             scores = ready.pop(0)
             if head + DOC_AHEAD < KVH:
                 ready.append(scores_of(head + DOC_AHEAD))
-            top, total, weights = partial_softmax(scores)
-            out = jnp.dot(
-                weights, dv_ref[head], preferred_element_type=jnp.float32
-            )
+            top, total, weights = softmax_of(head, scores)
+            out = jnp.dot(weights, dv_ref[head], preferred_element_type=jnp.float32)
             if local:
                 x_top, y_top = top[:GROUPS], top_ref[head, own, 0:1]
                 new_top = jnp.maximum(x_top, y_top)
@@ -338,13 +368,31 @@
     cost = pl.CostEstimate(flops=10**9, bytes_accessed=2 * size, transcendentals=10**6)
     span = doc_keys.shape[0]
     caches = (dk, dv, *local)
-    sent, bias = on_core(
-        functools.partial(attend_kernel, 1, flag_rows),
-        [half, VMEM((devices // 2 * GROUPS, span), jnp.float32)],
+    rows = devices // 2 * GROUPS
+    near_operands = (near,)
+    scored = devices // 2 == SLOTS
+    if scored:
+        near_operands += on_core(
+            score_kernel,
+            (
+                VMEM((KVH, rows, span), jnp.float32),
+                VMEM((KVH, rows, LANES), jnp.float32),
+            ),
+            (near, dk),
+            cost=cost,
+        )
+    sent, bias, mark = on_core(
+        functools.partial(attend_kernel, 1, flag_rows, False),
+        [half, VMEM((rows, span), jnp.float32), VMEM((rows, LANES), jnp.float32)],
         (far, near, *caches),
         cost=cost,
     )
-    kept = on_core(functools.partial(attend_kernel, 0, 0), half, (near, bias, *caches), cost=cost)
+    kept = on_core(
+        functools.partial(attend_kernel, 0, 0, scored),
+        half,
+        (*near_operands, bias, mark, *caches),
+        cost=cost,
+    )
     parts = [kept, sent]
     step = len(stages)
     stages.append((1,))

time: 32.9 us -> 33.4 us (1.015)
  Pallas kernels: 7.91 us -> 8.43 us
    pallas_call x7 -> x8, Pallas kernels: 7.91 us -> 8.43 us  [on_core(): pl.pallas_call(kernel, out_shape=out_shape, in_specs=kwargs.pop('in_specs...]
  transfers between devices with their start and end apart: 11 -> 11, of which waited for: 7 -> 7; matrix products, arithmetic and copies ran while one was open for 0% -> 0% of each run, Pallas kernels for 12% -> 13%
where the time goes in v6:
time: 33.4 us; the launch traced here: 33.3 us
  starting transfers between devices  14 us (42%)
  waiting for transfers between devices  10.6 us (32%)
  Pallas kernels  8.43 us (25%)
    ppermute x11, starting transfers between devices, swap(): return lax.ppermute(x, 'seq', [(i, i ^ bits) for i in range(devices)])  14 us
    ppermute x11, waiting for transfers between devices, swap(): return lax.ppermute(x, 'seq', [(i, i ^ bits) for i in range(devices)])  10.6 us
    pallas_call x8, Pallas kernels, on_core(): pl.pallas_call(kernel, out_shape=out_shape, in_specs=kwargs.pop('in_specs...  8.43 us
  transfers between devices with their start and end apart: 11, of which 7 were waited for; matrix products, arithmetic and copies ran while one was open for 0% of the time, Pallas kernels for 13%

profile of v6, /device:TPU:0, one launch (start us, length us, event | category | flops | bytes accessed | tf_op | source)
XLA Modules:
  0.0 33.3 jit_solution(12550399600354397454)
XLA Ops:
  0.0 1.0 %shard_map.91 = bf16[72,128]{1,0:T(8,128)(2,1)S(1)} custom-call(s32[1,32]{1,0:T(1,128)} %list_ref.1, bf16[1,8192]{1,0:T(2,128)(2,1)} %q_ref.1), custom_call_target="tpu_custom_call" | custom-call | flops 10000000000 | bytes 100000 | tf_op jit(solution)/shard_map/pallas_call | solution.py:288
  1.1 3.6 %collective-permute-start = (bf16[1,72,128]{2,1,0:T(8,128)(2,1)S(1)}, bf16[1,72,128]{2,1,0:T(8,128)(2,1)S(1)}, u32[]{:S(2)}, u32[]{:S(2)}) collective-permute-start(bf16[1,72,128]{2,1,0:T(8,128)(2,1)S(1)} %bitcast.3), channel_id=1, source_target_pairs={{0,9},{1,8},{2,11},{3,10},{4,13},{5,12},{6,15},{7,14},{8,1},{9,0},... | collective-permute-start | bytes 55304 | tf_op jit(solution)/shard_map/ppermute | solution.py:305
  4.7 1.5 %collective-permute-done = bf16[1,72,128]{2,1,0:T(8,128)(2,1)S(1)} collective-permute-done((bf16[1,72,128]{2,1,0:T(8,128)(2,1)S(1)}, bf16[1,72,128]{2,1,0:T(8,128)(2,1)S(1)}, u32[]{:S(2)}, u32[]{:S(2)}) %collective-permute-start) | collective-permute-done | bytes 18464 | tf_op jit(solution)/shard_map/ppermute | solution.py:305
  6.1 2.8 %collective-permute-start.3 = (bf16[2,72,128]{2,1,0:T(8,128)(2,1)S(1)}, bf16[2,72,128]{2,1,0:T(8,128)(2,1)S(1)}, u32[]{:S(2)}, u32[]{:S(2)}) collective-permute-start(bf16[2,72,128]{2,1,0:T(8,128)(2,1)S(1)} %pad_maximum_fusion), channel_id=1, source_target_pairs={{0,7},{1,6},{2,5},{3,4},{4,3},{5,2},{6,1},{7,0},{8,15},{9,14},{10,... | collective-permute-start | bytes 110600 | tf_op jit(solution)/shard_map/ppermute | solution.py:305
  9.0 0.4 %collective-permute-start.2 = (bf16[2,72,128]{2,1,0:T(8,128)(2,1)S(1)}, bf16[2,72,128]{2,1,0:T(8,128)(2,1)S(1)}, u32[]{:S(2)}, u32[]{:S(2)}) collective-permute-start(bf16[2,72,128]{2,1,0:T(8,128)(2,1)S(1)} %pad_maximum_fusion), channel_id=1, source_target_pairs={{0,5},{1,4},{2,7},{3,6},{4,1},{5,0},{6,3},{7,2},{8,13},{9,12},{10,... | collective-permute-start | bytes 110600 | tf_op jit(solution)/shard_map/ppermute | solution.py:305
  9.6 3.3 %collective-permute-done.1 = bf16[2,72,128]{2,1,0:T(8,128)(2,1)S(1)} collective-permute-done((bf16[2,72,128]{2,1,0:T(8,128)(2,1)S(1)}, bf16[2,72,128]{2,1,0:T(8,128)(2,1)S(1)}, u32[]{:S(2)}, u32[]{:S(2)}) %collective-permute-start.1) | collective-permute-done | bytes 36896 | tf_op jit(solution)/shard_map/ppermute | solution.py:305
  13.1 0.4 %collective-permute-start.4 = (bf16[1,72,128]{2,1,0:T(8,128)(2,1)S(1)}, bf16[1,72,128]{2,1,0:T(8,128)(2,1)S(1)}, u32[]{:S(2)}, u32[]{:S(2)}) collective-permute-start(bf16[1,72,128]{2,1,0:T(8,128)(2,1)S(1)} %bitcast.5), channel_id=1, source_target_pairs={{0,1},{1,0},{2,3},{3,2},{4,5},{5,4},{6,7},{7,6},{8,9},{9,8},{10,11... | collective-permute-start | bytes 55304 | tf_op jit(solution)/shard_map/ppermute | solution.py:305
  13.5 0.9 %collective-permute-done.4.pair_ref = bf16[1,72,128]{2,1,0:T(8,128)(2,1)S(1)} collective-permute-done((bf16[1,72,128]{2,1,0:T(8,128)(2,1)S(1)}, bf16[1,72,128]{2,1,0:T(8,128)(2,1)S(1)}, u32[]{:S(2)}, u32[]{:S(2)}) %collective-permute-start.4) | collective-permute-done | bytes 18464 | tf_op jit(solution)/shard_map/ppermute | solution.py:305
  14.5 2.1 %shard_map.92 = (f32[8,16,128]{2,1,0:T(8,128)S(1)}, f32[8,16,128]{2,1,0:T(8,128)S(1)}, f32[8,16,128]{2,1,0:T(8,128)S(1)}, bf16[8,1024,128]{2,1,0:T(8,128)(2,1)S(1)}, bf16[8,1024,128]{2,1,0:T(8,128)(2,1)S(1)}) custom-call(s32[1,8]{1,0:T(1,128)S(1)} %bitcast.7, bf16[1,72,128]{2,1,0:T(8,128)(2,1)S(1)} %bitcast.6, ...), custom_call_target="tpu_custom_call" | custom-call | flops 1000000000 | bytes 6291456 | tf_op jit(solution)/shard_map/pallas_call | solution.py:288
  16.6 1.7 %shard_map.94 = (bf16[8,72,128]{2,1,0:T(8,128)(2,1)S(1)}, f32[64,1024]{1,0:T(8,128)S(1)}, f32[64,128]{1,0:T(8,128)S(1)}) custom-call(bf16[8,72,128]{2,1,0:T(8,128)(2,1)S(1)} %collective-permute-done.5.refs_0_, bf16[8,72,128]{2,1,0:T(8,128)(2,1)S(1)} %constant_dynamic-update-slice_fusion.token_ref.refs_1_.refs_0_, ...), custom_call_target="tpu_custom_call" | custom-call | flops 1000000000 | bytes 4194304 | tf_op jit(solution)/shard_map/pallas_call | solution.py:288
  18.3 0.4 %collective-permute-start.6 = (bf16[8,72,128]{2,1,0:T(8,128)(2,1)S(1)}, bf16[8,72,128]{2,1,0:T(8,128)(2,1)S(1)}, u32[]{:S(2)}, u32[]{:S(2)}) collective-permute-start(bf16[8,72,128]{2,1,0:T(8,128)(2,1)S(1)} %get-tuple-element.30), channel_id=1, source_target_pairs={{0,1},{1,0},{2,3},{3,2},{4,5},{5,4},{6,7},{7,6},{8,9},{9,8},{10,11... | collective-permute-start | bytes 442376 | tf_op jit(solution)/shard_map/ppermute | solution.py:305
  18.6 0.9 %shard_map.93 = (f32[8,64,1024]{2,1,0:T(8,128)S(1)}, f32[8,64,128]{2,1,0:T(8,128)S(1)}) custom-call(bf16[8,72,128]{2,1,0:T(8,128)(2,1)S(1)} %constant_dynamic-update-slice_fusion.token_ref.refs_1_.refs_0_, bf16[8,1024,128]{2,1,0:T(8,128)(2,1)S(1)} %get-tuple-element.21.dk_ref.refs_2_.refs_5_), custom_call_target="tpu_custom_call" | custom-call | flops 1000000000 | bytes 4194304 | tf_op jit(solution)/shard_map/pallas_call | solution.py:288
  19.6 1.3 %shard_map.95.refs_0_ = bf16[8,72,128]{2,1,0:T(8,128)(2,1)S(1)} custom-call(bf16[8,72,128]{2,1,0:T(8,128)(2,1)S(1)} %constant_dynamic-update-slice_fusion.token_ref.refs_1_.refs_0_, f32[8,64,1024]{2,1,0:T(8,128)S(1)} %get-tuple-element.22.refs_1_, f32[8,64,128]{2,1,0:T(8,128)S(1)} %get-tuple-element.23.refs_2_, f32[64,1024]{1,0:T(8,128)S(1)} %get-tuple-element.28.refs_3_, ...), custom_call_target="tpu_custom_call" | custom-call | flops 1000000000 | bytes 4194304 | tf_op jit(solution)/shard_map/pallas_call | solution.py:288
  20.9 0.3 shard_map.96
  21.2 0.4 %collective-permute-start.7 = (bf16[2,72,128]{2,1,0:T(8,128)(2,1)S(1)}, bf16[2,72,128]{2,1,0:T(8,128)(2,1)S(1)}, u32[]{:S(2)}, u32[]{:S(2)}) collective-permute-start(bf16[2,72,128]{2,1,0:T(8,128)(2,1)S(1)} %get-tuple-element.32), channel_id=1, source_target_pairs={{0,3},{1,2},{2,1},{3,0},{4,7},{5,6},{6,5},{7,4},{8,11},{9,10},{10,... | collective-permute-start | bytes 110600 | tf_op jit(solution)/shard_map/ppermute | solution.py:305
  21.6 1.8 %collective-permute-start.8 = (bf16[2,72,128]{2,1,0:T(8,128)(2,1)S(1)}, bf16[2,72,128]{2,1,0:T(8,128)(2,1)S(1)}, u32[]{:S(2)}, u32[]{:S(2)}) collective-permute-start(bf16[2,72,128]{2,1,0:T(8,128)(2,1)S(1)} %get-tuple-element.33), channel_id=1, source_target_pairs={{0,5},{1,4},{2,7},{3,6},{4,1},{5,0},{6,3},{7,2},{8,13},{9,12},{10,... | collective-permute-start | bytes 110600 | tf_op jit(solution)/shard_map/ppermute | solution.py:305
  23.4 0.9 %collective-permute-start.9 = (bf16[2,72,128]{2,1,0:T(8,128)(2,1)S(1)}, bf16[2,72,128]{2,1,0:T(8,128)(2,1)S(1)}, u32[]{:S(2)}, u32[]{:S(2)}) collective-permute-start(bf16[2,72,128]{2,1,0:T(8,128)(2,1)S(1)} %get-tuple-element.34), channel_id=1, source_target_pairs={{0,7},{1,6},{2,5},{3,4},{4,3},{5,2},{6,1},{7,0},{8,15},{9,14},{10,... | collective-permute-start | bytes 110600 | tf_op jit(solution)/shard_map/ppermute | solution.py:305
  24.3 0.4 %collective-permute-done.7.refs_1_ = bf16[2,72,128]{2,1,0:T(8,128)(2,1)S(1)} collective-permute-done((bf16[2,72,128]{2,1,0:T(8,128)(2,1)S(1)}, bf16[2,72,128]{2,1,0:T(8,128)(2,1)S(1)}, u32[]{:S(2)}, u32[]{:S(2)}) %collective-permute-start.7) | collective-permute-done | bytes 36896 | tf_op jit(solution)/shard_map/ppermute | solution.py:305
  24.7 0.4 %collective-permute-done.8.refs_2_ = bf16[2,72,128]{2,1,0:T(8,128)(2,1)S(1)} collective-permute-done((bf16[2,72,128]{2,1,0:T(8,128)(2,1)S(1)}, bf16[2,72,128]{2,1,0:T(8,128)(2,1)S(1)}, u32[]{:S(2)}, u32[]{:S(2)}) %collective-permute-start.8) | collective-permute-done | bytes 36896 | tf_op jit(solution)/shard_map/ppermute | solution.py:305
  25.0 2.6 %collective-permute-done.9.refs_3_ = bf16[2,72,128]{2,1,0:T(8,128)(2,1)S(1)} collective-permute-done((bf16[2,72,128]{2,1,0:T(8,128)(2,1)S(1)}, bf16[2,72,128]{2,1,0:T(8,128)(2,1)S(1)}, u32[]{:S(2)}, u32[]{:S(2)}) %collective-permute-start.9) | collective-permute-done | bytes 36896 | tf_op jit(solution)/shard_map/ppermute | solution.py:305
  27.6 0.2 shard_map.97
  27.9 3.0 %collective-permute-start.10 = (bf16[1,72,128]{2,1,0:T(8,128)(2,1)S(1)}, bf16[1,72,128]{2,1,0:T(8,128)(2,1)S(1)}, u32[]{:S(2)}, u32[]{:S(2)}) collective-permute-start(bf16[1,72,128]{2,1,0:T(8,128)(2,1)S(1)} %get-tuple-element.36), channel_id=1, source_target_pairs={{0,9},{1,8},{2,11},{3,10},{4,13},{5,12},{6,15},{7,14},{8,1},{9,0},... | collective-permute-start | bytes 55304 | tf_op jit(solution)/shard_map/ppermute | solution.py:305
  30.9 1.6 %collective-permute-done.10.refs_1_ = bf16[1,72,128]{2,1,0:T(8,128)(2,1)S(1)} collective-permute-done((bf16[1,72,128]{2,1,0:T(8,128)(2,1)S(1)}, bf16[1,72,128]{2,1,0:T(8,128)(2,1)S(1)}, u32[]{:S(2)}, u32[]{:S(2)}) %collective-permute-start.10) | collective-permute-done | bytes 18464 | tf_op jit(solution)/shard_map/ppermute | solution.py:305
  32.5 0.8 %shard_map.98 = bf16[1,8192]{1,0:T(2,128)(2,1)} custom-call(bf16[1,72,128]{2,1,0:T(8,128)(2,1)S(1)} %get-tuple-element.35.refs_0_, bf16[1,72,128]{2,1,0:T(8,128)(2,1)S(1)} %collective-permute-done.10.refs_1_), custom_call_target="tpu_custom_call" | custom-call | tf_op jit(solution)/shard_map/pallas_call | solution.py:288
  (26 shorter events, 0.5 us)
Async XLA Ops:
  0.0 14.4 %copy-start.6 = (s32[8]{0:T(128)S(1)}, s32[8]{0:T(128)}, u32[]{:S(2)}) copy-start(s32[8]{0:T(128)} %param.17) | copy-start | bytes 100
  0.0 14.4 %copy-start.1 = (bf16[1024,1024]{1,0:T(8,128)(2,1)S(1)}, bf16[1024,1024]{1,0:T(8,128)(2,1)}, u32[]{:S(2)}) copy-start(bf16[1024,1024]{1,0:T(8,128)(2,1)} %sv_ref.1) | copy-start | bytes 6291460
  0.0 14.4 %copy-start = (bf16[1024,1024]{1,0:T(8,128)(2,1)S(1)}, bf16[1024,1024]{1,0:T(8,128)(2,1)}, u32[]{:S(2)}) copy-start(bf16[1024,1024]{1,0:T(8,128)(2,1)} %sk_ref.1) | copy-start | bytes 6291460
  0.0 14.4 %copy-start.3 = (bf16[1024,1024]{1,0:T(8,128)(2,1)S(1)}, bf16[1024,1024]{1,0:T(8,128)(2,1)}, u32[]{:S(2)}) copy-start(bf16[1024,1024]{1,0:T(8,128)(2,1)} %dv_ref.1) | copy-start | bytes 6291460
  0.0 14.4 %copy-start.2 = (bf16[1024,1024]{1,0:T(8,128)(2,1)S(1)}, bf16[1024,1024]{1,0:T(8,128)(2,1)}, u32[]{:S(2)}) copy-start(bf16[1024,1024]{1,0:T(8,128)(2,1)} %dk_ref.1) | copy-start | bytes 6291460
  0.0 14.4 %copy-start.5 = (bf16[1,1024]{1,0:T(2,128)(2,1)S(1)}, bf16[1,1024]{1,0:T(2,128)(2,1)}, u32[]{:S(2)}) copy-start(bf16[1,1024]{1,0:T(2,128)(2,1)} %nv_ref.1) | copy-start | bytes 6148
  0.0 14.4 %copy-start.4 = (bf16[1,1024]{1,0:T(2,128)(2,1)S(1)}, bf16[1,1024]{1,0:T(2,128)(2,1)}, u32[]{:S(2)}) copy-start(bf16[1,1024]{1,0:T(2,128)(2,1)} %nk_ref.1) | copy-start | bytes 6148
  1.1 5.1 %collective-permute-start = (bf16[1,72,128]{2,1,0:T(8,128)(2,1)S(1)}, bf16[1,72,128]{2,1,0:T(8,128)(2,1)S(1)}, u32[]{:S(2)}, u32[]{:S(2)}) collective-permute-start(bf16[1,72,128]{2,1,0:T(8,128)(2,1)S(1)} %bitcast.3), channel_id=1, source_target_pairs={{0,9},{1,8},{2,11},{3,10},{4,13},{5,12},{6,15},{7,14},{8,1},{9,0},... | collective-permute-start | bytes 55304 | tf_op jit(solution)/shard_map/ppermute | solution.py:305
  6.1 6.8 %collective-permute-start.3 = (bf16[2,72,128]{2,1,0:T(8,128)(2,1)S(1)}, bf16[2,72,128]{2,1,0:T(8,128)(2,1)S(1)}, u32[]{:S(2)}, u32[]{:S(2)}) collective-permute-start(bf16[2,72,128]{2,1,0:T(8,128)(2,1)S(1)} %pad_maximum_fusion), channel_id=1, source_target_pairs={{0,7},{1,6},{2,5},{3,4},{4,3},{5,2},{6,1},{7,0},{8,15},{9,14},{10,... | collective-permute-start | bytes 110600 | tf_op jit(solution)/shard_map/ppermute | solution.py:305
  9.0 3.9 %collective-permute-start.2 = (bf16[2,72,128]{2,1,0:T(8,128)(2,1)S(1)}, bf16[2,72,128]{2,1,0:T(8,128)(2,1)S(1)}, u32[]{:S(2)}, u32[]{:S(2)}) collective-permute-start(bf16[2,72,128]{2,1,0:T(8,128)(2,1)S(1)} %pad_maximum_fusion), channel_id=1, source_target_pairs={{0,5},{1,4},{2,7},{3,6},{4,1},{5,0},{6,3},{7,2},{8,13},{9,12},{10,... | collective-permute-start | bytes 110600 | tf_op jit(solution)/shard_map/ppermute | solution.py:305
  9.4 3.5 %collective-permute-start.1 = (bf16[2,72,128]{2,1,0:T(8,128)(2,1)S(1)}, bf16[2,72,128]{2,1,0:T(8,128)(2,1)S(1)}, u32[]{:S(2)}, u32[]{:S(2)}) collective-permute-start(bf16[2,72,128]{2,1,0:T(8,128)(2,1)S(1)} %pad_maximum_fusion), channel_id=1, source_target_pairs={{0,3},{1,2},{2,1},{3,0},{4,7},{5,6},{6,5},{7,4},{8,11},{9,10},{10,... | collective-permute-start | bytes 110600 | tf_op jit(solution)/shard_map/ppermute | solution.py:305
  12.9 3.6 %collective-permute-start.5 = (bf16[8,72,128]{2,1,0:T(8,128)(2,1)S(1)}, bf16[8,72,128]{2,1,0:T(8,128)(2,1)S(1)}, u32[]{:S(2)}, u32[]{:S(2)}) collective-permute-start(bf16[8,72,128]{2,1,0:T(8,128)(2,1)S(1)} %constant_dynamic-update-slice_fusion.token_ref.refs_1_.refs_0_), channel_id=1, source_target_pairs={{0,1},{1,0},{2,3},{3,2},{4,5},{5,4},{6,7},{7,6},{8,9},{9,8},{10,11... | collective-permute-start | bytes 442376 | tf_op jit(solution)/shard_map/ppermute | solution.py:305
  13.1 1.3 %collective-permute-start.4 = (bf16[1,72,128]{2,1,0:T(8,128)(2,1)S(1)}, bf16[1,72,128]{2,1,0:T(8,128)(2,1)S(1)}, u32[]{:S(2)}, u32[]{:S(2)}) collective-permute-start(bf16[1,72,128]{2,1,0:T(8,128)(2,1)S(1)} %bitcast.5), channel_id=1, source_target_pairs={{0,1},{1,0},{2,3},{3,2},{4,5},{5,4},{6,7},{7,6},{8,9},{9,8},{10,11... | collective-permute-start | bytes 55304 | tf_op jit(solution)/shard_map/ppermute | solution.py:305
  18.3 2.6 %collective-permute-start.6 = (bf16[8,72,128]{2,1,0:T(8,128)(2,1)S(1)}, bf16[8,72,128]{2,1,0:T(8,128)(2,1)S(1)}, u32[]{:S(2)}, u32[]{:S(2)}) collective-permute-start(bf16[8,72,128]{2,1,0:T(8,128)(2,1)S(1)} %get-tuple-element.30), channel_id=1, source_target_pairs={{0,1},{1,0},{2,3},{3,2},{4,5},{5,4},{6,7},{7,6},{8,9},{9,8},{10,11... | collective-permute-start | bytes 442376 | tf_op jit(solution)/shard_map/ppermute | solution.py:305
  21.2 3.4 %collective-permute-start.7 = (bf16[2,72,128]{2,1,0:T(8,128)(2,1)S(1)}, bf16[2,72,128]{2,1,0:T(8,128)(2,1)S(1)}, u32[]{:S(2)}, u32[]{:S(2)}) collective-permute-start(bf16[2,72,128]{2,1,0:T(8,128)(2,1)S(1)} %get-tuple-element.32), channel_id=1, source_target_pairs={{0,3},{1,2},{2,1},{3,0},{4,7},{5,6},{6,5},{7,4},{8,11},{9,10},{10,... | collective-permute-start | bytes 110600 | tf_op jit(solution)/shard_map/ppermute | solution.py:305
  21.6 3.4 %collective-permute-start.8 = (bf16[2,72,128]{2,1,0:T(8,128)(2,1)S(1)}, bf16[2,72,128]{2,1,0:T(8,128)(2,1)S(1)}, u32[]{:S(2)}, u32[]{:S(2)}) collective-permute-start(bf16[2,72,128]{2,1,0:T(8,128)(2,1)S(1)} %get-tuple-element.33), channel_id=1, source_target_pairs={{0,5},{1,4},{2,7},{3,6},{4,1},{5,0},{6,3},{7,2},{8,13},{9,12},{10,... | collective-permute-start | bytes 110600 | tf_op jit(solution)/shard_map/ppermute | solution.py:305
  23.4 4.3 %collective-permute-start.9 = (bf16[2,72,128]{2,1,0:T(8,128)(2,1)S(1)}, bf16[2,72,128]{2,1,0:T(8,128)(2,1)S(1)}, u32[]{:S(2)}, u32[]{:S(2)}) collective-permute-start(bf16[2,72,128]{2,1,0:T(8,128)(2,1)S(1)} %get-tuple-element.34), channel_id=1, source_target_pairs={{0,7},{1,6},{2,5},{3,4},{4,3},{5,2},{6,1},{7,0},{8,15},{9,14},{10,... | collective-permute-start | bytes 110600 | tf_op jit(solution)/shard_map/ppermute | solution.py:305
  27.9 4.6 %collective-permute-start.10 = (bf16[1,72,128]{2,1,0:T(8,128)(2,1)S(1)}, bf16[1,72,128]{2,1,0:T(8,128)(2,1)S(1)}, u32[]{:S(2)}, u32[]{:S(2)}) collective-permute-start(bf16[1,72,128]{2,1,0:T(8,128)(2,1)S(1)} %get-tuple-element.36), channel_id=1, source_target_pairs={{0,9},{1,8},{2,11},{3,10},{4,13},{5,12},{6,15},{7,14},{8,1},{9,0},... | collective-permute-start | bytes 55304 | tf_op jit(solution)/shard_map/ppermute | solution.py:305

commit v7 on v6

--- a/solution.py
+++ b/solution.py
@@ -20,7 +20,7 @@
 NEG_BIG = -1e30
 NEG_SAFE = -5e29
 AHEAD = 4
-DOC_AHEAD = 2
+DOC_AHEAD = 3
 EXP2_SCALE = HD**-0.5 * math.log2(math.e)
 
 VMEM = pltpu.VMEM
@@ -46,12 +46,6 @@
 
 def lane_dot(a, b):
     return lax.dot_general(a, b, (((1,), (1,)), ((), ())), preferred_element_type=jnp.float32)
-
-
-def partial_softmax(scores):
-    top = jnp.max(scores, axis=-1, keepdims=True)
-    weights = jnp.exp2((scores - jnp.maximum(top, NEG_SAFE)) * EXP2_SCALE)
-    return top, jnp.sum(weights, axis=-1, keepdims=True), weights.astype(jnp.bfloat16)
 
 
 def suffix_kernel(
@@ -195,12 +189,20 @@
             return lane_dot(q, dk_ref[head]) + bias_ref[here, :]
 
         def softmax_of(head, scores):
-            if not scored:
-                return partial_softmax(scores)
-            top = jnp.max(peak_ref[head] + mark_ref[here, :], axis=-1, keepdims=True)
-            shifted = score_ref[head] + bias_ref[here, :] - jnp.maximum(top, NEG_SAFE)
-            weights = jnp.exp2(shifted * EXP2_SCALE)
-            return top, jnp.sum(weights, axis=-1, keepdims=True), weights.astype(jnp.bfloat16)
+            if scored:
+                peaks = peak_ref[head] + mark_ref[here, :]
+                scores = score_ref[head] + bias_ref[here, :]
+                blocks = [scores[:, b * LANES : (b + 1) * LANES] for b in range(span // LANES)]
+            else:
+                blocks = [scores[:, b * LANES : (b + 1) * LANES] for b in range(span // LANES)]
+                peaks = functools.reduce(jnp.maximum, blocks)
+            top = jnp.broadcast_to(jnp.max(peaks, axis=-1, keepdims=True), (rows_here, LANES))
+            base = jnp.maximum(top, NEG_SAFE)
+            weights = [jnp.exp2((block - base) * EXP2_SCALE) for block in blocks]
+            total = jnp.sum(functools.reduce(jnp.add, weights), axis=-1, keepdims=True)
+            total = jnp.broadcast_to(total, (rows_here, LANES))
+            weights = jnp.concatenate([w.astype(jnp.bfloat16) for w in weights], axis=1)
+            return top, total, weights
 
         stats = jnp.zeros((rows_here, LANES), jnp.float32)
         ready = [scores_of(head) for head in range(DOC_AHEAD)]
@@ -212,12 +214,12 @@
             top, total, weights = softmax_of(head, scores)
             out = jnp.dot(weights, dv_ref[head], preferred_element_type=jnp.float32)
             if local:
-                x_top, y_top = top[:GROUPS], top_ref[head, own, 0:1]
+                x_top, y_top = top[:GROUPS], top_ref[head, own, :]
                 new_top = jnp.maximum(x_top, y_top)
                 base = jnp.maximum(new_top, NEG_SAFE)
                 x_scale = jnp.exp2((x_top - base) * EXP2_SCALE)
                 y_scale = jnp.exp2((y_top - base) * EXP2_SCALE)
-                new_total = x_scale * total[:GROUPS] + y_scale * total_ref[head, own, 0:1]
+                new_total = x_scale * total[:GROUPS] + y_scale * total_ref[head, own, :]
                 new_out = x_scale * out[:GROUPS] + y_scale * extra_ref[head, own, :]
                 top = jnp.concatenate([new_top, top[GROUPS:]], axis=0)
                 total = jnp.concatenate([new_total, total[GROUPS:]], axis=0)

time: 33.4 us -> 32.6 us (0.976)
  Pallas kernels: 8.43 us -> 7.79 us
    pallas_call x8, Pallas kernels: 8.43 us -> 7.79 us  [on_core(): pl.pallas_call(kernel, out_shape=out_shape, in_specs=kwargs.pop('in_specs...]
  transfers between devices with their start and end apart: 11 -> 11, of which waited for: 7 -> 7; matrix products, arithmetic and copies ran while one was open for 0% -> 0% of each run, Pallas kernels for 13% -> 12%
where the time goes in v7:
time: 32.6 us; the launch traced here: 32.5 us
  starting transfers between devices  14 us (43%)
  waiting for transfers between devices  10.5 us (32%)
  Pallas kernels  7.79 us (24%)
    ppermute x11, starting transfers between devices, swap(): return lax.ppermute(x, 'seq', [(i, i ^ bits) for i in range(devices)])  14 us
    ppermute x11, waiting for transfers between devices, swap(): return lax.ppermute(x, 'seq', [(i, i ^ bits) for i in range(devices)])  10.5 us
    pallas_call x8, Pallas kernels, on_core(): pl.pallas_call(kernel, out_shape=out_shape, in_specs=kwargs.pop('in_specs...  7.79 us
  transfers between devices with their start and end apart: 11, of which 7 were waited for; matrix products, arithmetic and copies ran while one was open for 0% of the time, Pallas kernels for 12%

profile of v7, /device:TPU:0, one launch (start us, length us, event | category | flops | bytes accessed | tf_op | source)
XLA Modules:
  0.0 32.5 jit_solution(8317012012246856968)
XLA Ops:
  0.0 1.0 %shard_map.91 = bf16[72,128]{1,0:T(8,128)(2,1)S(1)} custom-call(s32[1,32]{1,0:T(1,128)} %list_ref.1, bf16[1,8192]{1,0:T(2,128)(2,1)} %q_ref.1), custom_call_target="tpu_custom_call" | custom-call | flops 10000000000 | bytes 100000 | tf_op jit(solution)/shard_map/pallas_call | solution.py:290
  1.1 3.6 %collective-permute-start = (bf16[1,72,128]{2,1,0:T(8,128)(2,1)S(1)}, bf16[1,72,128]{2,1,0:T(8,128)(2,1)S(1)}, u32[]{:S(2)}, u32[]{:S(2)}) collective-permute-start(bf16[1,72,128]{2,1,0:T(8,128)(2,1)S(1)} %bitcast.3), channel_id=1, source_target_pairs={{0,9},{1,8},{2,11},{3,10},{4,13},{5,12},{6,15},{7,14},{8,1},{9,0},... | collective-permute-start | bytes 55304 | tf_op jit(solution)/shard_map/ppermute | solution.py:307
  4.7 1.5 %collective-permute-done = bf16[1,72,128]{2,1,0:T(8,128)(2,1)S(1)} collective-permute-done((bf16[1,72,128]{2,1,0:T(8,128)(2,1)S(1)}, bf16[1,72,128]{2,1,0:T(8,128)(2,1)S(1)}, u32[]{:S(2)}, u32[]{:S(2)}) %collective-permute-start) | collective-permute-done | bytes 18464 | tf_op jit(solution)/shard_map/ppermute | solution.py:307
  6.1 2.8 %collective-permute-start.3 = (bf16[2,72,128]{2,1,0:T(8,128)(2,1)S(1)}, bf16[2,72,128]{2,1,0:T(8,128)(2,1)S(1)}, u32[]{:S(2)}, u32[]{:S(2)}) collective-permute-start(bf16[2,72,128]{2,1,0:T(8,128)(2,1)S(1)} %pad_maximum_fusion), channel_id=1, source_target_pairs={{0,7},{1,6},{2,5},{3,4},{4,3},{5,2},{6,1},{7,0},{8,15},{9,14},{10,... | collective-permute-start | bytes 110600 | tf_op jit(solution)/shard_map/ppermute | solution.py:307
  9.0 0.4 %collective-permute-start.2 = (bf16[2,72,128]{2,1,0:T(8,128)(2,1)S(1)}, bf16[2,72,128]{2,1,0:T(8,128)(2,1)S(1)}, u32[]{:S(2)}, u32[]{:S(2)}) collective-permute-start(bf16[2,72,128]{2,1,0:T(8,128)(2,1)S(1)} %pad_maximum_fusion), channel_id=1, source_target_pairs={{0,5},{1,4},{2,7},{3,6},{4,1},{5,0},{6,3},{7,2},{8,13},{9,12},{10,... | collective-permute-start | bytes 110600 | tf_op jit(solution)/shard_map/ppermute | solution.py:307
  9.6 3.3 %collective-permute-done.1 = bf16[2,72,128]{2,1,0:T(8,128)(2,1)S(1)} collective-permute-done((bf16[2,72,128]{2,1,0:T(8,128)(2,1)S(1)}, bf16[2,72,128]{2,1,0:T(8,128)(2,1)S(1)}, u32[]{:S(2)}, u32[]{:S(2)}) %collective-permute-start.1) | collective-permute-done | bytes 36896 | tf_op jit(solution)/shard_map/ppermute | solution.py:307
  13.1 0.4 %collective-permute-start.4 = (bf16[1,72,128]{2,1,0:T(8,128)(2,1)S(1)}, bf16[1,72,128]{2,1,0:T(8,128)(2,1)S(1)}, u32[]{:S(2)}, u32[]{:S(2)}) collective-permute-start(bf16[1,72,128]{2,1,0:T(8,128)(2,1)S(1)} %bitcast.5), channel_id=1, source_target_pairs={{0,1},{1,0},{2,3},{3,2},{4,5},{5,4},{6,7},{7,6},{8,9},{9,8},{10,11... | collective-permute-start | bytes 55304 | tf_op jit(solution)/shard_map/ppermute | solution.py:307
  13.5 0.9 %collective-permute-done.4.pair_ref = bf16[1,72,128]{2,1,0:T(8,128)(2,1)S(1)} collective-permute-done((bf16[1,72,128]{2,1,0:T(8,128)(2,1)S(1)}, bf16[1,72,128]{2,1,0:T(8,128)(2,1)S(1)}, u32[]{:S(2)}, u32[]{:S(2)}) %collective-permute-start.4) | collective-permute-done | bytes 18464 | tf_op jit(solution)/shard_map/ppermute | solution.py:307
  14.5 2.1 %shard_map.92 = (f32[8,16,128]{2,1,0:T(8,128)S(1)}, f32[8,16,128]{2,1,0:T(8,128)S(1)}, f32[8,16,128]{2,1,0:T(8,128)S(1)}, bf16[8,1024,128]{2,1,0:T(8,128)(2,1)S(1)}, bf16[8,1024,128]{2,1,0:T(8,128)(2,1)S(1)}) custom-call(s32[1,8]{1,0:T(1,128)S(1)} %bitcast.7, bf16[1,72,128]{2,1,0:T(8,128)(2,1)S(1)} %bitcast.6, ...), custom_call_target="tpu_custom_call" | custom-call | flops 1000000000 | bytes 6291456 | tf_op jit(solution)/shard_map/pallas_call | solution.py:290
  16.6 1.5 %shard_map.94 = (bf16[8,72,128]{2,1,0:T(8,128)(2,1)S(1)}, f32[64,1024]{1,0:T(8,128)S(1)}, f32[64,128]{1,0:T(8,128)S(1)}) custom-call(bf16[8,72,128]{2,1,0:T(8,128)(2,1)S(1)} %collective-permute-done.5.refs_0_, bf16[8,72,128]{2,1,0:T(8,128)(2,1)S(1)} %constant_dynamic-update-slice_fusion.token_ref.refs_1_.refs_0_, ...), custom_call_target="tpu_custom_call" | custom-call | flops 1000000000 | bytes 4194304 | tf_op jit(solution)/shard_map/pallas_call | solution.py:290
  18.0 0.4 %collective-permute-start.6 = (bf16[8,72,128]{2,1,0:T(8,128)(2,1)S(1)}, bf16[8,72,128]{2,1,0:T(8,128)(2,1)S(1)}, u32[]{:S(2)}, u32[]{:S(2)}) collective-permute-start(bf16[8,72,128]{2,1,0:T(8,128)(2,1)S(1)} %get-tuple-element.30), channel_id=1, source_target_pairs={{0,1},{1,0},{2,3},{3,2},{4,5},{5,4},{6,7},{7,6},{8,9},{9,8},{10,11... | collective-permute-start | bytes 442376 | tf_op jit(solution)/shard_map/ppermute | solution.py:307
  18.4 0.9 %shard_map.93 = (f32[8,64,1024]{2,1,0:T(8,128)S(1)}, f32[8,64,128]{2,1,0:T(8,128)S(1)}) custom-call(bf16[8,72,128]{2,1,0:T(8,128)(2,1)S(1)} %constant_dynamic-update-slice_fusion.token_ref.refs_1_.refs_0_, bf16[8,1024,128]{2,1,0:T(8,128)(2,1)S(1)} %get-tuple-element.21.dk_ref.refs_2_.refs_5_), custom_call_target="tpu_custom_call" | custom-call | flops 1000000000 | bytes 4194304 | tf_op jit(solution)/shard_map/pallas_call | solution.py:290
  19.4 0.9 %shard_map.95.refs_0_ = bf16[8,72,128]{2,1,0:T(8,128)(2,1)S(1)} custom-call(bf16[8,72,128]{2,1,0:T(8,128)(2,1)S(1)} %constant_dynamic-update-slice_fusion.token_ref.refs_1_.refs_0_, f32[8,64,1024]{2,1,0:T(8,128)S(1)} %get-tuple-element.22.refs_1_, f32[8,64,128]{2,1,0:T(8,128)S(1)} %get-tuple-element.23.refs_2_, f32[64,1024]{1,0:T(8,128)S(1)} %get-tuple-element.28.refs_3_, ...), custom_call_target="tpu_custom_call" | custom-call | flops 1000000000 | bytes 4194304 | tf_op jit(solution)/shard_map/pallas_call | solution.py:290
  20.2 0.3 %shard_map.96 = (bf16[2,72,128]{2,1,0:T(8,128)(2,1)S(1)}, bf16[2,72,128]{2,1,0:T(8,128)(2,1)S(1)}, bf16[2,72,128]{2,1,0:T(8,128)(2,1)S(1)}, bf16[2,72,128]{2,1,0:T(8,128)(2,1)S(1)}) custom-call(bf16[8,72,128]{2,1,0:T(8,128)(2,1)S(1)} %shard_map.95.refs_0_, bf16[8,72,128]{2,1,0:T(8,128)(2,1)S(1)} %collective-permute-done.6.refs_1_), custom_call_target="tpu_custom_call" | custom-call | tf_op jit(solution)/shard_map/pallas_call | solution.py:290
  20.6 0.4 %collective-permute-start.7 = (bf16[2,72,128]{2,1,0:T(8,128)(2,1)S(1)}, bf16[2,72,128]{2,1,0:T(8,128)(2,1)S(1)}, u32[]{:S(2)}, u32[]{:S(2)}) collective-permute-start(bf16[2,72,128]{2,1,0:T(8,128)(2,1)S(1)} %get-tuple-element.32), channel_id=1, source_target_pairs={{0,3},{1,2},{2,1},{3,0},{4,7},{5,6},{6,5},{7,4},{8,11},{9,10},{10,... | collective-permute-start | bytes 110600 | tf_op jit(solution)/shard_map/ppermute | solution.py:307
  21.0 1.8 %collective-permute-start.8 = (bf16[2,72,128]{2,1,0:T(8,128)(2,1)S(1)}, bf16[2,72,128]{2,1,0:T(8,128)(2,1)S(1)}, u32[]{:S(2)}, u32[]{:S(2)}) collective-permute-start(bf16[2,72,128]{2,1,0:T(8,128)(2,1)S(1)} %get-tuple-element.33), channel_id=1, source_target_pairs={{0,5},{1,4},{2,7},{3,6},{4,1},{5,0},{6,3},{7,2},{8,13},{9,12},{10,... | collective-permute-start | bytes 110600 | tf_op jit(solution)/shard_map/ppermute | solution.py:307
  22.7 0.9 %collective-permute-start.9 = (bf16[2,72,128]{2,1,0:T(8,128)(2,1)S(1)}, bf16[2,72,128]{2,1,0:T(8,128)(2,1)S(1)}, u32[]{:S(2)}, u32[]{:S(2)}) collective-permute-start(bf16[2,72,128]{2,1,0:T(8,128)(2,1)S(1)} %get-tuple-element.34), channel_id=1, source_target_pairs={{0,7},{1,6},{2,5},{3,4},{4,3},{5,2},{6,1},{7,0},{8,15},{9,14},{10,... | collective-permute-start | bytes 110600 | tf_op jit(solution)/shard_map/ppermute | solution.py:307
  23.6 0.4 %collective-permute-done.7.refs_1_ = bf16[2,72,128]{2,1,0:T(8,128)(2,1)S(1)} collective-permute-done((bf16[2,72,128]{2,1,0:T(8,128)(2,1)S(1)}, bf16[2,72,128]{2,1,0:T(8,128)(2,1)S(1)}, u32[]{:S(2)}, u32[]{:S(2)}) %collective-permute-start.7) | collective-permute-done | bytes 36896 | tf_op jit(solution)/shard_map/ppermute | solution.py:307
  24.0 0.3 %collective-permute-done.8.refs_2_ = bf16[2,72,128]{2,1,0:T(8,128)(2,1)S(1)} collective-permute-done((bf16[2,72,128]{2,1,0:T(8,128)(2,1)S(1)}, bf16[2,72,128]{2,1,0:T(8,128)(2,1)S(1)}, u32[]{:S(2)}, u32[]{:S(2)}) %collective-permute-start.8) | collective-permute-done | bytes 36896 | tf_op jit(solution)/shard_map/ppermute | solution.py:307
  24.4 2.6 %collective-permute-done.9.refs_3_ = bf16[2,72,128]{2,1,0:T(8,128)(2,1)S(1)} collective-permute-done((bf16[2,72,128]{2,1,0:T(8,128)(2,1)S(1)}, bf16[2,72,128]{2,1,0:T(8,128)(2,1)S(1)}, u32[]{:S(2)}, u32[]{:S(2)}) %collective-permute-start.9) | collective-permute-done | bytes 36896 | tf_op jit(solution)/shard_map/ppermute | solution.py:307
  27.0 0.2 shard_map.97
  27.3 2.9 %collective-permute-start.10 = (bf16[1,72,128]{2,1,0:T(8,128)(2,1)S(1)}, bf16[1,72,128]{2,1,0:T(8,128)(2,1)S(1)}, u32[]{:S(2)}, u32[]{:S(2)}) collective-permute-start(bf16[1,72,128]{2,1,0:T(8,128)(2,1)S(1)} %get-tuple-element.36), channel_id=1, source_target_pairs={{0,9},{1,8},{2,11},{3,10},{4,13},{5,12},{6,15},{7,14},{8,1},{9,0},... | collective-permute-start | bytes 55304 | tf_op jit(solution)/shard_map/ppermute | solution.py:307
  30.2 1.5 %collective-permute-done.10.refs_1_ = bf16[1,72,128]{2,1,0:T(8,128)(2,1)S(1)} collective-permute-done((bf16[1,72,128]{2,1,0:T(8,128)(2,1)S(1)}, bf16[1,72,128]{2,1,0:T(8,128)(2,1)S(1)}, u32[]{:S(2)}, u32[]{:S(2)}) %collective-permute-start.10) | collective-permute-done | bytes 18464 | tf_op jit(solution)/shard_map/ppermute | solution.py:307
  31.7 0.8 %shard_map.98 = bf16[1,8192]{1,0:T(2,128)(2,1)} custom-call(bf16[1,72,128]{2,1,0:T(8,128)(2,1)S(1)} %get-tuple-element.35.refs_0_, bf16[1,72,128]{2,1,0:T(8,128)(2,1)S(1)} %collective-permute-done.10.refs_1_), custom_call_target="tpu_custom_call" | custom-call | tf_op jit(solution)/shard_map/pallas_call | solution.py:290
  (26 shorter events, 0.5 us)
Async XLA Ops:
  0.0 14.4 %copy-start.6 = (s32[8]{0:T(128)S(1)}, s32[8]{0:T(128)}, u32[]{:S(2)}) copy-start(s32[8]{0:T(128)} %param.17) | copy-start | bytes 100
  0.0 14.4 %copy-start.1 = (bf16[1024,1024]{1,0:T(8,128)(2,1)S(1)}, bf16[1024,1024]{1,0:T(8,128)(2,1)}, u32[]{:S(2)}) copy-start(bf16[1024,1024]{1,0:T(8,128)(2,1)} %sv_ref.1) | copy-start | bytes 6291460
  0.0 14.4 %copy-start = (bf16[1024,1024]{1,0:T(8,128)(2,1)S(1)}, bf16[1024,1024]{1,0:T(8,128)(2,1)}, u32[]{:S(2)}) copy-start(bf16[1024,1024]{1,0:T(8,128)(2,1)} %sk_ref.1) | copy-start | bytes 6291460
  0.0 14.4 %copy-start.3 = (bf16[1024,1024]{1,0:T(8,128)(2,1)S(1)}, bf16[1024,1024]{1,0:T(8,128)(2,1)}, u32[]{:S(2)}) copy-start(bf16[1024,1024]{1,0:T(8,128)(2,1)} %dv_ref.1) | copy-start | bytes 6291460
  0.0 14.4 %copy-start.2 = (bf16[1024,1024]{1,0:T(8,128)(2,1)S(1)}, bf16[1024,1024]{1,0:T(8,128)(2,1)}, u32[]{:S(2)}) copy-start(bf16[1024,1024]{1,0:T(8,128)(2,1)} %dk_ref.1) | copy-start | bytes 6291460
  0.0 14.4 %copy-start.5 = (bf16[1,1024]{1,0:T(2,128)(2,1)S(1)}, bf16[1,1024]{1,0:T(2,128)(2,1)}, u32[]{:S(2)}) copy-start(bf16[1,1024]{1,0:T(2,128)(2,1)} %nv_ref.1) | copy-start | bytes 6148
  0.0 14.4 %copy-start.4 = (bf16[1,1024]{1,0:T(2,128)(2,1)S(1)}, bf16[1,1024]{1,0:T(2,128)(2,1)}, u32[]{:S(2)}) copy-start(bf16[1,1024]{1,0:T(2,128)(2,1)} %nk_ref.1) | copy-start | bytes 6148
  1.1 5.1 %collective-permute-start = (bf16[1,72,128]{2,1,0:T(8,128)(2,1)S(1)}, bf16[1,72,128]{2,1,0:T(8,128)(2,1)S(1)}, u32[]{:S(2)}, u32[]{:S(2)}) collective-permute-start(bf16[1,72,128]{2,1,0:T(8,128)(2,1)S(1)} %bitcast.3), channel_id=1, source_target_pairs={{0,9},{1,8},{2,11},{3,10},{4,13},{5,12},{6,15},{7,14},{8,1},{9,0},... | collective-permute-start | bytes 55304 | tf_op jit(solution)/shard_map/ppermute | solution.py:307
  6.1 6.8 %collective-permute-start.3 = (bf16[2,72,128]{2,1,0:T(8,128)(2,1)S(1)}, bf16[2,72,128]{2,1,0:T(8,128)(2,1)S(1)}, u32[]{:S(2)}, u32[]{:S(2)}) collective-permute-start(bf16[2,72,128]{2,1,0:T(8,128)(2,1)S(1)} %pad_maximum_fusion), channel_id=1, source_target_pairs={{0,7},{1,6},{2,5},{3,4},{4,3},{5,2},{6,1},{7,0},{8,15},{9,14},{10,... | collective-permute-start | bytes 110600 | tf_op jit(solution)/shard_map/ppermute | solution.py:307
  9.0 3.9 %collective-permute-start.2 = (bf16[2,72,128]{2,1,0:T(8,128)(2,1)S(1)}, bf16[2,72,128]{2,1,0:T(8,128)(2,1)S(1)}, u32[]{:S(2)}, u32[]{:S(2)}) collective-permute-start(bf16[2,72,128]{2,1,0:T(8,128)(2,1)S(1)} %pad_maximum_fusion), channel_id=1, source_target_pairs={{0,5},{1,4},{2,7},{3,6},{4,1},{5,0},{6,3},{7,2},{8,13},{9,12},{10,... | collective-permute-start | bytes 110600 | tf_op jit(solution)/shard_map/ppermute | solution.py:307
  9.4 3.5 %collective-permute-start.1 = (bf16[2,72,128]{2,1,0:T(8,128)(2,1)S(1)}, bf16[2,72,128]{2,1,0:T(8,128)(2,1)S(1)}, u32[]{:S(2)}, u32[]{:S(2)}) collective-permute-start(bf16[2,72,128]{2,1,0:T(8,128)(2,1)S(1)} %pad_maximum_fusion), channel_id=1, source_target_pairs={{0,3},{1,2},{2,1},{3,0},{4,7},{5,6},{6,5},{7,4},{8,11},{9,10},{10,... | collective-permute-start | bytes 110600 | tf_op jit(solution)/shard_map/ppermute | solution.py:307
  12.9 3.6 %collective-permute-start.5 = (bf16[8,72,128]{2,1,0:T(8,128)(2,1)S(1)}, bf16[8,72,128]{2,1,0:T(8,128)(2,1)S(1)}, u32[]{:S(2)}, u32[]{:S(2)}) collective-permute-start(bf16[8,72,128]{2,1,0:T(8,128)(2,1)S(1)} %constant_dynamic-update-slice_fusion.token_ref.refs_1_.refs_0_), channel_id=1, source_target_pairs={{0,1},{1,0},{2,3},{3,2},{4,5},{5,4},{6,7},{7,6},{8,9},{9,8},{10,11... | collective-permute-start | bytes 442376 | tf_op jit(solution)/shard_map/ppermute | solution.py:307
  13.1 1.3 %collective-permute-start.4 = (bf16[1,72,128]{2,1,0:T(8,128)(2,1)S(1)}, bf16[1,72,128]{2,1,0:T(8,128)(2,1)S(1)}, u32[]{:S(2)}, u32[]{:S(2)}) collective-permute-start(bf16[1,72,128]{2,1,0:T(8,128)(2,1)S(1)} %bitcast.5), channel_id=1, source_target_pairs={{0,1},{1,0},{2,3},{3,2},{4,5},{5,4},{6,7},{7,6},{8,9},{9,8},{10,11... | collective-permute-start | bytes 55304 | tf_op jit(solution)/shard_map/ppermute | solution.py:307
  18.0 2.2 %collective-permute-start.6 = (bf16[8,72,128]{2,1,0:T(8,128)(2,1)S(1)}, bf16[8,72,128]{2,1,0:T(8,128)(2,1)S(1)}, u32[]{:S(2)}, u32[]{:S(2)}) collective-permute-start(bf16[8,72,128]{2,1,0:T(8,128)(2,1)S(1)} %get-tuple-element.30), channel_id=1, source_target_pairs={{0,1},{1,0},{2,3},{3,2},{4,5},{5,4},{6,7},{7,6},{8,9},{9,8},{10,11... | collective-permute-start | bytes 442376 | tf_op jit(solution)/shard_map/ppermute | solution.py:307
  20.6 3.5 %collective-permute-start.7 = (bf16[2,72,128]{2,1,0:T(8,128)(2,1)S(1)}, bf16[2,72,128]{2,1,0:T(8,128)(2,1)S(1)}, u32[]{:S(2)}, u32[]{:S(2)}) collective-permute-start(bf16[2,72,128]{2,1,0:T(8,128)(2,1)S(1)} %get-tuple-element.32), channel_id=1, source_target_pairs={{0,3},{1,2},{2,1},{3,0},{4,7},{5,6},{6,5},{7,4},{8,11},{9,10},{10,... | collective-permute-start | bytes 110600 | tf_op jit(solution)/shard_map/ppermute | solution.py:307
  21.0 3.4 %collective-permute-start.8 = (bf16[2,72,128]{2,1,0:T(8,128)(2,1)S(1)}, bf16[2,72,128]{2,1,0:T(8,128)(2,1)S(1)}, u32[]{:S(2)}, u32[]{:S(2)}) collective-permute-start(bf16[2,72,128]{2,1,0:T(8,128)(2,1)S(1)} %get-tuple-element.33), channel_id=1, source_target_pairs={{0,5},{1,4},{2,7},{3,6},{4,1},{5,0},{6,3},{7,2},{8,13},{9,12},{10,... | collective-permute-start | bytes 110600 | tf_op jit(solution)/shard_map/ppermute | solution.py:307
  22.7 4.3 %collective-permute-start.9 = (bf16[2,72,128]{2,1,0:T(8,128)(2,1)S(1)}, bf16[2,72,128]{2,1,0:T(8,128)(2,1)S(1)}, u32[]{:S(2)}, u32[]{:S(2)}) collective-permute-start(bf16[2,72,128]{2,1,0:T(8,128)(2,1)S(1)} %get-tuple-element.34), channel_id=1, source_target_pairs={{0,7},{1,6},{2,5},{3,4},{4,3},{5,2},{6,1},{7,0},{8,15},{9,14},{10,... | collective-permute-start | bytes 110600 | tf_op jit(solution)/shard_map/ppermute | solution.py:307
  27.3 4.4 %collective-permute-start.10 = (bf16[1,72,128]{2,1,0:T(8,128)(2,1)S(1)}, bf16[1,72,128]{2,1,0:T(8,128)(2,1)S(1)}, u32[]{:S(2)}, u32[]{:S(2)}) collective-permute-start(bf16[1,72,128]{2,1,0:T(8,128)(2,1)S(1)} %get-tuple-element.36), channel_id=1, source_target_pairs={{0,9},{1,8},{2,11},{3,10},{4,13},{5,12},{6,15},{7,14},{8,1},{9,0},... | collective-permute-start | bytes 55304 | tf_op jit(solution)/shard_map/ppermute | solution.py:307

commit v8 on v7

--- a/solution.py
+++ b/solution.py
@@ -58,9 +58,8 @@
     nv_ref,
     dk_ref,
     dv_ref,
-    top_ref,
-    total_ref,
-    out_ref,
+    own_out_ref,
+    pair_out_ref,
     dk_out_ref,
     dv_out_ref,
 ):
@@ -99,9 +98,12 @@
         out = jnp.dot(
             weights.astype(jnp.bfloat16), sv_ref[:, cols], preferred_element_type=jnp.float32
         )
-        top_ref[head] = jnp.broadcast_to(top, (2 * GROUPS, LANES))
-        total_ref[head] = jnp.broadcast_to(total, (2 * GROUPS, LANES))
-        out_ref[head] = out + n_scale * nv_ref[:, cols].astype(jnp.float32)
+        out = out + n_scale * nv_ref[:, cols].astype(jnp.float32)
+        for i, target in enumerate((own_out_ref, pair_out_ref)):
+            mine = slice(i * GROUPS, (i + 1) * GROUPS)
+            target[head, 0:GROUPS] = jnp.broadcast_to(top[mine], (GROUPS, LANES))
+            target[head, GROUPS : 2 * GROUPS] = jnp.broadcast_to(total[mine], (GROUPS, LANES))
+            target[head, 2 * GROUPS :] = out[mine]
         dk_out_ref[head] = dk_ref[:, cols]
         dv_out_ref[head] = dv_ref[:, cols]
 
@@ -142,99 +144,130 @@
         peak_ref[head] = peaks
 
 
-def attend_kernel(which, flag_rows, scored, *refs):
-    if flag_rows:
-        token_ref, other_ref, *refs = refs
-    elif scored:
-        token_ref, score_ref, peak_ref, bias_ref, mark_ref, *refs = refs
-    else:
-        token_ref, bias_ref, mark_ref, *refs = refs
-    dk_ref, dv_ref, top_ref, total_ref, extra_ref, out_ref, *refs = refs
-    if flag_rows:
-        bias_ref, mark_ref = refs
-    tokens = token_ref.shape[0]
-    span = dk_ref.shape[1]
+def attend_kernel(flag_rows, scored, pieces, *refs):
+    near_ref, other_ref, *refs = refs
+    if scored:
+        score_ref, peak_ref, *refs = refs
+    dk_ref, dv_ref, far_dk_ref, far_dv_ref, own_ref, theirs_ref, *refs = refs
+    out_refs, (bias_ref,) = refs[:pieces], refs[pieces:]
+    span = far_dk_ref.shape[0]
     blocks_here = span // BLOCK
     rows_here = SLOTS * GROUPS
-    first_block = lax.axis_index("seq") * blocks_here
-    flag_row = lax.div(first_block, LANES)
-    flag_lane = lax.rem(first_block, LANES)
+    me = lax.axis_index("seq")
+    flag_row = lax.div(me * blocks_here, LANES)
+    row_ids = lax.broadcasted_iota(jnp.int32, (1, flag_rows, LANES), 1)
     lane_ids = lax.broadcasted_iota(jnp.int32, (rows_here, LANES), 1)
-    own = slice(which * GROUPS, (which + 1) * GROUPS)
-
-    def do_chunk(chunk, local):
+
+    def tall(x):
+        wide = jnp.broadcast_to(x[:, None, :], (SLOTS, GROUPS, LANES))
+        return wide.reshape(rows_here, LANES)
+
+    def do_chunk(chunk, local, put):
         slots = pl.ds(chunk * SLOTS, SLOTS)
-        here = pl.ds(chunk * rows_here, rows_here)
-        if flag_rows:
-            flags = token_ref[slots, HEADS:, :].astype(jnp.float32) + other_ref[
-                slots, HEADS:, :
-            ].astype(jnp.float32)
-            row_ids = lax.broadcasted_iota(jnp.int32, (1, flag_rows, LANES), 1)
-            flags = jnp.sum(jnp.where(row_ids == flag_row, flags, 0.0), axis=1)
-            flags = pltpu.roll(flags, LANES - flag_lane, 1)
-            bias = jnp.where(flags > 0.5, 0.0, NEG_BIG)
-            mark_ref[here, :] = jnp.broadcast_to(
-                bias[:, None, :], (SLOTS, GROUPS, LANES)
-            ).reshape(rows_here, LANES)
+        flags = near_ref[slots, HEADS:, :].astype(jnp.float32)
+        flags = flags + other_ref[slots].astype(jnp.float32)
+        flags = jnp.sum(jnp.where(row_ids == flag_row, flags, 0.0), axis=1)
+        marks = []
+        for i, device in enumerate((me, me ^ 1)):
+            lane = lax.rem(device * blocks_here, LANES)
+            bias = jnp.where(pltpu.roll(flags, LANES - lane, 1) > 0.5, 0.0, NEG_BIG)
+            marks.append(bias)
             for b in range(blocks_here):
-                wide = jnp.broadcast_to(bias[:, b : b + 1], (SLOTS, BLOCK))
-                bias_ref[here, b * BLOCK : (b + 1) * BLOCK] = jnp.broadcast_to(
-                    wide[:, None, :], (SLOTS, GROUPS, BLOCK)
-                ).reshape(rows_here, BLOCK)
+                wide = jnp.broadcast_to(bias[:, b : b + 1], (SLOTS, LANES))
+                at = i * span + b * BLOCK
+                bias_ref[:, at : at + BLOCK] = tall(wide)
+        mark = tall(marks[0])
+
+        def blocks_of(scores):
+            return [scores[:, b * LANES : (b + 1) * LANES] for b in range(span // LANES)]
 
         def scores_of(head):
+            q = head_queries(near_ref, slots, head)
+            cols = slice(head * HD, (head + 1) * HD)
+            far = lane_dot(q, far_dk_ref[:, cols]) + bias_ref[:, span:]
             if scored:
-                return None
-            q = head_queries(token_ref, slots, head)
-            return lane_dot(q, dk_ref[head]) + bias_ref[here, :]
+                return blocks_of(far)
+            return blocks_of(far), blocks_of(lane_dot(q, dk_ref[head]) + bias_ref[:, :span])
 
         def softmax_of(head, scores):
             if scored:
-                peaks = peak_ref[head] + mark_ref[here, :]
-                scores = score_ref[head] + bias_ref[here, :]
-                blocks = [scores[:, b * LANES : (b + 1) * LANES] for b in range(span // LANES)]
+                far = scores
+                near = blocks_of(score_ref[head] + bias_ref[:, :span])
+                peaks = functools.reduce(jnp.maximum, far, peak_ref[head] + mark)
             else:
-                blocks = [scores[:, b * LANES : (b + 1) * LANES] for b in range(span // LANES)]
-                peaks = functools.reduce(jnp.maximum, blocks)
+                far, near = scores
+                peaks = functools.reduce(jnp.maximum, far + near)
             top = jnp.broadcast_to(jnp.max(peaks, axis=-1, keepdims=True), (rows_here, LANES))
             base = jnp.maximum(top, NEG_SAFE)
-            weights = [jnp.exp2((block - base) * EXP2_SCALE) for block in blocks]
-            total = jnp.sum(functools.reduce(jnp.add, weights), axis=-1, keepdims=True)
-            total = jnp.broadcast_to(total, (rows_here, LANES))
-            weights = jnp.concatenate([w.astype(jnp.bfloat16) for w in weights], axis=1)
-            return top, total, weights
+            weights = [
+                [jnp.exp2((block - base) * EXP2_SCALE) for block in blocks]
+                for blocks in (near, far)
+            ]
+            total = functools.reduce(jnp.add, weights[0] + weights[1])
+            total = jnp.broadcast_to(
+                jnp.sum(total, axis=-1, keepdims=True), (rows_here, LANES)
+            )
+            near, far = [
+                jnp.concatenate([w.astype(jnp.bfloat16) for w in ws], axis=1) for ws in weights
+            ]
+            return top, total, near, far
 
         stats = jnp.zeros((rows_here, LANES), jnp.float32)
         ready = [scores_of(head) for head in range(DOC_AHEAD)]
         for head in range(KVH):
-            rows = slice(head * GROUPS, (head + 1) * GROUPS)
+            cols = slice(head * HD, (head + 1) * HD)
             scores = ready.pop(0)
             if head + DOC_AHEAD < KVH:
                 ready.append(scores_of(head + DOC_AHEAD))
-            top, total, weights = softmax_of(head, scores)
-            out = jnp.dot(weights, dv_ref[head], preferred_element_type=jnp.float32)
+            top, total, near, far = softmax_of(head, scores)
+            out = jnp.dot(near, dv_ref[head], preferred_element_type=jnp.float32)
+            out = out + jnp.dot(far, far_dv_ref[:, cols], preferred_element_type=jnp.float32)
             if local:
-                x_top, y_top = top[:GROUPS], top_ref[head, own, :]
-                new_top = jnp.maximum(x_top, y_top)
+                terms = [(top[:GROUPS], total[:GROUPS], out[:GROUPS])]
+                for ref in (own_ref, theirs_ref):
+                    terms.append(
+                        tuple(ref[head, i * GROUPS : (i + 1) * GROUPS] for i in range(3))
+                    )
+                new_top = functools.reduce(jnp.maximum, [t for t, _, _ in terms])
                 base = jnp.maximum(new_top, NEG_SAFE)
-                x_scale = jnp.exp2((x_top - base) * EXP2_SCALE)
-                y_scale = jnp.exp2((y_top - base) * EXP2_SCALE)
-                new_total = x_scale * total[:GROUPS] + y_scale * total_ref[head, own, :]
-                new_out = x_scale * out[:GROUPS] + y_scale * extra_ref[head, own, :]
+                scales = [jnp.exp2((t - base) * EXP2_SCALE) for t, _, _ in terms]
+                new_total = sum(s * l for s, (_, l, _) in zip(scales, terms))
+                new_out = sum(s * o for s, (_, _, o) in zip(scales, terms))
                 top = jnp.concatenate([new_top, top[GROUPS:]], axis=0)
                 total = jnp.concatenate([new_total, total[GROUPS:]], axis=0)
                 out = jnp.concatenate([new_out, out[GROUPS:]], axis=0)
             units = (out / jnp.maximum(total, 1.0)).astype(jnp.bfloat16)
             stats = jnp.where(lane_ids == head, top * EXP2_SCALE, stats)
             stats = jnp.where(lane_ids == KVH + head, total, stats)
-            out_ref[slots, rows, :] = units.reshape(SLOTS, GROUPS, HD)
-        rows = slice(HEADS, HEADS + GROUPS)
-        out_ref[slots, rows, :] = split_stats(stats, 1).reshape(SLOTS, GROUPS, LANES)
-
-    do_chunk(0, True)
-    chunks = tokens // SLOTS
-    if chunks > 1:
-        lax.fori_loop(1, chunks, lambda c, _: do_chunk(c, False), None)
+            put(head * GROUPS, units.reshape(SLOTS, GROUPS, HD))
+        put(HEADS, split_stats(stats, 1).reshape(SLOTS, GROUPS, LANES))
+
+    size = out_refs[0].shape[0]
+    if size < SLOTS:
+
+        def put(row, value):
+            for i, ref in enumerate(out_refs):
+                ref[:, row : row + GROUPS, :] = value[i * size : (i + 1) * size]
+
+        do_chunk(0, True, put)
+        return
+    steps = size // SLOTS
+    for i, ref in enumerate(out_refs):
+
+        def put_at(step):
+            def put(row, value):
+                ref[pl.ds(step * SLOTS, SLOTS), row : row + GROUPS, :] = value
+
+            return put
+
+        if i == 0:
+            do_chunk(0, True, put_at(0))
+        lax.fori_loop(
+            1 if i == 0 else 0,
+            steps,
+            lambda step, _: do_chunk(i * steps + step, False, put_at(step)),
+            None,
+        )
 
 
 def mix_weights(refs):
@@ -340,11 +373,12 @@
     heads_of = lambda x: VMEM((KVH, x.shape[0], HD), x.dtype)
     size = 2 * suffix_keys.size
     pair = swap(own, 1)
-    stat = VMEM((KVH, 2 * GROUPS, LANES), jnp.float32)
-    *local, dk, dv = on_core(
+    far_dk = swap(doc_keys, 1)
+    far_dv = swap(doc_values, 1)
+    partial = VMEM((KVH, 3 * GROUPS, LANES), jnp.float32)
+    local, pair_local, dk, dv = on_core(
         suffix_kernel,
-        [stat, stat, VMEM((KVH, 2 * GROUPS, HD), jnp.float32)]
-        + [heads_of(doc_keys), heads_of(doc_values)],
+        [partial, partial, heads_of(doc_keys), heads_of(doc_values)],
         (
             near_core(suffix_lengths[None]),
             own,
@@ -363,18 +397,17 @@
         for bits in stage:
             arrived.append(swap(near, bits))
         near = jnp.concatenate([near] + arrived, axis=0)
-    far = swap(near, 1)
+    other = swap(near[:, HEADS:, :], 1)
+    near = near_core(near)
+    theirs = swap(pair_local, 1)
     tokens = lambda count: VMEM((count, HEADS + GROUPS, HD), jnp.bfloat16)
-    near, far = near_core(near), near_core(far)
-    half = tokens(devices // 2)
     cost = pl.CostEstimate(flops=10**9, bytes_accessed=2 * size, transcendentals=10**6)
     span = doc_keys.shape[0]
-    caches = (dk, dv, *local)
     rows = devices // 2 * GROUPS
-    near_operands = (near,)
     scored = devices // 2 == SLOTS
+    scores = ()
     if scored:
-        near_operands += on_core(
+        scores = on_core(
             score_kernel,
             (
                 VMEM((KVH, rows, span), jnp.float32),
@@ -383,21 +416,25 @@
             (near, dk),
             cost=cost,
         )
-    sent, bias, mark = on_core(
-        functools.partial(attend_kernel, 1, flag_rows, False),
-        [half, VMEM((rows, span), jnp.float32), VMEM((rows, LANES), jnp.float32)],
-        (far, near, *caches),
+    pieces = len(stages[-1]) + 1
+    parts = on_core(
+        functools.partial(attend_kernel, flag_rows, scored, pieces),
+        [tokens(devices // 2 // pieces)] * pieces,
+        (
+            near,
+            near_core(other),
+            *scores,
+            dk,
+            dv,
+            near_core(far_dk),
+            near_core(far_dv),
+            local,
+            near_core(theirs),
+        ),
+        scratch_shapes=[VMEM((SLOTS * GROUPS, 2 * span), jnp.float32)],
         cost=cost,
     )
-    kept = on_core(
-        functools.partial(attend_kernel, 0, 0, scored),
-        half,
-        (*near_operands, bias, mark, *caches),
-        cost=cost,
-    )
-    parts = [kept, sent]
-    step = len(stages)
-    stages.append((1,))
+    step = len(stages) - 1
     while stages:
         stage = stages.pop()
         sources = [parts[0]]

time: 32.6 us -> 29.9 us (0.917)
  waiting for transfers between devices: 10.5 us -> 7.43 us
    ppermute x11 -> x13, waiting for transfers between devices: 10.5 us -> 7.43 us  [swap(): return lax.ppermute(x, 'seq', [(i, i ^ bits) for i in range(devices)])]
    pallas_call x8 -> x6, Pallas kernels: 7.79 us -> 7.97 us  [on_core(): pl.pallas_call(kernel, out_shape=out_shape, in_specs=kwargs.pop('in_specs...]
    ppermute x11 -> x13, starting transfers between devices: 14 us -> 14.2 us  [swap(): return lax.ppermute(x, 'seq', [(i, i ^ bits) for i in range(devices)])]
  transfers between devices with their start and end apart: 11 -> 13, of which waited for: 7 -> 6; matrix products, arithmetic and copies ran while one was open for 0% -> 0% of each run, Pallas kernels for 12% -> 14%
where the time goes in v8:
time: 29.9 us; the launch traced here: 29.8 us
  starting transfers between devices  14.2 us (47%)
  Pallas kernels  7.97 us (27%)
  waiting for transfers between devices  7.43 us (25%)
    ppermute x13, starting transfers between devices, swap(): return lax.ppermute(x, 'seq', [(i, i ^ bits) for i in range(devices)])  14.2 us
    pallas_call x6, Pallas kernels, on_core(): pl.pallas_call(kernel, out_shape=out_shape, in_specs=kwargs.pop('in_specs...  7.97 us
    ppermute x13, waiting for transfers between devices, swap(): return lax.ppermute(x, 'seq', [(i, i ^ bits) for i in range(devices)])  7.43 us
  transfers between devices with their start and end apart: 13, of which 6 were waited for; matrix products, arithmetic and copies ran while one was open for 0% of the time, Pallas kernels for 14%

profile of v8, /device:TPU:0, one launch (start us, length us, event | category | flops | bytes accessed | tf_op | source)
XLA Modules:
  0.0 29.8 jit_solution(17952040572507279300)
XLA Ops:
  0.0 0.6 %collective-permute-start.6 = (bf16[1024,1024]{1,0:T(8,128)(2,1)}, bf16[1024,1024]{1,0:T(8,128)(2,1)S(1)}, u32[]{:S(2)}, u32[]{:S(2)}) collective-permute-start(bf16[1024,1024]{1,0:T(8,128)(2,1)} %dk_ref.1), channel_id=1, source_target_pairs={{0,1},{1,0},{2,3},{3,2},{4,5},{5,4},{6,7},{7,6},{8,9},{9,8},{10,11... | collective-permute-start | bytes 6291464 | tf_op jit(solution)/shard_map/ppermute | solution.py:340
  0.7 1.2 %shard_map.91 = bf16[72,128]{1,0:T(8,128)(2,1)S(1)} custom-call(s32[1,32]{1,0:T(1,128)} %list_ref.1, bf16[1,8192]{1,0:T(2,128)(2,1)} %q_ref.1), custom_call_target="tpu_custom_call" | custom-call | flops 10000000000 | bytes 100000 | tf_op jit(solution)/shard_map/pallas_call | solution.py:323
  1.9 0.5 %collective-permute-start.5 = (bf16[1,72,128]{2,1,0:T(8,128)(2,1)S(1)}, bf16[1,72,128]{2,1,0:T(8,128)(2,1)S(1)}, u32[]{:S(2)}, u32[]{:S(2)}) collective-permute-start(bf16[1,72,128]{2,1,0:T(8,128)(2,1)S(1)} %bitcast.3), channel_id=1, source_target_pairs={{0,1},{1,0},{2,3},{3,2},{4,5},{5,4},{6,7},{7,6},{8,9},{9,8},{10,11... | collective-permute-start | bytes 55304 | tf_op jit(solution)/shard_map/ppermute | solution.py:340
  2.4 3.7 %collective-permute-start = (bf16[1,72,128]{2,1,0:T(8,128)(2,1)S(1)}, bf16[1,72,128]{2,1,0:T(8,128)(2,1)S(1)}, u32[]{:S(2)}, u32[]{:S(2)}) collective-permute-start(bf16[1,72,128]{2,1,0:T(8,128)(2,1)S(1)} %bitcast.4), channel_id=1, source_target_pairs={{0,9},{1,8},{2,11},{3,10},{4,13},{5,12},{6,15},{7,14},{8,1},{9,0},... | collective-permute-start | bytes 55304 | tf_op jit(solution)/shard_map/ppermute | solution.py:340
  6.1 1.5 %collective-permute-done = bf16[1,72,128]{2,1,0:T(8,128)(2,1)S(1)} collective-permute-done((bf16[1,72,128]{2,1,0:T(8,128)(2,1)S(1)}, bf16[1,72,128]{2,1,0:T(8,128)(2,1)S(1)}, u32[]{:S(2)}, u32[]{:S(2)}) %collective-permute-start) | collective-permute-done | bytes 18464 | tf_op jit(solution)/shard_map/ppermute | solution.py:340
  7.5 2.5 %collective-permute-start.3 = (bf16[2,72,128]{2,1,0:T(8,128)(2,1)S(1)}, bf16[2,72,128]{2,1,0:T(8,128)(2,1)S(1)}, u32[]{:S(2)}, u32[]{:S(2)}) collective-permute-start(bf16[2,72,128]{2,1,0:T(8,128)(2,1)S(1)} %pad_maximum_fusion), channel_id=1, source_target_pairs={{0,7},{1,6},{2,5},{3,4},{4,3},{5,2},{6,1},{7,0},{8,15},{9,14},{10,... | collective-permute-start | bytes 110600 | tf_op jit(solution)/shard_map/ppermute | solution.py:340
  10.1 0.3 collective-permute-start.2
  10.4 0.3 collective-permute-start.1
  10.7 2.1 %shard_map.92 = (f32[8,24,128]{2,1,0:T(8,128)S(1)}, f32[8,24,128]{2,1,0:T(8,128)S(1)}, bf16[8,1024,128]{2,1,0:T(8,128)(2,1)S(1)}, bf16[8,1024,128]{2,1,0:T(8,128)(2,1)S(1)}) custom-call(s32[1,8]{1,0:T(1,128)S(1)} %bitcast.7, bf16[1,72,128]{2,1,0:T(8,128)(2,1)S(1)} %bitcast.6, bf16[1,72,128]{2,1,0:T(8,128)(2,1)S(1)} %collective-permute-done.5.pair_ref, ...), custom_call_target="tpu_custom_call" | custom-call | flops 1000000000 | bytes 6291456 | tf_op jit(solution)/shard_map/pallas_call | solution.py:323
  12.8 1.0 %collective-permute-done.1 = bf16[2,72,128]{2,1,0:T(8,128)(2,1)S(1)} collective-permute-done((bf16[2,72,128]{2,1,0:T(8,128)(2,1)S(1)}, bf16[2,72,128]{2,1,0:T(8,128)(2,1)S(1)}, u32[]{:S(2)}, u32[]{:S(2)}) %collective-permute-start.1) | collective-permute-done | bytes 36896 | tf_op jit(solution)/shard_map/ppermute | solution.py:340
  13.8 0.3 %collective-permute-start.8 = (f32[8,24,128]{2,1,0:T(8,128)S(1)}, f32[8,24,128]{2,1,0:T(8,128)S(1)}, u32[]{:S(2)}, u32[]{:S(2)}) collective-permute-start(f32[8,24,128]{2,1,0:T(8,128)S(1)} %get-tuple-element.22), channel_id=1, source_target_pairs={{0,1},{1,0},{2,3},{3,2},{4,5},{5,4},{6,7},{7,6},{8,9},{9,8},{10,11... | collective-permute-start | bytes 294920 | tf_op jit(solution)/shard_map/ppermute | solution.py:340
  14.2 0.3 collective-permute-start.4
  14.4 0.9 %shard_map.93 = (f32[8,64,1024]{2,1,0:T(8,128)S(1)}, f32[8,64,128]{2,1,0:T(8,128)S(1)}) custom-call(bf16[8,72,128]{2,1,0:T(8,128)(2,1)S(1)} %constant_dynamic-update-slice_fusion.token_ref.refs_0_, bf16[8,1024,128]{2,1,0:T(8,128)(2,1)S(1)} %get-tuple-element.17.dk_ref.refs_4_), custom_call_target="tpu_custom_call" | custom-call | flops 1000000000 | bytes 4194304 | tf_op jit(solution)/shard_map/pallas_call | solution.py:323
  15.4 2.7 %shard_map.94 = (bf16[2,72,128]{2,1,0:T(8,128)(2,1)S(1)}, bf16[2,72,128]{2,1,0:T(8,128)(2,1)S(1)}, bf16[2,72,128]{2,1,0:T(8,128)(2,1)S(1)}, bf16[2,72,128]{2,1,0:T(8,128)(2,1)S(1)}) custom-call(bf16[8,72,128]{2,1,0:T(8,128)(2,1)S(1)} %constant_dynamic-update-slice_fusion.token_ref.refs_0_, bf16[8,8,128]{2,1,0:T(8,128)(2,1)S(1)} %collective-permute-done.4.refs_1_, ...), custom_call_target="tpu_custom_call" | custom-call | flops 1000000000 | bytes 4194304 | tf_op jit(solution)/shard_map/pallas_call | solution.py:323
  18.1 0.6 %collective-permute-start.9 = (bf16[2,72,128]{2,1,0:T(8,128)(2,1)S(1)}, bf16[2,72,128]{2,1,0:T(8,128)(2,1)S(1)}, u32[]{:S(2)}, u32[]{:S(2)}) collective-permute-start(bf16[2,72,128]{2,1,0:T(8,128)(2,1)S(1)} %get-tuple-element.24), channel_id=1, source_target_pairs={{0,3},{1,2},{2,1},{3,0},{4,7},{5,6},{6,5},{7,4},{8,11},{9,10},{10,... | collective-permute-start | bytes 110600 | tf_op jit(solution)/shard_map/ppermute | solution.py:340
  18.7 1.5 %collective-permute-start.10 = (bf16[2,72,128]{2,1,0:T(8,128)(2,1)S(1)}, bf16[2,72,128]{2,1,0:T(8,128)(2,1)S(1)}, u32[]{:S(2)}, u32[]{:S(2)}) collective-permute-start(bf16[2,72,128]{2,1,0:T(8,128)(2,1)S(1)} %get-tuple-element.25), channel_id=1, source_target_pairs={{0,5},{1,4},{2,7},{3,6},{4,1},{5,0},{6,3},{7,2},{8,13},{9,12},{10,... | collective-permute-start | bytes 110600 | tf_op jit(solution)/shard_map/ppermute | solution.py:340
  20.3 1.0 %collective-permute-start.11 = (bf16[2,72,128]{2,1,0:T(8,128)(2,1)S(1)}, bf16[2,72,128]{2,1,0:T(8,128)(2,1)S(1)}, u32[]{:S(2)}, u32[]{:S(2)}) collective-permute-start(bf16[2,72,128]{2,1,0:T(8,128)(2,1)S(1)} %get-tuple-element.26), channel_id=1, source_target_pairs={{0,7},{1,6},{2,5},{3,4},{4,3},{5,2},{6,1},{7,0},{8,15},{9,14},{10,... | collective-permute-start | bytes 110600 | tf_op jit(solution)/shard_map/ppermute | solution.py:340
  21.3 0.3 collective-permute-done.9.refs_1_
  21.6 0.6 %collective-permute-done.10.refs_2_ = bf16[2,72,128]{2,1,0:T(8,128)(2,1)S(1)} collective-permute-done((bf16[2,72,128]{2,1,0:T(8,128)(2,1)S(1)}, bf16[2,72,128]{2,1,0:T(8,128)(2,1)S(1)}, u32[]{:S(2)}, u32[]{:S(2)}) %collective-permute-start.10) | collective-permute-done | bytes 36896 | tf_op jit(solution)/shard_map/ppermute | solution.py:340
  22.1 2.4 %collective-permute-done.11.refs_3_ = bf16[2,72,128]{2,1,0:T(8,128)(2,1)S(1)} collective-permute-done((bf16[2,72,128]{2,1,0:T(8,128)(2,1)S(1)}, bf16[2,72,128]{2,1,0:T(8,128)(2,1)S(1)}, u32[]{:S(2)}, u32[]{:S(2)}) %collective-permute-start.11) | collective-permute-done | bytes 36896 | tf_op jit(solution)/shard_map/ppermute | solution.py:340
  24.6 0.2 shard_map.95
  24.8 2.6 %collective-permute-start.12 = (bf16[1,72,128]{2,1,0:T(8,128)(2,1)S(1)}, bf16[1,72,128]{2,1,0:T(8,128)(2,1)S(1)}, u32[]{:S(2)}, u32[]{:S(2)}) collective-permute-start(bf16[1,72,128]{2,1,0:T(8,128)(2,1)S(1)} %get-tuple-element.28), channel_id=1, source_target_pairs={{0,9},{1,8},{2,11},{3,10},{4,13},{5,12},{6,15},{7,14},{8,1},{9,0},... | collective-permute-start | bytes 55304 | tf_op jit(solution)/shard_map/ppermute | solution.py:340
  27.4 1.6 %collective-permute-done.12.refs_1_ = bf16[1,72,128]{2,1,0:T(8,128)(2,1)S(1)} collective-permute-done((bf16[1,72,128]{2,1,0:T(8,128)(2,1)S(1)}, bf16[1,72,128]{2,1,0:T(8,128)(2,1)S(1)}, u32[]{:S(2)}, u32[]{:S(2)}) %collective-permute-start.12) | collective-permute-done | bytes 18464 | tf_op jit(solution)/shard_map/ppermute | solution.py:340
  29.0 0.8 %shard_map.96 = bf16[1,8192]{1,0:T(2,128)(2,1)} custom-call(bf16[1,72,128]{2,1,0:T(8,128)(2,1)S(1)} %get-tuple-element.27.refs_0_, bf16[1,72,128]{2,1,0:T(8,128)(2,1)S(1)} %collective-permute-done.12.refs_1_), custom_call_target="tpu_custom_call" | custom-call | tf_op jit(solution)/shard_map/pallas_call | solution.py:323
  (29 shorter events, 0.2 us)
Async XLA Ops:
  0.0 10.6 %copy-start.2 = (bf16[1024,1024]{1,0:T(8,128)(2,1)S(1)}, bf16[1024,1024]{1,0:T(8,128)(2,1)}, u32[]{:S(2)}) copy-start(bf16[1024,1024]{1,0:T(8,128)(2,1)} %dk_ref.1) | copy-start | bytes 6291460
  0.0 10.6 %copy-start.3 = (bf16[1024,1024]{1,0:T(8,128)(2,1)S(1)}, bf16[1024,1024]{1,0:T(8,128)(2,1)}, u32[]{:S(2)}) copy-start(bf16[1024,1024]{1,0:T(8,128)(2,1)} %dv_ref.1) | copy-start | bytes 6291460
  0.0 10.6 %copy-start.6 = (s32[8]{0:T(128)S(1)}, s32[8]{0:T(128)}, u32[]{:S(2)}) copy-start(s32[8]{0:T(128)} %param.17) | copy-start | bytes 100
  0.0 10.6 %copy-start.1 = (bf16[1024,1024]{1,0:T(8,128)(2,1)S(1)}, bf16[1024,1024]{1,0:T(8,128)(2,1)}, u32[]{:S(2)}) copy-start(bf16[1024,1024]{1,0:T(8,128)(2,1)} %sv_ref.1) | copy-start | bytes 6291460
  0.0 10.6 %copy-start = (bf16[1024,1024]{1,0:T(8,128)(2,1)S(1)}, bf16[1024,1024]{1,0:T(8,128)(2,1)}, u32[]{:S(2)}) copy-start(bf16[1024,1024]{1,0:T(8,128)(2,1)} %sk_ref.1) | copy-start | bytes 6291460
  0.0 10.6 %copy-start.5 = (bf16[1,1024]{1,0:T(2,128)(2,1)S(1)}, bf16[1,1024]{1,0:T(2,128)(2,1)}, u32[]{:S(2)}) copy-start(bf16[1,1024]{1,0:T(2,128)(2,1)} %nv_ref.1) | copy-start | bytes 6148
  0.0 10.6 %copy-start.4 = (bf16[1,1024]{1,0:T(2,128)(2,1)S(1)}, bf16[1,1024]{1,0:T(2,128)(2,1)}, u32[]{:S(2)}) copy-start(bf16[1,1024]{1,0:T(2,128)(2,1)} %nk_ref.1) | copy-start | bytes 6148
  0.0 15.4 %collective-permute-start.6 = (bf16[1024,1024]{1,0:T(8,128)(2,1)}, bf16[1024,1024]{1,0:T(8,128)(2,1)S(1)}, u32[]{:S(2)}, u32[]{:S(2)}) collective-permute-start(bf16[1024,1024]{1,0:T(8,128)(2,1)} %dk_ref.1), channel_id=1, source_target_pairs={{0,1},{1,0},{2,3},{3,2},{4,5},{5,4},{6,7},{7,6},{8,9},{9,8},{10,11... | collective-permute-start | bytes 6291464 | tf_op jit(solution)/shard_map/ppermute | solution.py:340
  0.6 14.8 %collective-permute-start.7 = (bf16[1024,1024]{1,0:T(8,128)(2,1)}, bf16[1024,1024]{1,0:T(8,128)(2,1)S(1)}, u32[]{:S(2)}, u32[]{:S(2)}) collective-permute-start(bf16[1024,1024]{1,0:T(8,128)(2,1)} %dv_ref.1), channel_id=1, source_target_pairs={{0,1},{1,0},{2,3},{3,2},{4,5},{5,4},{6,7},{7,6},{8,9},{9,8},{10,11... | collective-permute-start | bytes 6291464 | tf_op jit(solution)/shard_map/ppermute | solution.py:340
  1.9 8.4 %collective-permute-start.5 = (bf16[1,72,128]{2,1,0:T(8,128)(2,1)S(1)}, bf16[1,72,128]{2,1,0:T(8,128)(2,1)S(1)}, u32[]{:S(2)}, u32[]{:S(2)}) collective-permute-start(bf16[1,72,128]{2,1,0:T(8,128)(2,1)S(1)} %bitcast.3), channel_id=1, source_target_pairs={{0,1},{1,0},{2,3},{3,2},{4,5},{5,4},{6,7},{7,6},{8,9},{9,8},{10,11... | collective-permute-start | bytes 55304 | tf_op jit(solution)/shard_map/ppermute | solution.py:340
  2.4 5.2 %collective-permute-start = (bf16[1,72,128]{2,1,0:T(8,128)(2,1)S(1)}, bf16[1,72,128]{2,1,0:T(8,128)(2,1)S(1)}, u32[]{:S(2)}, u32[]{:S(2)}) collective-permute-start(bf16[1,72,128]{2,1,0:T(8,128)(2,1)S(1)} %bitcast.4), channel_id=1, source_target_pairs={{0,9},{1,8},{2,11},{3,10},{4,13},{5,12},{6,15},{7,14},{8,1},{9,0},... | collective-permute-start | bytes 55304 | tf_op jit(solution)/shard_map/ppermute | solution.py:340
  7.5 6.6 %collective-permute-start.3 = (bf16[2,72,128]{2,1,0:T(8,128)(2,1)S(1)}, bf16[2,72,128]{2,1,0:T(8,128)(2,1)S(1)}, u32[]{:S(2)}, u32[]{:S(2)}) collective-permute-start(bf16[2,72,128]{2,1,0:T(8,128)(2,1)S(1)} %pad_maximum_fusion), channel_id=1, source_target_pairs={{0,7},{1,6},{2,5},{3,4},{4,3},{5,2},{6,1},{7,0},{8,15},{9,14},{10,... | collective-permute-start | bytes 110600 | tf_op jit(solution)/shard_map/ppermute | solution.py:340
  10.1 4.0 %collective-permute-start.2 = (bf16[2,72,128]{2,1,0:T(8,128)(2,1)S(1)}, bf16[2,72,128]{2,1,0:T(8,128)(2,1)S(1)}, u32[]{:S(2)}, u32[]{:S(2)}) collective-permute-start(bf16[2,72,128]{2,1,0:T(8,128)(2,1)S(1)} %pad_maximum_fusion), channel_id=1, source_target_pairs={{0,5},{1,4},{2,7},{3,6},{4,1},{5,0},{6,3},{7,2},{8,13},{9,12},{10,... | collective-permute-start | bytes 110600 | tf_op jit(solution)/shard_map/ppermute | solution.py:340
  10.4 3.4 %collective-permute-start.1 = (bf16[2,72,128]{2,1,0:T(8,128)(2,1)S(1)}, bf16[2,72,128]{2,1,0:T(8,128)(2,1)S(1)}, u32[]{:S(2)}, u32[]{:S(2)}) collective-permute-start(bf16[2,72,128]{2,1,0:T(8,128)(2,1)S(1)} %pad_maximum_fusion), channel_id=1, source_target_pairs={{0,3},{1,2},{2,1},{3,0},{4,7},{5,6},{6,5},{7,4},{8,11},{9,10},{10,... | collective-permute-start | bytes 110600 | tf_op jit(solution)/shard_map/ppermute | solution.py:340
  13.8 1.6 %collective-permute-start.8 = (f32[8,24,128]{2,1,0:T(8,128)S(1)}, f32[8,24,128]{2,1,0:T(8,128)S(1)}, u32[]{:S(2)}, u32[]{:S(2)}) collective-permute-start(f32[8,24,128]{2,1,0:T(8,128)S(1)} %get-tuple-element.22), channel_id=1, source_target_pairs={{0,1},{1,0},{2,3},{3,2},{4,5},{5,4},{6,7},{7,6},{8,9},{9,8},{10,11... | collective-permute-start | bytes 294920 | tf_op jit(solution)/shard_map/ppermute | solution.py:340
  14.2 1.2 %collective-permute-start.4 = (bf16[8,8,128]{2,1,0:T(8,128)(2,1)S(1)}, bf16[8,8,128]{2,1,0:T(8,128)(2,1)S(1)}, u32[]{:S(2)}, u32[]{:S(2)}) collective-permute-start(bf16[8,8,128]{2,1,0:T(8,128)(2,1)S(1)} %slice.4), channel_id=1, source_target_pairs={{0,1},{1,0},{2,3},{3,2},{4,5},{5,4},{6,7},{7,6},{8,9},{9,8},{10,11... | collective-permute-start | bytes 49160 | tf_op jit(solution)/shard_map/ppermute | solution.py:340
  18.1 3.4 %collective-permute-start.9 = (bf16[2,72,128]{2,1,0:T(8,128)(2,1)S(1)}, bf16[2,72,128]{2,1,0:T(8,128)(2,1)S(1)}, u32[]{:S(2)}, u32[]{:S(2)}) collective-permute-start(bf16[2,72,128]{2,1,0:T(8,128)(2,1)S(1)} %get-tuple-element.24), channel_id=1, source_target_pairs={{0,3},{1,2},{2,1},{3,0},{4,7},{5,6},{6,5},{7,4},{8,11},{9,10},{10,... | collective-permute-start | bytes 110600 | tf_op jit(solution)/shard_map/ppermute | solution.py:340
  18.7 3.4 %collective-permute-start.10 = (bf16[2,72,128]{2,1,0:T(8,128)(2,1)S(1)}, bf16[2,72,128]{2,1,0:T(8,128)(2,1)S(1)}, u32[]{:S(2)}, u32[]{:S(2)}) collective-permute-start(bf16[2,72,128]{2,1,0:T(8,128)(2,1)S(1)} %get-tuple-element.25), channel_id=1, source_target_pairs={{0,5},{1,4},{2,7},{3,6},{4,1},{5,0},{6,3},{7,2},{8,13},{9,12},{10,... | collective-permute-start | bytes 110600 | tf_op jit(solution)/shard_map/ppermute | solution.py:340
  20.3 4.3 %collective-permute-start.11 = (bf16[2,72,128]{2,1,0:T(8,128)(2,1)S(1)}, bf16[2,72,128]{2,1,0:T(8,128)(2,1)S(1)}, u32[]{:S(2)}, u32[]{:S(2)}) collective-permute-start(bf16[2,72,128]{2,1,0:T(8,128)(2,1)S(1)} %get-tuple-element.26), channel_id=1, source_target_pairs={{0,7},{1,6},{2,5},{3,4},{4,3},{5,2},{6,1},{7,0},{8,15},{9,14},{10,... | collective-permute-start | bytes 110600 | tf_op jit(solution)/shard_map/ppermute | solution.py:340
  24.8 4.2 %collective-permute-start.12 = (bf16[1,72,128]{2,1,0:T(8,128)(2,1)S(1)}, bf16[1,72,128]{2,1,0:T(8,128)(2,1)S(1)}, u32[]{:S(2)}, u32[]{:S(2)}) collective-permute-start(bf16[1,72,128]{2,1,0:T(8,128)(2,1)S(1)} %get-tuple-element.28), channel_id=1, source_target_pairs={{0,9},{1,8},{2,11},{3,10},{4,13},{5,12},{6,15},{7,14},{8,1},{9,0},... | collective-permute-start | bytes 55304 | tf_op jit(solution)/shard_map/ppermute | solution.py:340

commit v9 on v8

--- a/solution.py
+++ b/solution.py
@@ -56,12 +56,8 @@
     sv_ref,
     nk_ref,
     nv_ref,
-    dk_ref,
-    dv_ref,
     own_out_ref,
     pair_out_ref,
-    dk_out_ref,
-    dv_out_ref,
 ):
     me = lax.axis_index("seq")
     parity = lax.rem(me, 2)
@@ -104,8 +100,11 @@
             target[head, 0:GROUPS] = jnp.broadcast_to(top[mine], (GROUPS, LANES))
             target[head, GROUPS : 2 * GROUPS] = jnp.broadcast_to(total[mine], (GROUPS, LANES))
             target[head, 2 * GROUPS :] = out[mine]
-        dk_out_ref[head] = dk_ref[:, cols]
-        dv_out_ref[head] = dv_ref[:, cols]
+
+
+def order_kernel(_, source, target):
+    for head in range(KVH):
+        target[head] = source[:, head * HD : (head + 1) * HD]
 
 
 def split_stats(stats, axis):
@@ -150,7 +149,7 @@
         score_ref, peak_ref, *refs = refs
     dk_ref, dv_ref, far_dk_ref, far_dv_ref, own_ref, theirs_ref, *refs = refs
     out_refs, (bias_ref,) = refs[:pieces], refs[pieces:]
-    span = far_dk_ref.shape[0]
+    span = far_dk_ref.shape[1]
     blocks_here = span // BLOCK
     rows_here = SLOTS * GROUPS
     me = lax.axis_index("seq")
@@ -183,8 +182,7 @@
 
         def scores_of(head):
             q = head_queries(near_ref, slots, head)
-            cols = slice(head * HD, (head + 1) * HD)
-            far = lane_dot(q, far_dk_ref[:, cols]) + bias_ref[:, span:]
+            far = lane_dot(q, far_dk_ref[head]) + bias_ref[:, span:]
             if scored:
                 return blocks_of(far)
             return blocks_of(far), blocks_of(lane_dot(q, dk_ref[head]) + bias_ref[:, :span])
@@ -375,10 +373,21 @@
     pair = swap(own, 1)
     far_dk = swap(doc_keys, 1)
     far_dv = swap(doc_values, 1)
+
+    def ordered(after, cache):
+        return on_core(
+            order_kernel,
+            heads_of(cache),
+            (after, cache),
+            cost=pl.CostEstimate(flops=0, bytes_accessed=4 * size, transcendentals=0),
+        )
+
+    dk = ordered(own, doc_keys)
+    dv = ordered(own, doc_values)
     partial = VMEM((KVH, 3 * GROUPS, LANES), jnp.float32)
-    local, pair_local, dk, dv = on_core(
+    local, pair_local = on_core(
         suffix_kernel,
-        [partial, partial, heads_of(doc_keys), heads_of(doc_values)],
+        [partial, partial],
         (
             near_core(suffix_lengths[None]),
             own,
@@ -387,11 +396,10 @@
             suffix_values,
             new_keys,
             new_values,
-            doc_keys,
-            doc_values,
         ),
         cost=pl.CostEstimate(flops=10**9, bytes_accessed=3 * size, transcendentals=10**6),
     )
+    far_dk = ordered(local, near_core(far_dk))
     for step, stage in enumerate(stages):
         arrived = []
         for bits in stage:
@@ -426,7 +434,7 @@
             *scores,
             dk,
             dv,
-            near_core(far_dk),
+            far_dk,
             near_core(far_dv),
             local,
             near_core(theirs),

time: 29.9 us -> 30.3 us (1.013)
  local copies, waits for them, and re-layouts: 0.07 us -> 1.24 us
  starting transfers between devices: 14.2 us -> 13.2 us
  waiting for transfers between devices: 7.43 us -> 7.99 us
  Pallas kernels: 7.97 us -> 7.61 us
    unnamed x18, local copies, waits for them, and re-layouts: 0.06 us -> 1.22 us
    ppermute x13, starting transfers between devices: 14.2 us -> 13.2 us  [swap(): return lax.ppermute(x, 'seq', [(i, i ^ bits) for i in range(devices)])]
    ppermute x13, waiting for transfers between devices: 7.43 us -> 7.99 us  [swap(): return lax.ppermute(x, 'seq', [(i, i ^ bits) for i in range(devices)])]
    pallas_call x6 -> x9, Pallas kernels: 7.97 us -> 7.61 us  [on_core(): pl.pallas_call(kernel, out_shape=out_shape, in_specs=kwargs.pop('in_specs...]
  transfers between devices with their start and end apart: 13 -> 13, of which waited for: 6 -> 5; matrix products, arithmetic and copies ran while one was open for 0% -> 0% of each run, Pallas kernels for 14% -> 14%
where the time goes in v9:
time: 30.3 us; the launch traced here: 30.2 us
  starting transfers between devices  13.2 us (44%)
  waiting for transfers between devices  7.99 us (26%)
  Pallas kernels  7.61 us (25%)
  local copies, waits for them, and re-layouts  1.24 us (4%)
    ppermute x13, starting transfers between devices, swap(): return lax.ppermute(x, 'seq', [(i, i ^ bits) for i in range(devices)])  13.2 us
    ppermute x13, waiting for transfers between devices, swap(): return lax.ppermute(x, 'seq', [(i, i ^ bits) for i in range(devices)])  7.99 us
    pallas_call x9, Pallas kernels, on_core(): pl.pallas_call(kernel, out_shape=out_shape, in_specs=kwargs.pop('in_specs...  7.61 us
    unnamed x18, local copies, waits for them, and re-layouts  1.22 us
  transfers between devices with their start and end apart: 13, of which 5 were waited for; matrix products, arithmetic and copies ran while one was open for 0% of the time, Pallas kernels for 14%

profile of v9, /device:TPU:0, one launch (start us, length us, event | category | flops | bytes accessed | tf_op | source)
XLA Modules:
  0.0 30.2 jit_solution(10840875077759501786)
XLA Ops:
  0.0 0.5 %collective-permute-start.6 = (bf16[1024,1024]{1,0:T(8,128)(2,1)}, bf16[1024,1024]{1,0:T(8,128)(2,1)S(1)}, u32[]{:S(2)}, u32[]{:S(2)}) collective-permute-start(bf16[1024,1024]{1,0:T(8,128)(2,1)} %source.2), channel_id=1, source_target_pairs={{0,1},{1,0},{2,3},{3,2},{4,5},{5,4},{6,7},{7,6},{8,9},{9,8},{10,11... | collective-permute-start | bytes 6291464 | tf_op jit(solution)/shard_map/ppermute | solution.py:338
  0.6 1.0 %shard_map.91 = bf16[72,128]{1,0:T(8,128)(2,1)S(1)} custom-call(s32[1,32]{1,0:T(1,128)} %list_ref.1, bf16[1,8192]{1,0:T(2,128)(2,1)} %q_ref.1), custom_call_target="tpu_custom_call" | custom-call | flops 10000000000 | bytes 100000 | tf_op jit(solution)/shard_map/pallas_call | solution.py:321
  1.5 0.6 %collective-permute-start.5 = (bf16[1,72,128]{2,1,0:T(8,128)(2,1)S(1)}, bf16[1,72,128]{2,1,0:T(8,128)(2,1)S(1)}, u32[]{:S(2)}, u32[]{:S(2)}) collective-permute-start(bf16[1,72,128]{2,1,0:T(8,128)(2,1)S(1)} %bitcast.3), channel_id=1, source_target_pairs={{0,1},{1,0},{2,3},{3,2},{4,5},{5,4},{6,7},{7,6},{8,9},{9,8},{10,11... | collective-permute-start | bytes 55304 | tf_op jit(solution)/shard_map/ppermute | solution.py:338
  2.1 3.7 %collective-permute-start = (bf16[1,72,128]{2,1,0:T(8,128)(2,1)S(1)}, bf16[1,72,128]{2,1,0:T(8,128)(2,1)S(1)}, u32[]{:S(2)}, u32[]{:S(2)}) collective-permute-start(bf16[1,72,128]{2,1,0:T(8,128)(2,1)S(1)} %bitcast.4), channel_id=1, source_target_pairs={{0,9},{1,8},{2,11},{3,10},{4,13},{5,12},{6,15},{7,14},{8,1},{9,0},... | collective-permute-start | bytes 55304 | tf_op jit(solution)/shard_map/ppermute | solution.py:338
  5.8 0.4 %shard_map.92.dk_ref.refs_4_ = bf16[8,1024,128]{2,1,0:T(8,128)(2,1)S(1)} custom-call(bf16[1,72,128]{2,1,0:T(8,128)(2,1)S(1)} %bitcast.5, bf16[1024,1024]{1,0:T(8,128)(2,1)S(1)} %copy-done.2), custom_call_target="tpu_custom_call" | custom-call | bytes 8388608 | tf_op jit(solution)/shard_map/pallas_call | solution.py:321
  6.2 1.2 %copy-done.3 = bf16[1024,1024]{1,0:T(8,128)(2,1)S(1)} copy-done((bf16[1024,1024]{1,0:T(8,128)(2,1)S(1)}, bf16[1024,1024]{1,0:T(8,128)(2,1)}, u32[]{:S(2)}) %copy-start.3) | copy-done | bytes 2097176
  7.4 0.4 %shard_map.94.refs_5_ = bf16[8,1024,128]{2,1,0:T(8,128)(2,1)S(1)} custom-call(bf16[1,72,128]{2,1,0:T(8,128)(2,1)S(1)} %bitcast.6, bf16[1024,1024]{1,0:T(8,128)(2,1)S(1)} %copy-done.3), custom_call_target="tpu_custom_call" | custom-call | bytes 8388608 | tf_op jit(solution)/shard_map/pallas_call | solution.py:321
  7.8 2.3 %collective-permute-start.3 = (bf16[2,72,128]{2,1,0:T(8,128)(2,1)S(1)}, bf16[2,72,128]{2,1,0:T(8,128)(2,1)S(1)}, u32[]{:S(2)}, u32[]{:S(2)}) collective-permute-start(bf16[2,72,128]{2,1,0:T(8,128)(2,1)S(1)} %pad_maximum_fusion), channel_id=1, source_target_pairs={{0,7},{1,6},{2,5},{3,4},{4,3},{5,2},{6,1},{7,0},{8,15},{9,14},{10,... | collective-permute-start | bytes 110600 | tf_op jit(solution)/shard_map/ppermute | solution.py:338
  10.1 0.5 %collective-permute-start.2 = (bf16[2,72,128]{2,1,0:T(8,128)(2,1)S(1)}, bf16[2,72,128]{2,1,0:T(8,128)(2,1)S(1)}, u32[]{:S(2)}, u32[]{:S(2)}) collective-permute-start(bf16[2,72,128]{2,1,0:T(8,128)(2,1)S(1)} %pad_maximum_fusion), channel_id=1, source_target_pairs={{0,5},{1,4},{2,7},{3,6},{4,1},{5,0},{6,3},{7,2},{8,13},{9,12},{10,... | collective-permute-start | bytes 110600 | tf_op jit(solution)/shard_map/ppermute | solution.py:338
  10.6 0.3 collective-permute-start.1
  10.9 1.2 %shard_map.95 = (f32[8,24,128]{2,1,0:T(8,128)S(1)}, f32[8,24,128]{2,1,0:T(8,128)S(1)}) custom-call(s32[1,8]{1,0:T(1,128)S(1)} %bitcast.9, bf16[1,72,128]{2,1,0:T(8,128)(2,1)S(1)} %bitcast.8, bf16[1,72,128]{2,1,0:T(8,128)(2,1)S(1)} %collective-permute-done.5.pair_ref, bf16[1024,1024]{1,0:T(8,128)(2,1)S(1)} %copy-done, bf16[1024,1024]{1,0:T(8,128)(2,1)S(1)} %copy-done.1, ...), custom_call_target="tpu_custom_call" | custom-call | flops 1000000000 | bytes 6291456 | tf_op jit(solution)/shard_map/pallas_call | solution.py:321
  12.1 2.1 %collective-permute-done.1 = bf16[2,72,128]{2,1,0:T(8,128)(2,1)S(1)} collective-permute-done((bf16[2,72,128]{2,1,0:T(8,128)(2,1)S(1)}, bf16[2,72,128]{2,1,0:T(8,128)(2,1)S(1)}, u32[]{:S(2)}, u32[]{:S(2)}) %collective-permute-start.1) | collective-permute-done | bytes 36896 | tf_op jit(solution)/shard_map/ppermute | solution.py:338
  14.4 0.5 %collective-permute-start.4 = (bf16[8,8,128]{2,1,0:T(8,128)(2,1)S(1)}, bf16[8,8,128]{2,1,0:T(8,128)(2,1)S(1)}, u32[]{:S(2)}, u32[]{:S(2)}) collective-permute-start(bf16[8,8,128]{2,1,0:T(8,128)(2,1)S(1)} %slice.4), channel_id=1, source_target_pairs={{0,1},{1,0},{2,3},{3,2},{4,5},{5,4},{6,7},{7,6},{8,9},{9,8},{10,11... | collective-permute-start | bytes 49160 | tf_op jit(solution)/shard_map/ppermute | solution.py:338
  14.8 0.9 %shard_map.93 = (f32[8,64,1024]{2,1,0:T(8,128)S(1)}, f32[8,64,128]{2,1,0:T(8,128)S(1)}) custom-call(bf16[8,72,128]{2,1,0:T(8,128)(2,1)S(1)} %constant_dynamic-update-slice_fusion.token_ref.refs_0_, bf16[8,1024,128]{2,1,0:T(8,128)(2,1)S(1)} %shard_map.92.dk_ref.refs_4_), custom_call_target="tpu_custom_call" | custom-call | flops 1000000000 | bytes 4194304 | tf_op jit(solution)/shard_map/pallas_call | solution.py:321
  15.8 0.4 %shard_map.96.refs_6_ = bf16[8,1024,128]{2,1,0:T(8,128)(2,1)S(1)} custom-call(f32[8,24,128]{2,1,0:T(8,128)S(1)} %get-tuple-element.17._.refs_8_, bf16[1024,1024]{1,0:T(8,128)(2,1)S(1)} %collective-permute-done.6.source), custom_call_target="tpu_custom_call" | custom-call | bytes 8388608 | tf_op jit(solution)/shard_map/pallas_call | solution.py:321
  16.2 2.2 %shard_map.97 = (bf16[2,72,128]{2,1,0:T(8,128)(2,1)S(1)}, bf16[2,72,128]{2,1,0:T(8,128)(2,1)S(1)}, bf16[2,72,128]{2,1,0:T(8,128)(2,1)S(1)}, bf16[2,72,128]{2,1,0:T(8,128)(2,1)S(1)}) custom-call(bf16[8,72,128]{2,1,0:T(8,128)(2,1)S(1)} %constant_dynamic-update-slice_fusion.token_ref.refs_0_, bf16[8,8,128]{2,1,0:T(8,128)(2,1)S(1)} %collective-permute-done.4.refs_1_, ...), custom_call_target="tpu_custom_call" | custom-call | flops 1000000000 | bytes 4194304 | tf_op jit(solution)/shard_map/pallas_call | solution.py:321
  18.5 0.3 %collective-permute-start.9 = (bf16[2,72,128]{2,1,0:T(8,128)(2,1)S(1)}, bf16[2,72,128]{2,1,0:T(8,128)(2,1)S(1)}, u32[]{:S(2)}, u32[]{:S(2)}) collective-permute-start(bf16[2,72,128]{2,1,0:T(8,128)(2,1)S(1)} %get-tuple-element.20), channel_id=1, source_target_pairs={{0,3},{1,2},{2,1},{3,0},{4,7},{5,6},{6,5},{7,4},{8,11},{9,10},{10,... | collective-permute-start | bytes 110600 | tf_op jit(solution)/shard_map/ppermute | solution.py:338
  18.8 1.7 %collective-permute-start.10 = (bf16[2,72,128]{2,1,0:T(8,128)(2,1)S(1)}, bf16[2,72,128]{2,1,0:T(8,128)(2,1)S(1)}, u32[]{:S(2)}, u32[]{:S(2)}) collective-permute-start(bf16[2,72,128]{2,1,0:T(8,128)(2,1)S(1)} %get-tuple-element.21), channel_id=1, source_target_pairs={{0,5},{1,4},{2,7},{3,6},{4,1},{5,0},{6,3},{7,2},{8,13},{9,12},{10,... | collective-permute-start | bytes 110600 | tf_op jit(solution)/shard_map/ppermute | solution.py:338
  20.5 0.9 %collective-permute-start.11 = (bf16[2,72,128]{2,1,0:T(8,128)(2,1)S(1)}, bf16[2,72,128]{2,1,0:T(8,128)(2,1)S(1)}, u32[]{:S(2)}, u32[]{:S(2)}) collective-permute-start(bf16[2,72,128]{2,1,0:T(8,128)(2,1)S(1)} %get-tuple-element.22), channel_id=1, source_target_pairs={{0,7},{1,6},{2,5},{3,4},{4,3},{5,2},{6,1},{7,0},{8,15},{9,14},{10,... | collective-permute-start | bytes 110600 | tf_op jit(solution)/shard_map/ppermute | solution.py:338
  21.5 0.6 %collective-permute-done.9.refs_1_ = bf16[2,72,128]{2,1,0:T(8,128)(2,1)S(1)} collective-permute-done((bf16[2,72,128]{2,1,0:T(8,128)(2,1)S(1)}, bf16[2,72,128]{2,1,0:T(8,128)(2,1)S(1)}, u32[]{:S(2)}, u32[]{:S(2)}) %collective-permute-start.9) | collective-permute-done | bytes 36896 | tf_op jit(solution)/shard_map/ppermute | solution.py:338
  22.2 2.7 %collective-permute-done.11.refs_3_ = bf16[2,72,128]{2,1,0:T(8,128)(2,1)S(1)} collective-permute-done((bf16[2,72,128]{2,1,0:T(8,128)(2,1)S(1)}, bf16[2,72,128]{2,1,0:T(8,128)(2,1)S(1)}, u32[]{:S(2)}, u32[]{:S(2)}) %collective-permute-start.11) | collective-permute-done | bytes 36896 | tf_op jit(solution)/shard_map/ppermute | solution.py:338
  25.1 1.8 %collective-permute-start.12 = (bf16[1,72,128]{2,1,0:T(8,128)(2,1)S(1)}, bf16[1,72,128]{2,1,0:T(8,128)(2,1)S(1)}, u32[]{:S(2)}, u32[]{:S(2)}) collective-permute-start(bf16[1,72,128]{2,1,0:T(8,128)(2,1)S(1)} %get-tuple-element.24), channel_id=1, source_target_pairs={{0,9},{1,8},{2,11},{3,10},{4,13},{5,12},{6,15},{7,14},{8,1},{9,0},... | collective-permute-start | bytes 55304 | tf_op jit(solution)/shard_map/ppermute | solution.py:338
  26.9 2.4 %collective-permute-done.12.refs_1_ = bf16[1,72,128]{2,1,0:T(8,128)(2,1)S(1)} collective-permute-done((bf16[1,72,128]{2,1,0:T(8,128)(2,1)S(1)}, bf16[1,72,128]{2,1,0:T(8,128)(2,1)S(1)}, u32[]{:S(2)}, u32[]{:S(2)}) %collective-permute-start.12) | collective-permute-done | bytes 18464 | tf_op jit(solution)/shard_map/ppermute | solution.py:338
  29.4 0.8 %shard_map.99 = bf16[1,8192]{1,0:T(2,128)(2,1)} custom-call(bf16[1,72,128]{2,1,0:T(8,128)(2,1)S(1)} %get-tuple-element.23.refs_0_, bf16[1,72,128]{2,1,0:T(8,128)(2,1)S(1)} %collective-permute-done.12.refs_1_), custom_call_target="tpu_custom_call" | custom-call | tf_op jit(solution)/shard_map/pallas_call | solution.py:321
  (32 shorter events, 0.7 us)
Async XLA Ops:
  0.0 5.8 %copy-start.2 = (bf16[1024,1024]{1,0:T(8,128)(2,1)S(1)}, bf16[1024,1024]{1,0:T(8,128)(2,1)}, u32[]{:S(2)}) copy-start(bf16[1024,1024]{1,0:T(8,128)(2,1)} %source.2) | copy-start | bytes 6291460
  0.0 15.8 %collective-permute-start.6 = (bf16[1024,1024]{1,0:T(8,128)(2,1)}, bf16[1024,1024]{1,0:T(8,128)(2,1)S(1)}, u32[]{:S(2)}, u32[]{:S(2)}) collective-permute-start(bf16[1024,1024]{1,0:T(8,128)(2,1)} %source.2), channel_id=1, source_target_pairs={{0,1},{1,0},{2,3},{3,2},{4,5},{5,4},{6,7},{7,6},{8,9},{9,8},{10,11... | collective-permute-start | bytes 6291464 | tf_op jit(solution)/shard_map/ppermute | solution.py:338
  0.5 15.7 %collective-permute-start.7 = (bf16[1024,1024]{1,0:T(8,128)(2,1)}, bf16[1024,1024]{1,0:T(8,128)(2,1)S(1)}, u32[]{:S(2)}, u32[]{:S(2)}) collective-permute-start(bf16[1024,1024]{1,0:T(8,128)(2,1)} %source.3), channel_id=1, source_target_pairs={{0,1},{1,0},{2,3},{3,2},{4,5},{5,4},{6,7},{7,6},{8,9},{9,8},{10,11... | collective-permute-start | bytes 6291464 | tf_op jit(solution)/shard_map/ppermute | solution.py:338
  1.5 9.1 %collective-permute-start.5 = (bf16[1,72,128]{2,1,0:T(8,128)(2,1)S(1)}, bf16[1,72,128]{2,1,0:T(8,128)(2,1)S(1)}, u32[]{:S(2)}, u32[]{:S(2)}) collective-permute-start(bf16[1,72,128]{2,1,0:T(8,128)(2,1)S(1)} %bitcast.3), channel_id=1, source_target_pairs={{0,1},{1,0},{2,3},{3,2},{4,5},{5,4},{6,7},{7,6},{8,9},{9,8},{10,11... | collective-permute-start | bytes 55304 | tf_op jit(solution)/shard_map/ppermute | solution.py:338
  2.1 5.7 %collective-permute-start = (bf16[1,72,128]{2,1,0:T(8,128)(2,1)S(1)}, bf16[1,72,128]{2,1,0:T(8,128)(2,1)S(1)}, u32[]{:S(2)}, u32[]{:S(2)}) collective-permute-start(bf16[1,72,128]{2,1,0:T(8,128)(2,1)S(1)} %bitcast.4), channel_id=1, source_target_pairs={{0,9},{1,8},{2,11},{3,10},{4,13},{5,12},{6,15},{7,14},{8,1},{9,0},... | collective-permute-start | bytes 55304 | tf_op jit(solution)/shard_map/ppermute | solution.py:338
  5.8 1.6 %copy-start.3 = (bf16[1024,1024]{1,0:T(8,128)(2,1)S(1)}, bf16[1024,1024]{1,0:T(8,128)(2,1)}, u32[]{:S(2)}) copy-start(bf16[1024,1024]{1,0:T(8,128)(2,1)} %source.3) | copy-start | bytes 6291460
  7.4 3.5 %copy-start = (bf16[1024,1024]{1,0:T(8,128)(2,1)S(1)}, bf16[1024,1024]{1,0:T(8,128)(2,1)}, u32[]{:S(2)}) copy-start(bf16[1024,1024]{1,0:T(8,128)(2,1)} %sk_ref.1) | copy-start | bytes 6291460
  7.4 3.5 %copy-start.1 = (bf16[1024,1024]{1,0:T(8,128)(2,1)S(1)}, bf16[1024,1024]{1,0:T(8,128)(2,1)}, u32[]{:S(2)}) copy-start(bf16[1024,1024]{1,0:T(8,128)(2,1)} %sv_ref.1) | copy-start | bytes 6291460
  7.4 3.5 %copy-start.4 = (bf16[1,1024]{1,0:T(2,128)(2,1)S(1)}, bf16[1,1024]{1,0:T(2,128)(2,1)}, u32[]{:S(2)}) copy-start(bf16[1,1024]{1,0:T(2,128)(2,1)} %nk_ref.1) | copy-start | bytes 6148
  7.4 3.5 %copy-start.5 = (bf16[1,1024]{1,0:T(2,128)(2,1)S(1)}, bf16[1,1024]{1,0:T(2,128)(2,1)}, u32[]{:S(2)}) copy-start(bf16[1,1024]{1,0:T(2,128)(2,1)} %nv_ref.1) | copy-start | bytes 6148
  7.4 3.5 %copy-start.6 = (s32[8]{0:T(128)S(1)}, s32[8]{0:T(128)}, u32[]{:S(2)}) copy-start(s32[8]{0:T(128)} %param.17) | copy-start | bytes 100
  7.8 6.5 %collective-permute-start.3 = (bf16[2,72,128]{2,1,0:T(8,128)(2,1)S(1)}, bf16[2,72,128]{2,1,0:T(8,128)(2,1)S(1)}, u32[]{:S(2)}, u32[]{:S(2)}) collective-permute-start(bf16[2,72,128]{2,1,0:T(8,128)(2,1)S(1)} %pad_maximum_fusion), channel_id=1, source_target_pairs={{0,7},{1,6},{2,5},{3,4},{4,3},{5,2},{6,1},{7,0},{8,15},{9,14},{10,... | collective-permute-start | bytes 110600 | tf_op jit(solution)/shard_map/ppermute | solution.py:338
  10.1 4.2 %collective-permute-start.2 = (bf16[2,72,128]{2,1,0:T(8,128)(2,1)S(1)}, bf16[2,72,128]{2,1,0:T(8,128)(2,1)S(1)}, u32[]{:S(2)}, u32[]{:S(2)}) collective-permute-start(bf16[2,72,128]{2,1,0:T(8,128)(2,1)S(1)} %pad_maximum_fusion), channel_id=1, source_target_pairs={{0,5},{1,4},{2,7},{3,6},{4,1},{5,0},{6,3},{7,2},{8,13},{9,12},{10,... | collective-permute-start | bytes 110600 | tf_op jit(solution)/shard_map/ppermute | solution.py:338
  10.6 3.6 %collective-permute-start.1 = (bf16[2,72,128]{2,1,0:T(8,128)(2,1)S(1)}, bf16[2,72,128]{2,1,0:T(8,128)(2,1)S(1)}, u32[]{:S(2)}, u32[]{:S(2)}) collective-permute-start(bf16[2,72,128]{2,1,0:T(8,128)(2,1)S(1)} %pad_maximum_fusion), channel_id=1, source_target_pairs={{0,3},{1,2},{2,1},{3,0},{4,7},{5,6},{6,5},{7,4},{8,11},{9,10},{10,... | collective-permute-start | bytes 110600 | tf_op jit(solution)/shard_map/ppermute | solution.py:338
  14.2 2.0 %collective-permute-start.8 = (f32[8,24,128]{2,1,0:T(8,128)S(1)}, f32[8,24,128]{2,1,0:T(8,128)S(1)}, u32[]{:S(2)}, u32[]{:S(2)}) collective-permute-start(f32[8,24,128]{2,1,0:T(8,128)S(1)} %get-tuple-element.18), channel_id=1, source_target_pairs={{0,1},{1,0},{2,3},{3,2},{4,5},{5,4},{6,7},{7,6},{8,9},{9,8},{10,11... | collective-permute-start | bytes 294920 | tf_op jit(solution)/shard_map/ppermute | solution.py:338
  14.4 1.9 %collective-permute-start.4 = (bf16[8,8,128]{2,1,0:T(8,128)(2,1)S(1)}, bf16[8,8,128]{2,1,0:T(8,128)(2,1)S(1)}, u32[]{:S(2)}, u32[]{:S(2)}) collective-permute-start(bf16[8,8,128]{2,1,0:T(8,128)(2,1)S(1)} %slice.4), channel_id=1, source_target_pairs={{0,1},{1,0},{2,3},{3,2},{4,5},{5,4},{6,7},{7,6},{8,9},{9,8},{10,11... | collective-permute-start | bytes 49160 | tf_op jit(solution)/shard_map/ppermute | solution.py:338
  18.5 3.5 %collective-permute-start.9 = (bf16[2,72,128]{2,1,0:T(8,128)(2,1)S(1)}, bf16[2,72,128]{2,1,0:T(8,128)(2,1)S(1)}, u32[]{:S(2)}, u32[]{:S(2)}) collective-permute-start(bf16[2,72,128]{2,1,0:T(8,128)(2,1)S(1)} %get-tuple-element.20), channel_id=1, source_target_pairs={{0,3},{1,2},{2,1},{3,0},{4,7},{5,6},{6,5},{7,4},{8,11},{9,10},{10,... | collective-permute-start | bytes 110600 | tf_op jit(solution)/shard_map/ppermute | solution.py:338
  18.8 3.4 %collective-permute-start.10 = (bf16[2,72,128]{2,1,0:T(8,128)(2,1)S(1)}, bf16[2,72,128]{2,1,0:T(8,128)(2,1)S(1)}, u32[]{:S(2)}, u32[]{:S(2)}) collective-permute-start(bf16[2,72,128]{2,1,0:T(8,128)(2,1)S(1)} %get-tuple-element.21), channel_id=1, source_target_pairs={{0,5},{1,4},{2,7},{3,6},{4,1},{5,0},{6,3},{7,2},{8,13},{9,12},{10,... | collective-permute-start | bytes 110600 | tf_op jit(solution)/shard_map/ppermute | solution.py:338
  20.5 4.4 %collective-permute-start.11 = (bf16[2,72,128]{2,1,0:T(8,128)(2,1)S(1)}, bf16[2,72,128]{2,1,0:T(8,128)(2,1)S(1)}, u32[]{:S(2)}, u32[]{:S(2)}) collective-permute-start(bf16[2,72,128]{2,1,0:T(8,128)(2,1)S(1)} %get-tuple-element.22), channel_id=1, source_target_pairs={{0,7},{1,6},{2,5},{3,4},{4,3},{5,2},{6,1},{7,0},{8,15},{9,14},{10,... | collective-permute-start | bytes 110600 | tf_op jit(solution)/shard_map/ppermute | solution.py:338
  25.1 4.2 %collective-permute-start.12 = (bf16[1,72,128]{2,1,0:T(8,128)(2,1)S(1)}, bf16[1,72,128]{2,1,0:T(8,128)(2,1)S(1)}, u32[]{:S(2)}, u32[]{:S(2)}) collective-permute-start(bf16[1,72,128]{2,1,0:T(8,128)(2,1)S(1)} %get-tuple-element.24), channel_id=1, source_target_pairs={{0,9},{1,8},{2,11},{3,10},{4,13},{5,12},{6,15},{7,14},{8,1},{9,0},... | collective-permute-start | bytes 55304 | tf_op jit(solution)/shard_map/ppermute | solution.py:338

commit v10 on v9

--- a/solution.py
+++ b/solution.py
@@ -149,7 +149,7 @@
         score_ref, peak_ref, *refs = refs
     dk_ref, dv_ref, far_dk_ref, far_dv_ref, own_ref, theirs_ref, *refs = refs
     out_refs, (bias_ref,) = refs[:pieces], refs[pieces:]
-    span = far_dk_ref.shape[1]
+    span = far_dk_ref.shape[0]
     blocks_here = span // BLOCK
     rows_here = SLOTS * GROUPS
     me = lax.axis_index("seq")
@@ -169,7 +169,7 @@
         marks = []
         for i, device in enumerate((me, me ^ 1)):
             lane = lax.rem(device * blocks_here, LANES)
-            bias = jnp.where(pltpu.roll(flags, LANES - lane, 1) > 0.5, 0.0, NEG_BIG)
+            bias = jnp.where(pltpu.roll(flags, lax.rem(LANES - lane, LANES), 1) > 0.5, 0.0, NEG_BIG)
             marks.append(bias)
             for b in range(blocks_here):
                 wide = jnp.broadcast_to(bias[:, b : b + 1], (SLOTS, LANES))
@@ -182,7 +182,8 @@
 
         def scores_of(head):
             q = head_queries(near_ref, slots, head)
-            far = lane_dot(q, far_dk_ref[head]) + bias_ref[:, span:]
+            cols = slice(head * HD, (head + 1) * HD)
+            far = lane_dot(q, far_dk_ref[:, cols]) + bias_ref[:, span:]
             if scored:
                 return blocks_of(far)
             return blocks_of(far), blocks_of(lane_dot(q, dk_ref[head]) + bias_ref[:, :span])
@@ -213,13 +214,12 @@
         stats = jnp.zeros((rows_here, LANES), jnp.float32)
         ready = [scores_of(head) for head in range(DOC_AHEAD)]
         for head in range(KVH):
-            cols = slice(head * HD, (head + 1) * HD)
             scores = ready.pop(0)
             if head + DOC_AHEAD < KVH:
                 ready.append(scores_of(head + DOC_AHEAD))
             top, total, near, far = softmax_of(head, scores)
             out = jnp.dot(near, dv_ref[head], preferred_element_type=jnp.float32)
-            out = out + jnp.dot(far, far_dv_ref[:, cols], preferred_element_type=jnp.float32)
+            out = out + jnp.dot(far, far_dv_ref[head], preferred_element_type=jnp.float32)
             if local:
                 terms = [(top[:GROUPS], total[:GROUPS], out[:GROUPS])]
                 for ref in (own_ref, theirs_ref):
@@ -371,8 +371,8 @@
     heads_of = lambda x: VMEM((KVH, x.shape[0], HD), x.dtype)
     size = 2 * suffix_keys.size
     pair = swap(own, 1)
+    far_dv = swap(doc_values, 1)
     far_dk = swap(doc_keys, 1)
-    far_dv = swap(doc_values, 1)
 
     def ordered(after, cache):
         return on_core(
@@ -399,7 +399,7 @@
         ),
         cost=pl.CostEstimate(flops=10**9, bytes_accessed=3 * size, transcendentals=10**6),
     )
-    far_dk = ordered(local, near_core(far_dk))
+    far_dv = ordered(local, near_core(far_dv))
     for step, stage in enumerate(stages):
         arrived = []
         for bits in stage:
@@ -434,8 +434,8 @@
             *scores,
             dk,
             dv,
-            far_dk,
-            near_core(far_dv),
+            near_core(far_dk),
+            far_dv,
             local,
             near_core(theirs),
         ),

time: 30.3 us -> 30.2 us (level)
  no operation moved by 1% of the time
where the time goes in v10:
time: 30.2 us; the launch traced here: 30.1 us
  starting transfers between devices  13.2 us (44%)
  waiting for transfers between devices  7.99 us (26%)
  Pallas kernels  7.5 us (25%)
  local copies, waits for them, and re-layouts  1.24 us (4%)
    ppermute x13, starting transfers between devices, swap(): return lax.ppermute(x, 'seq', [(i, i ^ bits) for i in range(devices)])  13.2 us
    ppermute x13, waiting for transfers between devices, swap(): return lax.ppermute(x, 'seq', [(i, i ^ bits) for i in range(devices)])  7.99 us
    pallas_call x9, Pallas kernels, on_core(): pl.pallas_call(kernel, out_shape=out_shape, in_specs=kwargs.pop('in_specs...  7.5 us
    unnamed x18, local copies, waits for them, and re-layouts  1.22 us
  transfers between devices with their start and end apart: 13, of which 5 were waited for; matrix products, arithmetic and copies ran while one was open for 0% of the time, Pallas kernels for 14%

profile of v10, /device:TPU:0, one launch (start us, length us, event | category | flops | bytes accessed | tf_op | source)
XLA Modules:
  0.0 30.1 jit_solution(14608989271936250856)
XLA Ops:
  0.0 0.5 %collective-permute-start.7 = (bf16[1024,1024]{1,0:T(8,128)(2,1)}, bf16[1024,1024]{1,0:T(8,128)(2,1)S(1)}, u32[]{:S(2)}, u32[]{:S(2)}) collective-permute-start(bf16[1024,1024]{1,0:T(8,128)(2,1)} %source.3), channel_id=1, source_target_pairs={{0,1},{1,0},{2,3},{3,2},{4,5},{5,4},{6,7},{7,6},{8,9},{9,8},{10,11... | collective-permute-start | bytes 6291464 | tf_op jit(solution)/shard_map/ppermute | solution.py:338
  0.6 1.0 %shard_map.91 = bf16[72,128]{1,0:T(8,128)(2,1)S(1)} custom-call(s32[1,32]{1,0:T(1,128)} %list_ref.1, bf16[1,8192]{1,0:T(2,128)(2,1)} %q_ref.1), custom_call_target="tpu_custom_call" | custom-call | flops 10000000000 | bytes 100000 | tf_op jit(solution)/shard_map/pallas_call | solution.py:321
  1.5 0.6 %collective-permute-start.6 = (bf16[1,72,128]{2,1,0:T(8,128)(2,1)S(1)}, bf16[1,72,128]{2,1,0:T(8,128)(2,1)S(1)}, u32[]{:S(2)}, u32[]{:S(2)}) collective-permute-start(bf16[1,72,128]{2,1,0:T(8,128)(2,1)S(1)} %bitcast.3), channel_id=1, source_target_pairs={{0,1},{1,0},{2,3},{3,2},{4,5},{5,4},{6,7},{7,6},{8,9},{9,8},{10,11... | collective-permute-start | bytes 55304 | tf_op jit(solution)/shard_map/ppermute | solution.py:338
  2.1 3.7 %collective-permute-start = (bf16[1,72,128]{2,1,0:T(8,128)(2,1)S(1)}, bf16[1,72,128]{2,1,0:T(8,128)(2,1)S(1)}, u32[]{:S(2)}, u32[]{:S(2)}) collective-permute-start(bf16[1,72,128]{2,1,0:T(8,128)(2,1)S(1)} %bitcast.4), channel_id=1, source_target_pairs={{0,9},{1,8},{2,11},{3,10},{4,13},{5,12},{6,15},{7,14},{8,1},{9,0},... | collective-permute-start | bytes 55304 | tf_op jit(solution)/shard_map/ppermute | solution.py:338
  5.8 0.4 %shard_map.92.dk_ref.refs_4_ = bf16[8,1024,128]{2,1,0:T(8,128)(2,1)S(1)} custom-call(bf16[1,72,128]{2,1,0:T(8,128)(2,1)S(1)} %bitcast.5, bf16[1024,1024]{1,0:T(8,128)(2,1)S(1)} %copy-done.3), custom_call_target="tpu_custom_call" | custom-call | bytes 8388608 | tf_op jit(solution)/shard_map/pallas_call | solution.py:321
  6.2 1.2 %copy-done.2 = bf16[1024,1024]{1,0:T(8,128)(2,1)S(1)} copy-done((bf16[1024,1024]{1,0:T(8,128)(2,1)S(1)}, bf16[1024,1024]{1,0:T(8,128)(2,1)}, u32[]{:S(2)}) %copy-start.2) | copy-done | bytes 2097176
  7.4 0.4 %shard_map.94.refs_5_ = bf16[8,1024,128]{2,1,0:T(8,128)(2,1)S(1)} custom-call(bf16[1,72,128]{2,1,0:T(8,128)(2,1)S(1)} %bitcast.6, bf16[1024,1024]{1,0:T(8,128)(2,1)S(1)} %copy-done.2), custom_call_target="tpu_custom_call" | custom-call | bytes 8388608 | tf_op jit(solution)/shard_map/pallas_call | solution.py:321
  7.8 2.3 %collective-permute-start.3 = (bf16[2,72,128]{2,1,0:T(8,128)(2,1)S(1)}, bf16[2,72,128]{2,1,0:T(8,128)(2,1)S(1)}, u32[]{:S(2)}, u32[]{:S(2)}) collective-permute-start(bf16[2,72,128]{2,1,0:T(8,128)(2,1)S(1)} %pad_maximum_fusion), channel_id=1, source_target_pairs={{0,7},{1,6},{2,5},{3,4},{4,3},{5,2},{6,1},{7,0},{8,15},{9,14},{10,... | collective-permute-start | bytes 110600 | tf_op jit(solution)/shard_map/ppermute | solution.py:338
  10.1 0.5 %collective-permute-start.2 = (bf16[2,72,128]{2,1,0:T(8,128)(2,1)S(1)}, bf16[2,72,128]{2,1,0:T(8,128)(2,1)S(1)}, u32[]{:S(2)}, u32[]{:S(2)}) collective-permute-start(bf16[2,72,128]{2,1,0:T(8,128)(2,1)S(1)} %pad_maximum_fusion), channel_id=1, source_target_pairs={{0,5},{1,4},{2,7},{3,6},{4,1},{5,0},{6,3},{7,2},{8,13},{9,12},{10,... | collective-permute-start | bytes 110600 | tf_op jit(solution)/shard_map/ppermute | solution.py:338
  10.6 0.3 collective-permute-start.1
  10.9 1.2 %shard_map.95 = (f32[8,24,128]{2,1,0:T(8,128)S(1)}, f32[8,24,128]{2,1,0:T(8,128)S(1)}) custom-call(s32[1,8]{1,0:T(1,128)S(1)} %bitcast.9, bf16[1,72,128]{2,1,0:T(8,128)(2,1)S(1)} %bitcast.8, bf16[1,72,128]{2,1,0:T(8,128)(2,1)S(1)} %collective-permute-done.6.pair_ref, bf16[1024,1024]{1,0:T(8,128)(2,1)S(1)} %copy-done, bf16[1024,1024]{1,0:T(8,128)(2,1)S(1)} %copy-done.1, ...), custom_call_target="tpu_custom_call" | custom-call | flops 1000000000 | bytes 6291456 | tf_op jit(solution)/shard_map/pallas_call | solution.py:321
  12.1 2.1 %collective-permute-done.1 = bf16[2,72,128]{2,1,0:T(8,128)(2,1)S(1)} collective-permute-done((bf16[2,72,128]{2,1,0:T(8,128)(2,1)S(1)}, bf16[2,72,128]{2,1,0:T(8,128)(2,1)S(1)}, u32[]{:S(2)}, u32[]{:S(2)}) %collective-permute-start.1) | collective-permute-done | bytes 36896 | tf_op jit(solution)/shard_map/ppermute | solution.py:338
  14.4 0.5 %collective-permute-start.4 = (bf16[8,8,128]{2,1,0:T(8,128)(2,1)S(1)}, bf16[8,8,128]{2,1,0:T(8,128)(2,1)S(1)}, u32[]{:S(2)}, u32[]{:S(2)}) collective-permute-start(bf16[8,8,128]{2,1,0:T(8,128)(2,1)S(1)} %slice.4), channel_id=1, source_target_pairs={{0,1},{1,0},{2,3},{3,2},{4,5},{5,4},{6,7},{7,6},{8,9},{9,8},{10,11... | collective-permute-start | bytes 49160 | tf_op jit(solution)/shard_map/ppermute | solution.py:338
  14.8 0.9 %shard_map.93 = (f32[8,64,1024]{2,1,0:T(8,128)S(1)}, f32[8,64,128]{2,1,0:T(8,128)S(1)}) custom-call(bf16[8,72,128]{2,1,0:T(8,128)(2,1)S(1)} %constant_dynamic-update-slice_fusion.token_ref.refs_0_, bf16[8,1024,128]{2,1,0:T(8,128)(2,1)S(1)} %shard_map.92.dk_ref.refs_4_), custom_call_target="tpu_custom_call" | custom-call | flops 1000000000 | bytes 4194304 | tf_op jit(solution)/shard_map/pallas_call | solution.py:321
  15.8 0.4 %shard_map.96.refs_7_ = bf16[8,1024,128]{2,1,0:T(8,128)(2,1)S(1)} custom-call(f32[8,24,128]{2,1,0:T(8,128)S(1)} %get-tuple-element.17._.refs_8_, bf16[1024,1024]{1,0:T(8,128)(2,1)S(1)} %collective-permute-done.7.source), custom_call_target="tpu_custom_call" | custom-call | bytes 8388608 | tf_op jit(solution)/shard_map/pallas_call | solution.py:321
  16.2 2.1 %shard_map.97 = (bf16[2,72,128]{2,1,0:T(8,128)(2,1)S(1)}, bf16[2,72,128]{2,1,0:T(8,128)(2,1)S(1)}, bf16[2,72,128]{2,1,0:T(8,128)(2,1)S(1)}, bf16[2,72,128]{2,1,0:T(8,128)(2,1)S(1)}) custom-call(bf16[8,72,128]{2,1,0:T(8,128)(2,1)S(1)} %constant_dynamic-update-slice_fusion.token_ref.refs_0_, bf16[8,8,128]{2,1,0:T(8,128)(2,1)S(1)} %collective-permute-done.4.refs_1_, ...), custom_call_target="tpu_custom_call" | custom-call | flops 1000000000 | bytes 4194304 | tf_op jit(solution)/shard_map/pallas_call | solution.py:321
  18.4 0.3 %collective-permute-start.9 = (bf16[2,72,128]{2,1,0:T(8,128)(2,1)S(1)}, bf16[2,72,128]{2,1,0:T(8,128)(2,1)S(1)}, u32[]{:S(2)}, u32[]{:S(2)}) collective-permute-start(bf16[2,72,128]{2,1,0:T(8,128)(2,1)S(1)} %get-tuple-element.20), channel_id=1, source_target_pairs={{0,3},{1,2},{2,1},{3,0},{4,7},{5,6},{6,5},{7,4},{8,11},{9,10},{10,... | collective-permute-start | bytes 110600 | tf_op jit(solution)/shard_map/ppermute | solution.py:338
  18.7 1.7 %collective-permute-start.10 = (bf16[2,72,128]{2,1,0:T(8,128)(2,1)S(1)}, bf16[2,72,128]{2,1,0:T(8,128)(2,1)S(1)}, u32[]{:S(2)}, u32[]{:S(2)}) collective-permute-start(bf16[2,72,128]{2,1,0:T(8,128)(2,1)S(1)} %get-tuple-element.21), channel_id=1, source_target_pairs={{0,5},{1,4},{2,7},{3,6},{4,1},{5,0},{6,3},{7,2},{8,13},{9,12},{10,... | collective-permute-start | bytes 110600 | tf_op jit(solution)/shard_map/ppermute | solution.py:338
  20.4 0.9 %collective-permute-start.11 = (bf16[2,72,128]{2,1,0:T(8,128)(2,1)S(1)}, bf16[2,72,128]{2,1,0:T(8,128)(2,1)S(1)}, u32[]{:S(2)}, u32[]{:S(2)}) collective-permute-start(bf16[2,72,128]{2,1,0:T(8,128)(2,1)S(1)} %get-tuple-element.22), channel_id=1, source_target_pairs={{0,7},{1,6},{2,5},{3,4},{4,3},{5,2},{6,1},{7,0},{8,15},{9,14},{10,... | collective-permute-start | bytes 110600 | tf_op jit(solution)/shard_map/ppermute | solution.py:338
  21.3 0.6 %collective-permute-done.9.refs_1_ = bf16[2,72,128]{2,1,0:T(8,128)(2,1)S(1)} collective-permute-done((bf16[2,72,128]{2,1,0:T(8,128)(2,1)S(1)}, bf16[2,72,128]{2,1,0:T(8,128)(2,1)S(1)}, u32[]{:S(2)}, u32[]{:S(2)}) %collective-permute-start.9) | collective-permute-done | bytes 36896 | tf_op jit(solution)/shard_map/ppermute | solution.py:338
  22.1 2.7 %collective-permute-done.11.refs_3_ = bf16[2,72,128]{2,1,0:T(8,128)(2,1)S(1)} collective-permute-done((bf16[2,72,128]{2,1,0:T(8,128)(2,1)S(1)}, bf16[2,72,128]{2,1,0:T(8,128)(2,1)S(1)}, u32[]{:S(2)}, u32[]{:S(2)}) %collective-permute-start.11) | collective-permute-done | bytes 36896 | tf_op jit(solution)/shard_map/ppermute | solution.py:338
  25.0 1.8 %collective-permute-start.12 = (bf16[1,72,128]{2,1,0:T(8,128)(2,1)S(1)}, bf16[1,72,128]{2,1,0:T(8,128)(2,1)S(1)}, u32[]{:S(2)}, u32[]{:S(2)}) collective-permute-start(bf16[1,72,128]{2,1,0:T(8,128)(2,1)S(1)} %get-tuple-element.24), channel_id=1, source_target_pairs={{0,9},{1,8},{2,11},{3,10},{4,13},{5,12},{6,15},{7,14},{8,1},{9,0},... | collective-permute-start | bytes 55304 | tf_op jit(solution)/shard_map/ppermute | solution.py:338
  26.8 2.4 %collective-permute-done.12.refs_1_ = bf16[1,72,128]{2,1,0:T(8,128)(2,1)S(1)} collective-permute-done((bf16[1,72,128]{2,1,0:T(8,128)(2,1)S(1)}, bf16[1,72,128]{2,1,0:T(8,128)(2,1)S(1)}, u32[]{:S(2)}, u32[]{:S(2)}) %collective-permute-start.12) | collective-permute-done | bytes 18464 | tf_op jit(solution)/shard_map/ppermute | solution.py:338
  29.3 0.8 %shard_map.99 = bf16[1,8192]{1,0:T(2,128)(2,1)} custom-call(bf16[1,72,128]{2,1,0:T(8,128)(2,1)S(1)} %get-tuple-element.23.refs_0_, bf16[1,72,128]{2,1,0:T(8,128)(2,1)S(1)} %collective-permute-done.12.refs_1_), custom_call_target="tpu_custom_call" | custom-call | tf_op jit(solution)/shard_map/pallas_call | solution.py:321
  (32 shorter events, 0.7 us)
Async XLA Ops:
  0.0 5.8 %copy-start.3 = (bf16[1024,1024]{1,0:T(8,128)(2,1)S(1)}, bf16[1024,1024]{1,0:T(8,128)(2,1)}, u32[]{:S(2)}) copy-start(bf16[1024,1024]{1,0:T(8,128)(2,1)} %source.2) | copy-start | bytes 6291460
  0.0 15.8 %collective-permute-start.7 = (bf16[1024,1024]{1,0:T(8,128)(2,1)}, bf16[1024,1024]{1,0:T(8,128)(2,1)S(1)}, u32[]{:S(2)}, u32[]{:S(2)}) collective-permute-start(bf16[1024,1024]{1,0:T(8,128)(2,1)} %source.3), channel_id=1, source_target_pairs={{0,1},{1,0},{2,3},{3,2},{4,5},{5,4},{6,7},{7,6},{8,9},{9,8},{10,11... | collective-permute-start | bytes 6291464 | tf_op jit(solution)/shard_map/ppermute | solution.py:338
  0.5 15.7 %collective-permute-start.5 = (bf16[1024,1024]{1,0:T(8,128)(2,1)}, bf16[1024,1024]{1,0:T(8,128)(2,1)S(1)}, u32[]{:S(2)}, u32[]{:S(2)}) collective-permute-start(bf16[1024,1024]{1,0:T(8,128)(2,1)} %source.2), channel_id=1, source_target_pairs={{0,1},{1,0},{2,3},{3,2},{4,5},{5,4},{6,7},{7,6},{8,9},{9,8},{10,11... | collective-permute-start | bytes 6291464 | tf_op jit(solution)/shard_map/ppermute | solution.py:338
  1.5 9.1 %collective-permute-start.6 = (bf16[1,72,128]{2,1,0:T(8,128)(2,1)S(1)}, bf16[1,72,128]{2,1,0:T(8,128)(2,1)S(1)}, u32[]{:S(2)}, u32[]{:S(2)}) collective-permute-start(bf16[1,72,128]{2,1,0:T(8,128)(2,1)S(1)} %bitcast.3), channel_id=1, source_target_pairs={{0,1},{1,0},{2,3},{3,2},{4,5},{5,4},{6,7},{7,6},{8,9},{9,8},{10,11... | collective-permute-start | bytes 55304 | tf_op jit(solution)/shard_map/ppermute | solution.py:338
  2.1 5.7 %collective-permute-start = (bf16[1,72,128]{2,1,0:T(8,128)(2,1)S(1)}, bf16[1,72,128]{2,1,0:T(8,128)(2,1)S(1)}, u32[]{:S(2)}, u32[]{:S(2)}) collective-permute-start(bf16[1,72,128]{2,1,0:T(8,128)(2,1)S(1)} %bitcast.4), channel_id=1, source_target_pairs={{0,9},{1,8},{2,11},{3,10},{4,13},{5,12},{6,15},{7,14},{8,1},{9,0},... | collective-permute-start | bytes 55304 | tf_op jit(solution)/shard_map/ppermute | solution.py:338
  5.8 1.6 %copy-start.2 = (bf16[1024,1024]{1,0:T(8,128)(2,1)S(1)}, bf16[1024,1024]{1,0:T(8,128)(2,1)}, u32[]{:S(2)}) copy-start(bf16[1024,1024]{1,0:T(8,128)(2,1)} %source.3) | copy-start | bytes 6291460
  7.4 3.5 %copy-start = (bf16[1024,1024]{1,0:T(8,128)(2,1)S(1)}, bf16[1024,1024]{1,0:T(8,128)(2,1)}, u32[]{:S(2)}) copy-start(bf16[1024,1024]{1,0:T(8,128)(2,1)} %sk_ref.1) | copy-start | bytes 6291460
  7.4 3.5 %copy-start.1 = (bf16[1024,1024]{1,0:T(8,128)(2,1)S(1)}, bf16[1024,1024]{1,0:T(8,128)(2,1)}, u32[]{:S(2)}) copy-start(bf16[1024,1024]{1,0:T(8,128)(2,1)} %sv_ref.1) | copy-start | bytes 6291460
  7.4 3.5 %copy-start.4 = (bf16[1,1024]{1,0:T(2,128)(2,1)S(1)}, bf16[1,1024]{1,0:T(2,128)(2,1)}, u32[]{:S(2)}) copy-start(bf16[1,1024]{1,0:T(2,128)(2,1)} %nk_ref.1) | copy-start | bytes 6148
  7.4 3.5 %copy-start.5 = (bf16[1,1024]{1,0:T(2,128)(2,1)S(1)}, bf16[1,1024]{1,0:T(2,128)(2,1)}, u32[]{:S(2)}) copy-start(bf16[1,1024]{1,0:T(2,128)(2,1)} %nv_ref.1) | copy-start | bytes 6148
  7.4 3.5 %copy-start.6 = (s32[8]{0:T(128)S(1)}, s32[8]{0:T(128)}, u32[]{:S(2)}) copy-start(s32[8]{0:T(128)} %param.17) | copy-start | bytes 100
  7.8 6.5 %collective-permute-start.3 = (bf16[2,72,128]{2,1,0:T(8,128)(2,1)S(1)}, bf16[2,72,128]{2,1,0:T(8,128)(2,1)S(1)}, u32[]{:S(2)}, u32[]{:S(2)}) collective-permute-start(bf16[2,72,128]{2,1,0:T(8,128)(2,1)S(1)} %pad_maximum_fusion), channel_id=1, source_target_pairs={{0,7},{1,6},{2,5},{3,4},{4,3},{5,2},{6,1},{7,0},{8,15},{9,14},{10,... | collective-permute-start | bytes 110600 | tf_op jit(solution)/shard_map/ppermute | solution.py:338
  10.1 4.2 %collective-permute-start.2 = (bf16[2,72,128]{2,1,0:T(8,128)(2,1)S(1)}, bf16[2,72,128]{2,1,0:T(8,128)(2,1)S(1)}, u32[]{:S(2)}, u32[]{:S(2)}) collective-permute-start(bf16[2,72,128]{2,1,0:T(8,128)(2,1)S(1)} %pad_maximum_fusion), channel_id=1, source_target_pairs={{0,5},{1,4},{2,7},{3,6},{4,1},{5,0},{6,3},{7,2},{8,13},{9,12},{10,... | collective-permute-start | bytes 110600 | tf_op jit(solution)/shard_map/ppermute | solution.py:338
  10.6 3.6 %collective-permute-start.1 = (bf16[2,72,128]{2,1,0:T(8,128)(2,1)S(1)}, bf16[2,72,128]{2,1,0:T(8,128)(2,1)S(1)}, u32[]{:S(2)}, u32[]{:S(2)}) collective-permute-start(bf16[2,72,128]{2,1,0:T(8,128)(2,1)S(1)} %pad_maximum_fusion), channel_id=1, source_target_pairs={{0,3},{1,2},{2,1},{3,0},{4,7},{5,6},{6,5},{7,4},{8,11},{9,10},{10,... | collective-permute-start | bytes 110600 | tf_op jit(solution)/shard_map/ppermute | solution.py:338
  14.2 2.0 %collective-permute-start.8 = (f32[8,24,128]{2,1,0:T(8,128)S(1)}, f32[8,24,128]{2,1,0:T(8,128)S(1)}, u32[]{:S(2)}, u32[]{:S(2)}) collective-permute-start(f32[8,24,128]{2,1,0:T(8,128)S(1)} %get-tuple-element.18), channel_id=1, source_target_pairs={{0,1},{1,0},{2,3},{3,2},{4,5},{5,4},{6,7},{7,6},{8,9},{9,8},{10,11... | collective-permute-start | bytes 294920 | tf_op jit(solution)/shard_map/ppermute | solution.py:338
  14.4 1.9 %collective-permute-start.4 = (bf16[8,8,128]{2,1,0:T(8,128)(2,1)S(1)}, bf16[8,8,128]{2,1,0:T(8,128)(2,1)S(1)}, u32[]{:S(2)}, u32[]{:S(2)}) collective-permute-start(bf16[8,8,128]{2,1,0:T(8,128)(2,1)S(1)} %slice.4), channel_id=1, source_target_pairs={{0,1},{1,0},{2,3},{3,2},{4,5},{5,4},{6,7},{7,6},{8,9},{9,8},{10,11... | collective-permute-start | bytes 49160 | tf_op jit(solution)/shard_map/ppermute | solution.py:338
  18.4 3.5 %collective-permute-start.9 = (bf16[2,72,128]{2,1,0:T(8,128)(2,1)S(1)}, bf16[2,72,128]{2,1,0:T(8,128)(2,1)S(1)}, u32[]{:S(2)}, u32[]{:S(2)}) collective-permute-start(bf16[2,72,128]{2,1,0:T(8,128)(2,1)S(1)} %get-tuple-element.20), channel_id=1, source_target_pairs={{0,3},{1,2},{2,1},{3,0},{4,7},{5,6},{6,5},{7,4},{8,11},{9,10},{10,... | collective-permute-start | bytes 110600 | tf_op jit(solution)/shard_map/ppermute | solution.py:338
  18.7 3.4 %collective-permute-start.10 = (bf16[2,72,128]{2,1,0:T(8,128)(2,1)S(1)}, bf16[2,72,128]{2,1,0:T(8,128)(2,1)S(1)}, u32[]{:S(2)}, u32[]{:S(2)}) collective-permute-start(bf16[2,72,128]{2,1,0:T(8,128)(2,1)S(1)} %get-tuple-element.21), channel_id=1, source_target_pairs={{0,5},{1,4},{2,7},{3,6},{4,1},{5,0},{6,3},{7,2},{8,13},{9,12},{10,... | collective-permute-start | bytes 110600 | tf_op jit(solution)/shard_map/ppermute | solution.py:338
  20.4 4.4 %collective-permute-start.11 = (bf16[2,72,128]{2,1,0:T(8,128)(2,1)S(1)}, bf16[2,72,128]{2,1,0:T(8,128)(2,1)S(1)}, u32[]{:S(2)}, u32[]{:S(2)}) collective-permute-start(bf16[2,72,128]{2,1,0:T(8,128)(2,1)S(1)} %get-tuple-element.22), channel_id=1, source_target_pairs={{0,7},{1,6},{2,5},{3,4},{4,3},{5,2},{6,1},{7,0},{8,15},{9,14},{10,... | collective-permute-start | bytes 110600 | tf_op jit(solution)/shard_map/ppermute | solution.py:338
  25.0 4.2 %collective-permute-start.12 = (bf16[1,72,128]{2,1,0:T(8,128)(2,1)S(1)}, bf16[1,72,128]{2,1,0:T(8,128)(2,1)S(1)}, u32[]{:S(2)}, u32[]{:S(2)}) collective-permute-start(bf16[1,72,128]{2,1,0:T(8,128)(2,1)S(1)} %get-tuple-element.24), channel_id=1, source_target_pairs={{0,9},{1,8},{2,11},{3,10},{4,13},{5,12},{6,15},{7,14},{8,1},{9,0},... | collective-permute-start | bytes 55304 | tf_op jit(solution)/shard_map/ppermute | solution.py:338

commit v11 on v10

--- a/solution.py
+++ b/solution.py
@@ -102,9 +102,11 @@
             target[head, 2 * GROUPS :] = out[mine]
 
 
-def order_kernel(_, source, target):
-    for head in range(KVH):
-        target[head] = source[:, head * HD : (head + 1) * HD]
+def order_kernel(_, *refs):
+    half = len(refs) // 2
+    for source, target in zip(refs[:half], refs[half:]):
+        for head in range(KVH):
+            target[head] = source[:, head * HD : (head + 1) * HD]
 
 
 def split_stats(stats, axis):
@@ -374,16 +376,15 @@
     far_dv = swap(doc_values, 1)
     far_dk = swap(doc_keys, 1)
 
-    def ordered(after, cache):
+    def ordered(after, caches):
         return on_core(
             order_kernel,
-            heads_of(cache),
-            (after, cache),
+            [heads_of(cache) for cache in caches],
+            (after, *caches),
             cost=pl.CostEstimate(flops=0, bytes_accessed=4 * size, transcendentals=0),
         )
 
-    dk = ordered(own, doc_keys)
-    dv = ordered(own, doc_values)
+    dk, dv = ordered(own, (doc_keys, doc_values))
     partial = VMEM((KVH, 3 * GROUPS, LANES), jnp.float32)
     local, pair_local = on_core(
         suffix_kernel,
@@ -399,7 +400,7 @@
         ),
         cost=pl.CostEstimate(flops=10**9, bytes_accessed=3 * size, transcendentals=10**6),
     )
-    far_dv = ordered(local, near_core(far_dv))
+    (far_dv,) = ordered(local, (near_core(far_dv),))
     for step, stage in enumerate(stages):
         arrived = []
         for bits in stage:

time: 30.2 us -> 30 us (level)
  local copies, waits for them, and re-layouts: 1.24 us -> 0.08 us
  starting transfers between devices: 13.2 us -> 14 us
  Pallas kernels: 7.5 us -> 7.81 us
    unnamed x18, local copies, waits for them, and re-layouts: 1.22 us -> 0.07 us
    ppermute x13, starting transfers between devices: 13.2 us -> 14 us  [swap(): return lax.ppermute(x, 'seq', [(i, i ^ bits) for i in range(devices)])]
    pallas_call x9 -> x8, Pallas kernels: 7.5 us -> 7.81 us  [on_core(): pl.pallas_call(kernel, out_shape=out_shape, in_specs=kwargs.pop('in_specs...]
  transfers between devices with their start and end apart: 13 -> 13, of which waited for: 5 -> 6; matrix products, arithmetic and copies ran while one was open for 0% -> 0% of each run, Pallas kernels for 14% -> 15%
where the time goes in v11:
time: 30 us; the launch traced here: 29.9 us
  starting transfers between devices  14 us (47%)
  Pallas kernels  7.81 us (26%)
  waiting for transfers between devices  7.81 us (26%)
    ppermute x13, starting transfers between devices, swap(): return lax.ppermute(x, 'seq', [(i, i ^ bits) for i in range(devices)])  14 us
    pallas_call x8, Pallas kernels, on_core(): pl.pallas_call(kernel, out_shape=out_shape, in_specs=kwargs.pop('in_specs...  7.81 us
    ppermute x13, waiting for transfers between devices, swap(): return lax.ppermute(x, 'seq', [(i, i ^ bits) for i in range(devices)])  7.81 us
  transfers between devices with their start and end apart: 13, of which 6 were waited for; matrix products, arithmetic and copies ran while one was open for 0% of the time, Pallas kernels for 15%

profile of v11, /device:TPU:0, one launch (start us, length us, event | category | flops | bytes accessed | tf_op | source)
XLA Modules:
  0.0 29.9 jit_solution(13308761010095883046)
XLA Ops:
  0.0 0.5 %collective-permute-start.7 = (bf16[1024,1024]{1,0:T(8,128)(2,1)}, bf16[1024,1024]{1,0:T(8,128)(2,1)S(1)}, u32[]{:S(2)}, u32[]{:S(2)}) collective-permute-start(bf16[1024,1024]{1,0:T(8,128)(2,1)} %refs_1_.1), channel_id=1, source_target_pairs={{0,1},{1,0},{2,3},{3,2},{4,5},{5,4},{6,7},{7,6},{8,9},{9,8},{10,11... | collective-permute-start | bytes 6291464 | tf_op jit(solution)/shard_map/ppermute | solution.py:340
  0.6 1.2 %shard_map.91 = bf16[72,128]{1,0:T(8,128)(2,1)S(1)} custom-call(s32[1,32]{1,0:T(1,128)} %list_ref.1, bf16[1,8192]{1,0:T(2,128)(2,1)} %q_ref.1), custom_call_target="tpu_custom_call" | custom-call | flops 10000000000 | bytes 100000 | tf_op jit(solution)/shard_map/pallas_call | solution.py:323
  1.7 0.5 %collective-permute-start.6 = (bf16[1,72,128]{2,1,0:T(8,128)(2,1)S(1)}, bf16[1,72,128]{2,1,0:T(8,128)(2,1)S(1)}, u32[]{:S(2)}, u32[]{:S(2)}) collective-permute-start(bf16[1,72,128]{2,1,0:T(8,128)(2,1)S(1)} %bitcast.3), channel_id=1, source_target_pairs={{0,1},{1,0},{2,3},{3,2},{4,5},{5,4},{6,7},{7,6},{8,9},{9,8},{10,11... | collective-permute-start | bytes 55304 | tf_op jit(solution)/shard_map/ppermute | solution.py:340
  2.2 3.7 %collective-permute-start = (bf16[1,72,128]{2,1,0:T(8,128)(2,1)S(1)}, bf16[1,72,128]{2,1,0:T(8,128)(2,1)S(1)}, u32[]{:S(2)}, u32[]{:S(2)}) collective-permute-start(bf16[1,72,128]{2,1,0:T(8,128)(2,1)S(1)} %bitcast.4), channel_id=1, source_target_pairs={{0,9},{1,8},{2,11},{3,10},{4,13},{5,12},{6,15},{7,14},{8,1},{9,0},... | collective-permute-start | bytes 55304 | tf_op jit(solution)/shard_map/ppermute | solution.py:340
  6.0 0.8 %shard_map.92 = (bf16[8,1024,128]{2,1,0:T(8,128)(2,1)S(1)}, bf16[8,1024,128]{2,1,0:T(8,128)(2,1)S(1)}) custom-call(bf16[1,72,128]{2,1,0:T(8,128)(2,1)S(1)} %bitcast.5, bf16[1024,1024]{1,0:T(8,128)(2,1)S(1)} %copy-done.3, bf16[1024,1024]{1,0:T(8,128)(2,1)S(1)} %copy-done.2), custom_call_target="tpu_custom_call" | custom-call | bytes 8388608 | tf_op jit(solution)/shard_map/pallas_call | solution.py:323
  6.8 0.5 %collective-permute-done = bf16[1,72,128]{2,1,0:T(8,128)(2,1)S(1)} collective-permute-done((bf16[1,72,128]{2,1,0:T(8,128)(2,1)S(1)}, bf16[1,72,128]{2,1,0:T(8,128)(2,1)S(1)}, u32[]{:S(2)}, u32[]{:S(2)}) %collective-permute-start) | collective-permute-done | bytes 18464 | tf_op jit(solution)/shard_map/ppermute | solution.py:340
  7.4 2.5 %collective-permute-start.3 = (bf16[2,72,128]{2,1,0:T(8,128)(2,1)S(1)}, bf16[2,72,128]{2,1,0:T(8,128)(2,1)S(1)}, u32[]{:S(2)}, u32[]{:S(2)}) collective-permute-start(bf16[2,72,128]{2,1,0:T(8,128)(2,1)S(1)} %pad_maximum_fusion), channel_id=1, source_target_pairs={{0,7},{1,6},{2,5},{3,4},{4,3},{5,2},{6,1},{7,0},{8,15},{9,14},{10,... | collective-permute-start | bytes 110600 | tf_op jit(solution)/shard_map/ppermute | solution.py:340
  10.2 0.3 collective-permute-start.1
  10.5 1.2 %shard_map.94 = (f32[8,24,128]{2,1,0:T(8,128)S(1)}, f32[8,24,128]{2,1,0:T(8,128)S(1)}) custom-call(s32[1,8]{1,0:T(1,128)S(1)} %bitcast.8, bf16[1,72,128]{2,1,0:T(8,128)(2,1)S(1)} %bitcast.7, bf16[1,72,128]{2,1,0:T(8,128)(2,1)S(1)} %collective-permute-done.6.pair_ref, bf16[1024,1024]{1,0:T(8,128)(2,1)S(1)} %copy-done, bf16[1024,1024]{1,0:T(8,128)(2,1)S(1)} %copy-done.1, ...), custom_call_target="tpu_custom_call" | custom-call | flops 1000000000 | bytes 6291456 | tf_op jit(solution)/shard_map/pallas_call | solution.py:323
  11.6 2.0 %collective-permute-done.1 = bf16[2,72,128]{2,1,0:T(8,128)(2,1)S(1)} collective-permute-done((bf16[2,72,128]{2,1,0:T(8,128)(2,1)S(1)}, bf16[2,72,128]{2,1,0:T(8,128)(2,1)S(1)}, u32[]{:S(2)}, u32[]{:S(2)}) %collective-permute-start.1) | collective-permute-done | bytes 36896 | tf_op jit(solution)/shard_map/ppermute | solution.py:340
  13.6 0.3 %collective-permute-start.8 = (f32[8,24,128]{2,1,0:T(8,128)S(1)}, f32[8,24,128]{2,1,0:T(8,128)S(1)}, u32[]{:S(2)}, u32[]{:S(2)}) collective-permute-start(f32[8,24,128]{2,1,0:T(8,128)S(1)} %get-tuple-element.22), channel_id=1, source_target_pairs={{0,1},{1,0},{2,3},{3,2},{4,5},{5,4},{6,7},{7,6},{8,9},{9,8},{10,11... | collective-permute-start | bytes 294920 | tf_op jit(solution)/shard_map/ppermute | solution.py:340
  14.0 0.3 collective-permute-start.4
  14.3 0.9 %shard_map.93 = (f32[8,64,1024]{2,1,0:T(8,128)S(1)}, f32[8,64,128]{2,1,0:T(8,128)S(1)}) custom-call(bf16[8,72,128]{2,1,0:T(8,128)(2,1)S(1)} %constant_dynamic-update-slice_fusion.token_ref.refs_0_, bf16[8,1024,128]{2,1,0:T(8,128)(2,1)S(1)} %get-tuple-element.17.dk_ref.refs_4_), custom_call_target="tpu_custom_call" | custom-call | flops 1000000000 | bytes 4194304 | tf_op jit(solution)/shard_map/pallas_call | solution.py:323
  15.2 0.4 %shard_map.95.refs_7_ = bf16[8,1024,128]{2,1,0:T(8,128)(2,1)S(1)} custom-call(f32[8,24,128]{2,1,0:T(8,128)S(1)} %get-tuple-element.21._.refs_8_, bf16[1024,1024]{1,0:T(8,128)(2,1)S(1)} %collective-permute-done.7.refs_0_), custom_call_target="tpu_custom_call" | custom-call | bytes 8388608 | tf_op jit(solution)/shard_map/pallas_call | solution.py:323
  15.7 2.2 %shard_map.96 = (bf16[2,72,128]{2,1,0:T(8,128)(2,1)S(1)}, bf16[2,72,128]{2,1,0:T(8,128)(2,1)S(1)}, bf16[2,72,128]{2,1,0:T(8,128)(2,1)S(1)}, bf16[2,72,128]{2,1,0:T(8,128)(2,1)S(1)}) custom-call(bf16[8,72,128]{2,1,0:T(8,128)(2,1)S(1)} %constant_dynamic-update-slice_fusion.token_ref.refs_0_, bf16[8,8,128]{2,1,0:T(8,128)(2,1)S(1)} %collective-permute-done.4.refs_1_, ...), custom_call_target="tpu_custom_call" | custom-call | flops 1000000000 | bytes 4194304 | tf_op jit(solution)/shard_map/pallas_call | solution.py:323
  17.9 0.5 %collective-permute-start.9 = (bf16[2,72,128]{2,1,0:T(8,128)(2,1)S(1)}, bf16[2,72,128]{2,1,0:T(8,128)(2,1)S(1)}, u32[]{:S(2)}, u32[]{:S(2)}) collective-permute-start(bf16[2,72,128]{2,1,0:T(8,128)(2,1)S(1)} %get-tuple-element.24), channel_id=1, source_target_pairs={{0,3},{1,2},{2,1},{3,0},{4,7},{5,6},{6,5},{7,4},{8,11},{9,10},{10,... | collective-permute-start | bytes 110600 | tf_op jit(solution)/shard_map/ppermute | solution.py:340
  18.4 1.7 %collective-permute-start.10 = (bf16[2,72,128]{2,1,0:T(8,128)(2,1)S(1)}, bf16[2,72,128]{2,1,0:T(8,128)(2,1)S(1)}, u32[]{:S(2)}, u32[]{:S(2)}) collective-permute-start(bf16[2,72,128]{2,1,0:T(8,128)(2,1)S(1)} %get-tuple-element.25), channel_id=1, source_target_pairs={{0,5},{1,4},{2,7},{3,6},{4,1},{5,0},{6,3},{7,2},{8,13},{9,12},{10,... | collective-permute-start | bytes 110600 | tf_op jit(solution)/shard_map/ppermute | solution.py:340
  20.1 1.0 %collective-permute-start.11 = (bf16[2,72,128]{2,1,0:T(8,128)(2,1)S(1)}, bf16[2,72,128]{2,1,0:T(8,128)(2,1)S(1)}, u32[]{:S(2)}, u32[]{:S(2)}) collective-permute-start(bf16[2,72,128]{2,1,0:T(8,128)(2,1)S(1)} %get-tuple-element.26), channel_id=1, source_target_pairs={{0,7},{1,6},{2,5},{3,4},{4,3},{5,2},{6,1},{7,0},{8,15},{9,14},{10,... | collective-permute-start | bytes 110600 | tf_op jit(solution)/shard_map/ppermute | solution.py:340
  21.1 0.3 collective-permute-done.9.refs_1_
  21.4 0.4 %collective-permute-done.10.refs_2_ = bf16[2,72,128]{2,1,0:T(8,128)(2,1)S(1)} collective-permute-done((bf16[2,72,128]{2,1,0:T(8,128)(2,1)S(1)}, bf16[2,72,128]{2,1,0:T(8,128)(2,1)S(1)}, u32[]{:S(2)}, u32[]{:S(2)}) %collective-permute-start.10) | collective-permute-done | bytes 36896 | tf_op jit(solution)/shard_map/ppermute | solution.py:340
  21.8 2.7 %collective-permute-done.11.refs_3_ = bf16[2,72,128]{2,1,0:T(8,128)(2,1)S(1)} collective-permute-done((bf16[2,72,128]{2,1,0:T(8,128)(2,1)S(1)}, bf16[2,72,128]{2,1,0:T(8,128)(2,1)S(1)}, u32[]{:S(2)}, u32[]{:S(2)}) %collective-permute-start.11) | collective-permute-done | bytes 36896 | tf_op jit(solution)/shard_map/ppermute | solution.py:340
  24.7 2.5 %collective-permute-start.12 = (bf16[1,72,128]{2,1,0:T(8,128)(2,1)S(1)}, bf16[1,72,128]{2,1,0:T(8,128)(2,1)S(1)}, u32[]{:S(2)}, u32[]{:S(2)}) collective-permute-start(bf16[1,72,128]{2,1,0:T(8,128)(2,1)S(1)} %get-tuple-element.28), channel_id=1, source_target_pairs={{0,9},{1,8},{2,11},{3,10},{4,13},{5,12},{6,15},{7,14},{8,1},{9,0},... | collective-permute-start | bytes 55304 | tf_op jit(solution)/shard_map/ppermute | solution.py:340
  27.2 1.9 %collective-permute-done.12.refs_1_ = bf16[1,72,128]{2,1,0:T(8,128)(2,1)S(1)} collective-permute-done((bf16[1,72,128]{2,1,0:T(8,128)(2,1)S(1)}, bf16[1,72,128]{2,1,0:T(8,128)(2,1)S(1)}, u32[]{:S(2)}, u32[]{:S(2)}) %collective-permute-start.12) | collective-permute-done | bytes 18464 | tf_op jit(solution)/shard_map/ppermute | solution.py:340
  29.1 0.8 %shard_map.98 = bf16[1,8192]{1,0:T(2,128)(2,1)} custom-call(bf16[1,72,128]{2,1,0:T(8,128)(2,1)S(1)} %get-tuple-element.27.refs_0_, bf16[1,72,128]{2,1,0:T(8,128)(2,1)S(1)} %collective-permute-done.12.refs_1_), custom_call_target="tpu_custom_call" | custom-call | tf_op jit(solution)/shard_map/pallas_call | solution.py:323
  (31 shorter events, 0.7 us)
Async XLA Ops:
  0.0 5.9 %copy-start.2 = (bf16[1024,1024]{1,0:T(8,128)(2,1)S(1)}, bf16[1024,1024]{1,0:T(8,128)(2,1)}, u32[]{:S(2)}) copy-start(bf16[1024,1024]{1,0:T(8,128)(2,1)} %refs_1_.1) | copy-start | bytes 6291460
  0.0 5.9 %copy-start.3 = (bf16[1024,1024]{1,0:T(8,128)(2,1)S(1)}, bf16[1024,1024]{1,0:T(8,128)(2,1)}, u32[]{:S(2)}) copy-start(bf16[1024,1024]{1,0:T(8,128)(2,1)} %refs_0_.1) | copy-start | bytes 6291460
  0.0 15.2 %collective-permute-start.7 = (bf16[1024,1024]{1,0:T(8,128)(2,1)}, bf16[1024,1024]{1,0:T(8,128)(2,1)S(1)}, u32[]{:S(2)}, u32[]{:S(2)}) collective-permute-start(bf16[1024,1024]{1,0:T(8,128)(2,1)} %refs_1_.1), channel_id=1, source_target_pairs={{0,1},{1,0},{2,3},{3,2},{4,5},{5,4},{6,7},{7,6},{8,9},{9,8},{10,11... | collective-permute-start | bytes 6291464 | tf_op jit(solution)/shard_map/ppermute | solution.py:340
  0.5 15.2 %collective-permute-start.5 = (bf16[1024,1024]{1,0:T(8,128)(2,1)}, bf16[1024,1024]{1,0:T(8,128)(2,1)S(1)}, u32[]{:S(2)}, u32[]{:S(2)}) collective-permute-start(bf16[1024,1024]{1,0:T(8,128)(2,1)} %refs_0_.1), channel_id=1, source_target_pairs={{0,1},{1,0},{2,3},{3,2},{4,5},{5,4},{6,7},{7,6},{8,9},{9,8},{10,11... | collective-permute-start | bytes 6291464 | tf_op jit(solution)/shard_map/ppermute | solution.py:340
  1.7 8.4 %collective-permute-start.6 = (bf16[1,72,128]{2,1,0:T(8,128)(2,1)S(1)}, bf16[1,72,128]{2,1,0:T(8,128)(2,1)S(1)}, u32[]{:S(2)}, u32[]{:S(2)}) collective-permute-start(bf16[1,72,128]{2,1,0:T(8,128)(2,1)S(1)} %bitcast.3), channel_id=1, source_target_pairs={{0,1},{1,0},{2,3},{3,2},{4,5},{5,4},{6,7},{7,6},{8,9},{9,8},{10,11... | collective-permute-start | bytes 55304 | tf_op jit(solution)/shard_map/ppermute | solution.py:340
  2.2 5.2 %collective-permute-start = (bf16[1,72,128]{2,1,0:T(8,128)(2,1)S(1)}, bf16[1,72,128]{2,1,0:T(8,128)(2,1)S(1)}, u32[]{:S(2)}, u32[]{:S(2)}) collective-permute-start(bf16[1,72,128]{2,1,0:T(8,128)(2,1)S(1)} %bitcast.4), channel_id=1, source_target_pairs={{0,9},{1,8},{2,11},{3,10},{4,13},{5,12},{6,15},{7,14},{8,1},{9,0},... | collective-permute-start | bytes 55304 | tf_op jit(solution)/shard_map/ppermute | solution.py:340
  5.9 4.5 %copy-start = (bf16[1024,1024]{1,0:T(8,128)(2,1)S(1)}, bf16[1024,1024]{1,0:T(8,128)(2,1)}, u32[]{:S(2)}) copy-start(bf16[1024,1024]{1,0:T(8,128)(2,1)} %sk_ref.1) | copy-start | bytes 6291460
  5.9 4.5 %copy-start.1 = (bf16[1024,1024]{1,0:T(8,128)(2,1)S(1)}, bf16[1024,1024]{1,0:T(8,128)(2,1)}, u32[]{:S(2)}) copy-start(bf16[1024,1024]{1,0:T(8,128)(2,1)} %sv_ref.1) | copy-start | bytes 6291460
  5.9 4.5 %copy-start.4 = (bf16[1,1024]{1,0:T(2,128)(2,1)S(1)}, bf16[1,1024]{1,0:T(2,128)(2,1)}, u32[]{:S(2)}) copy-start(bf16[1,1024]{1,0:T(2,128)(2,1)} %nk_ref.1) | copy-start | bytes 6148
  6.0 4.5 %copy-start.5 = (bf16[1,1024]{1,0:T(2,128)(2,1)S(1)}, bf16[1,1024]{1,0:T(2,128)(2,1)}, u32[]{:S(2)}) copy-start(bf16[1,1024]{1,0:T(2,128)(2,1)} %nv_ref.1) | copy-start | bytes 6148
  6.0 4.5 %copy-start.6 = (s32[8]{0:T(128)S(1)}, s32[8]{0:T(128)}, u32[]{:S(2)}) copy-start(s32[8]{0:T(128)} %param.17) | copy-start | bytes 100
  7.4 6.6 %collective-permute-start.3 = (bf16[2,72,128]{2,1,0:T(8,128)(2,1)S(1)}, bf16[2,72,128]{2,1,0:T(8,128)(2,1)S(1)}, u32[]{:S(2)}, u32[]{:S(2)}) collective-permute-start(bf16[2,72,128]{2,1,0:T(8,128)(2,1)S(1)} %pad_maximum_fusion), channel_id=1, source_target_pairs={{0,7},{1,6},{2,5},{3,4},{4,3},{5,2},{6,1},{7,0},{8,15},{9,14},{10,... | collective-permute-start | bytes 110600 | tf_op jit(solution)/shard_map/ppermute | solution.py:340
  9.9 4.0 %collective-permute-start.2 = (bf16[2,72,128]{2,1,0:T(8,128)(2,1)S(1)}, bf16[2,72,128]{2,1,0:T(8,128)(2,1)S(1)}, u32[]{:S(2)}, u32[]{:S(2)}) collective-permute-start(bf16[2,72,128]{2,1,0:T(8,128)(2,1)S(1)} %pad_maximum_fusion), channel_id=1, source_target_pairs={{0,5},{1,4},{2,7},{3,6},{4,1},{5,0},{6,3},{7,2},{8,13},{9,12},{10,... | collective-permute-start | bytes 110600 | tf_op jit(solution)/shard_map/ppermute | solution.py:340
  10.2 3.4 %collective-permute-start.1 = (bf16[2,72,128]{2,1,0:T(8,128)(2,1)S(1)}, bf16[2,72,128]{2,1,0:T(8,128)(2,1)S(1)}, u32[]{:S(2)}, u32[]{:S(2)}) collective-permute-start(bf16[2,72,128]{2,1,0:T(8,128)(2,1)S(1)} %pad_maximum_fusion), channel_id=1, source_target_pairs={{0,3},{1,2},{2,1},{3,0},{4,7},{5,6},{6,5},{7,4},{8,11},{9,10},{10,... | collective-permute-start | bytes 110600 | tf_op jit(solution)/shard_map/ppermute | solution.py:340
  13.6 2.0 %collective-permute-start.8 = (f32[8,24,128]{2,1,0:T(8,128)S(1)}, f32[8,24,128]{2,1,0:T(8,128)S(1)}, u32[]{:S(2)}, u32[]{:S(2)}) collective-permute-start(f32[8,24,128]{2,1,0:T(8,128)S(1)} %get-tuple-element.22), channel_id=1, source_target_pairs={{0,1},{1,0},{2,3},{3,2},{4,5},{5,4},{6,7},{7,6},{8,9},{9,8},{10,11... | collective-permute-start | bytes 294920 | tf_op jit(solution)/shard_map/ppermute | solution.py:340
  14.0 1.7 %collective-permute-start.4 = (bf16[8,8,128]{2,1,0:T(8,128)(2,1)S(1)}, bf16[8,8,128]{2,1,0:T(8,128)(2,1)S(1)}, u32[]{:S(2)}, u32[]{:S(2)}) collective-permute-start(bf16[8,8,128]{2,1,0:T(8,128)(2,1)S(1)} %slice.4), channel_id=1, source_target_pairs={{0,1},{1,0},{2,3},{3,2},{4,5},{5,4},{6,7},{7,6},{8,9},{9,8},{10,11... | collective-permute-start | bytes 49160 | tf_op jit(solution)/shard_map/ppermute | solution.py:340
  17.9 3.4 %collective-permute-start.9 = (bf16[2,72,128]{2,1,0:T(8,128)(2,1)S(1)}, bf16[2,72,128]{2,1,0:T(8,128)(2,1)S(1)}, u32[]{:S(2)}, u32[]{:S(2)}) collective-permute-start(bf16[2,72,128]{2,1,0:T(8,128)(2,1)S(1)} %get-tuple-element.24), channel_id=1, source_target_pairs={{0,3},{1,2},{2,1},{3,0},{4,7},{5,6},{6,5},{7,4},{8,11},{9,10},{10,... | collective-permute-start | bytes 110600 | tf_op jit(solution)/shard_map/ppermute | solution.py:340
  18.4 3.4 %collective-permute-start.10 = (bf16[2,72,128]{2,1,0:T(8,128)(2,1)S(1)}, bf16[2,72,128]{2,1,0:T(8,128)(2,1)S(1)}, u32[]{:S(2)}, u32[]{:S(2)}) collective-permute-start(bf16[2,72,128]{2,1,0:T(8,128)(2,1)S(1)} %get-tuple-element.25), channel_id=1, source_target_pairs={{0,5},{1,4},{2,7},{3,6},{4,1},{5,0},{6,3},{7,2},{8,13},{9,12},{10,... | collective-permute-start | bytes 110600 | tf_op jit(solution)/shard_map/ppermute | solution.py:340
  20.1 4.4 %collective-permute-start.11 = (bf16[2,72,128]{2,1,0:T(8,128)(2,1)S(1)}, bf16[2,72,128]{2,1,0:T(8,128)(2,1)S(1)}, u32[]{:S(2)}, u32[]{:S(2)}) collective-permute-start(bf16[2,72,128]{2,1,0:T(8,128)(2,1)S(1)} %get-tuple-element.26), channel_id=1, source_target_pairs={{0,7},{1,6},{2,5},{3,4},{4,3},{5,2},{6,1},{7,0},{8,15},{9,14},{10,... | collective-permute-start | bytes 110600 | tf_op jit(solution)/shard_map/ppermute | solution.py:340
  24.7 4.4 %collective-permute-start.12 = (bf16[1,72,128]{2,1,0:T(8,128)(2,1)S(1)}, bf16[1,72,128]{2,1,0:T(8,128)(2,1)S(1)}, u32[]{:S(2)}, u32[]{:S(2)}) collective-permute-start(bf16[1,72,128]{2,1,0:T(8,128)(2,1)S(1)} %get-tuple-element.28), channel_id=1, source_target_pairs={{0,9},{1,8},{2,11},{3,10},{4,13},{5,12},{6,15},{7,14},{8,1},{9,0},... | collective-permute-start | bytes 55304 | tf_op jit(solution)/shard_map/ppermute | solution.py:340
